TPU v7x, 256 devices: a whole 4x4x8 slice. The times are simulated.
256 devices in a mesh: gx: 32 (over y, z_lo, x), gy: 8 (over z_hi, core).
Axes of the slice: x: 4, y: 4, z: 8 (z_hi: 4, z_lo: 2; z = z_hi * 2 + z_lo), core: 2. Of those that a mesh axis runs over, the one named last changes fastest.
Arguments:
- hidden: bfloat16 [2240, 5120], P('gy', 'gx'), may hold values from -6 to 6
- norm_gain: float32 [5120], P('gx'), may hold values from 0.1 to 1.9
- qkv_weight: bfloat16 [5120, 7168], P('gx', 'gy'), may hold values from -0.078125 to 0.078125
- qkv_bias: bfloat16 [7168], P('gy'), may hold values from -5 to 5
- out_weight: bfloat16 [5120, 5120], P('gy', 'gx'), may hold values from -0.078125 to 0.078125
- key_cache: bfloat16 [5, 8704, 1024], P(None, 'gx', 'gy'), may hold values from -68 to 68
- value_cache: bfloat16 [5, 8704, 1024], P(None, 'gx', 'gy'), may hold values from -12 to 12
- cached_len: int32 [5], replicated, may hold values from 1 to 8192, as said below
- fresh_len: int32 [5], replicated, may hold values from 224 to 448, as said below
Outputs:
- output: bfloat16 [2240, 5120], P('gy', 'gx')
- key_out: bfloat16 [5, 8704, 1024], P(None, 'gx', 'gy')
- value_out: bfloat16 [5, 8704, 1024], P(None, 'gx', 'gy')
Inputs may be any that keep to these rules, and one draw needn't show every extreme that they name: `cached_len`: two requests have 8192 - 8192 // 32 or more cached tokens, one of them exactly 8192; the other three fewer than 256. `fresh_len`: one request has exactly 448 live new tokens.
All inputs are finite; a program needn't handle non-finite values.
Results may differ from a plain program's by a relative error of at most 0.012.
Values may be sent and summed in bfloat16 or wider, within the bound.
A program may use at most 128 MiB of HBM per device.

v0:
```python
import jax
import jax.numpy as jnp
from jax import lax
from jax.sharding import PartitionSpec as P

HEAD_DIM = 128
GROUP = 5
REQUESTS = 5
NEW_TOKENS = 448


ROPE_THETA = 1000000.0
NORM_EPS = 1e-06
NEG_LARGE = -1e30


def rotate(vectors, positions):
    half_dim = vectors.shape[-1] // 2
    exponent = jnp.arange(half_dim, dtype=jnp.int32).astype(jnp.float32) * (2.0 / vectors.shape[-1])
    frequency = 1.0 / ROPE_THETA**exponent
    angles = positions[:, None] * frequency[None, :]
    target = (positions.shape[0],) + (1,) * (vectors.ndim - 2) + (half_dim,)
    cos_table = jnp.cos(angles).reshape(target)
    sin_table = jnp.sin(angles).reshape(target)
    first_half = vectors[..., :half_dim]
    second_half = vectors[..., half_dim:]
    return jnp.concatenate(
        [
            first_half * cos_table - second_half * sin_table,
            second_half * cos_table + first_half * sin_table,
        ],
        -1,
    )


def token_positions(cached_len, fresh_len, first_row, row_count):
    rows_here = first_row + jnp.arange(row_count, dtype=jnp.int32)
    request = rows_here // NEW_TOKENS
    within = rows_here % NEW_TOKENS
    picked = request[:, None] == jnp.arange(REQUESTS, dtype=jnp.int32)[None, :]
    start_pos = jnp.sum(jnp.where(picked, cached_len[None, :], 0), 1)
    live_count = jnp.sum(jnp.where(picked, fresh_len[None, :], 0), 1)
    return (start_pos + within, within < live_count)


def finish_rows(projected, cached_len, fresh_len, first_row):
    row_count = projected.shape[0]
    groups_here = projected.shape[1] // ((GROUP + 2) * HEAD_DIM)
    shaped = projected.reshape(row_count, groups_here, GROUP + 2, HEAD_DIM)
    positions, unused_live = token_positions(cached_len, fresh_len, first_row, row_count)
    angle_pos = positions.astype(jnp.float32)
    queries = rotate(shaped[:, :, :GROUP], angle_pos).astype(jnp.bfloat16).reshape(row_count, -1)
    new_keys = rotate(shaped[:, :, GROUP], angle_pos).astype(jnp.bfloat16).reshape(row_count, -1)
    new_values = shaped[:, :, GROUP + 1].astype(jnp.bfloat16).reshape(row_count, -1)
    return (queries, new_keys, new_values)


def append_rows(cache, new_rows, cached_len, fresh_len, first_slot):
    slot_count = cache.shape[1]
    slot_pos = first_slot + jnp.arange(slot_count, dtype=jnp.int32)
    offsets = slot_pos[None, :] - cached_len[:, None]
    is_live = (offsets >= 0) & (offsets < fresh_len[:, None])
    source_rows = jnp.arange(REQUESTS, dtype=jnp.int32)[:, None] * NEW_TOKENS + jnp.clip(
        offsets, 0, NEW_TOKENS - 1
    )
    return jnp.where(is_live[:, :, None], jnp.take(new_rows, source_rows, axis=0), cache)


def share_rows(share_sum, cached_len, fresh_len, first_row):
    queries, new_keys, new_values = finish_rows(share_sum, cached_len, fresh_len, first_row)
    return (
        lax.all_gather(queries, "gx", axis=0, tiled=True),
        lax.all_gather(new_keys, "gx", axis=0, tiled=True),
        lax.all_gather(new_values, "gx", axis=0, tiled=True),
    )


def per_device(
    hidden,
    norm_gain,
    qkv_weight,
    qkv_bias,
    out_weight,
    key_cache,
    value_cache,
    cached_len,
    fresh_len,
):
    scale = HEAD_DIM ** (-0.5)
    token_count = REQUESTS * NEW_TOKENS
    model_width = hidden.shape[1] * lax.axis_size("gx")
    hidden_f = hidden.astype(jnp.float32)
    squares = lax.psum(jnp.sum(hidden_f * hidden_f, axis=1), "gx")
    normed = (
        hidden_f * lax.rsqrt(squares / model_width + NORM_EPS)[:, None] * norm_gain[None, :]
    ).astype(jnp.bfloat16)
    gathered = lax.all_gather(normed, "gy", axis=0, tiled=True)
    bias_f = qkv_bias.astype(jnp.float32)[None, :]
    row_share = token_count // lax.axis_size("gx")
    share_start = lax.axis_index("gx") * row_share
    summed = lax.psum_scatter(
        jnp.dot(gathered, qkv_weight, preferred_element_type=jnp.float32),
        "gx",
        scatter_dimension=0,
        tiled=True,
    )
    queries, new_keys, new_values = share_rows(summed + bias_f, cached_len, fresh_len, share_start)
    slot_count = key_cache.shape[1]
    first_slot = lax.axis_index("gx") * slot_count
    key_out = append_rows(key_cache, new_keys, cached_len, fresh_len, first_slot)
    value_out = append_rows(value_cache, new_values, cached_len, fresh_len, first_slot)
    groups_here = key_cache.shape[2] // HEAD_DIM
    query_blocks = queries.reshape(REQUESTS, NEW_TOKENS, groups_here, GROUP, HEAD_DIM)
    key_blocks = key_out.reshape(REQUESTS, slot_count, groups_here, HEAD_DIM)
    value_blocks = value_out.reshape(REQUESTS, slot_count, groups_here, HEAD_DIM)
    slot_pos = first_slot + jnp.arange(slot_count, dtype=jnp.int32)
    query_pos = jnp.arange(NEW_TOKENS, dtype=jnp.int32)

    def visible_for(cached_here, fresh_here):
        return (slot_pos[None, :] < cached_here + fresh_here) & (
            slot_pos[None, :] <= cached_here + query_pos[:, None]
        )

    def scores_for(query_req, key_req, visible):
        scores = (
            jnp.einsum("ikgd,pkd->kgip", query_req, key_req, preferred_element_type=jnp.float32)
            * scale
        )
        return jnp.where(visible[None, None], scores, NEG_LARGE)

    def local_top(items):
        query_req, key_req, cached_here, fresh_here = items
        return jnp.max(scores_for(query_req, key_req, visible_for(cached_here, fresh_here)), axis=3)

    highest = lax.map(local_top, (query_blocks, key_blocks, cached_len, fresh_len))
    highest = lax.pmax(highest.astype(jnp.bfloat16), "gx").astype(highest.dtype)

    def local_sums(items):
        query_req, key_req, value_req, cached_here, fresh_here, top_here = items
        visible = visible_for(cached_here, fresh_here)
        scores = scores_for(query_req, key_req, visible)
        weighted = jnp.where(visible[None, None], jnp.exp(scores - top_here[..., None]), 0.0)
        denom = jnp.sum(weighted, axis=3)
        mixed = jnp.einsum(
            "kgip,pkd->ikgd",
            weighted.astype(jnp.bfloat16),
            value_req,
            preferred_element_type=jnp.float32,
        )
        return (mixed.reshape(NEW_TOKENS, -1), denom.reshape(-1, NEW_TOKENS).T)

    mixed, denom = lax.map(
        local_sums, (query_blocks, key_blocks, value_blocks, cached_len, fresh_len, highest)
    )
    mixed = mixed.reshape(token_count, -1)
    denom = denom.reshape(token_count, -1)
    mixed, denom = (
        lax.psum_scatter(mixed.astype(jnp.bfloat16), "gx", scatter_dimension=0, tiled=True).astype(
            jnp.float32
        ),
        lax.psum_scatter(denom.astype(jnp.bfloat16), "gx", scatter_dimension=0, tiled=True).astype(
            jnp.float32
        ),
    )
    unused_pos, is_live = token_positions(cached_len, fresh_len, share_start, row_share)
    ratio = mixed.reshape(row_share, -1, HEAD_DIM) / denom[:, :, None]
    attended = jnp.where(is_live[:, None], ratio.reshape(row_share, -1), 0.0).astype(jnp.bfloat16)
    partial_out = jnp.dot(
        lax.all_gather(attended, "gx", axis=0, tiled=True),
        out_weight,
        preferred_element_type=jnp.float32,
    )
    summed_out = lax.psum_scatter(
        partial_out.astype(jnp.bfloat16), "gy", scatter_dimension=0, tiled=True
    ).astype(jnp.float32)
    output = (hidden_f + summed_out).astype(jnp.bfloat16)
    return (output, key_out, value_out)


def solution(mesh):
    in_specs = (
        P("gy", "gx"),
        P("gx"),
        P("gx", "gy"),
        P("gy"),
        P("gy", "gx"),
        P(None, "gx", "gy"),
        P(None, "gx", "gy"),
        P(),
        P(),
    )
    out_specs = (P("gy", "gx"), P(None, "gx", "gy"), P(None, "gx", "gy"))
    return jax.shard_map(
        per_device, mesh=mesh, in_specs=in_specs, out_specs=out_specs, check_vma=False
    )
```

profile of v0, /device:TPU:2, one launch (start us, length us, event | category | flops | bytes accessed | tf_op | source)
XLA Modules:
  0.0 1128.1 jit_solution(15803903244195452620)
XLA Ops:
  8.2 79.0 %psum.7 = f32[280]{0:T(512)S(1)} all-reduce(f32[280]{0:T(512)S(1)} %fusion.40), channel_id=1, replica_groups=mesh['gx'=32,'gy'=8] {'gx'}, use_global_device_ids=true, to_apply=%region_2.0 | all-reduce | flops 280 | bytes 2240 | tf_op jit(solution)/shard_map/psum | solution.py:93
  88.3 17.8 %all-gather.1 = bf16[8,280,160]{1,2,0:T(8,128)(2,1)S(1)} all-gather(bf16[1,280,160]{1,2,0:T(8,128)(2,1)S(1)} %fusion.44), channel_id=1, replica_groups=mesh['gx'=32,'gy'=8] {'gy'}, dimensions={0}, use_global_device_ids=true | all-gather | bytes 806400 | tf_op jit(solution)/shard_map/all_gather | solution.py:97
  107.2 4.5 fusion.62
  111.7 124.4 %fusion.8 = f32[80,896]{1,0:T(8,128)S(1)} fusion(f32[2240,896]{1,0:T(8,128)} %fusion.62), kind=kCustom, calls=%all-reduce-scatter | all-reduce-scatter fusion | flops 2293761 | bytes 8315904
  238.1 4.9 collective-permute-start.1
  247.3 3.9 collective-permute-done.3
  254.9 82.3 %all-gather.2 = bf16[32,70,128]{2,1,0:T(8,128)(2,1)S(1)} all-gather(bf16[1,70,128]{2,1,0:T(8,128)(2,1)S(1)} %copy.93), channel_id=1, replica_groups=mesh['gx'=32,'gy'=8] {'gx'}, dimensions={0}, use_global_device_ids=true | all-gather | bytes 591360 | tf_op jit(solution)/shard_map/all_gather | solution.py:73
  337.5 87.6 %all-gather = bf16[2240,1,1,128]{3,2,1,0:T(2,128)(2,1)S(1)} all-gather(bf16[70,1,1,128]{3,2,1,0:T(2,128)(2,1)S(1)} %fusion.50), channel_id=2, replica_groups=mesh['gx'=32,'gy'=8] {'gx'}, dimensions={0}, use_global_device_ids=true | all-gather | bytes 591360 | tf_op jit(solution)/shard_map/all_gather | solution.py:74
  425.2 3.3 gather_fusion.1
  428.5 3.3 gather_fusion
  432.4 7.3 reshape.441
  439.7 4.6 copy.98
  444.3 25.3 %while.24 = (s32[]{:T(128)}, bf16[5,1,5,448]{3,2,1,0:T(8,128)(2,1)S(1)}, s32[5]{0:T(128)S(1)}, s32[5]{0:T(128)S(1)}, bf16[5,272,1,128]{3,1,2,0:T(8,128)(2,1)S(1)...) while((s32[]{:T(128)}, bf16[5,1,5,448]{3,2,1,0:T(8,128)(2,1)S(1)}, ...), condition=%wide.region_7.9_spmd.clone, body=%wide.region_5.8_spmd.clone.sunk | while | flops 158046256 | bytes 932525 | solution.py:135
  469.6 149.5 %pmax.7 = bf16[5,1,5,448]{3,2,1,0:T(8,128)(2,1)S(1)} all-reduce(bf16[5,1,5,448]{3,2,1,0:T(8,128)(2,1)S(1)} %get-tuple-element.104), channel_id=1, replica_groups=mesh['gx'=32,'gy'=8] {'gx'}, use_global_device_ids=true, to_apply=%region_8.10 | all-reduce | flops 11200 | bytes 44800 | tf_op jit(solution)/shard_map/pmax | solution.py:136
  619.1 38.8 %while.25 = (s32[]{:T(128)}, bf16[5,448,640]{1,2,0:T(8,128)(2,1)}, bf16[5,448,5]{1,2,0:T(8,128)(2,1)S(1)}, bf16[5,272,1,128]{3,1,2,0:T(8,128)(2,1)S(1)}, s32[5]{...) while((s32[]{:T(128)}, bf16[5,448,640]{1,2,0:T(8,128)(2,1)}, ...), condition=%wide.region_11.13_spmd.clone, body=%wide.region_9.12_spmd.clone.sunk | while | flops 318286912 | bytes 9364173 | solution.py:152
  622.4 2.1 fusion.79
  653.5 2.1 fusion.79
  659.4 4.2 copy.99
  663.6 94.3 %fusion.9 = bf16[80,640]{1,0:T(8,128)(2,1)S(1)} fusion(bf16[2240,640]{1,0:T(8,128)(2,1)S(1)} %bitcast.157), kind=kCustom, calls=%all-reduce-scatter.1 | all-reduce-scatter fusion | flops 1638401 | bytes 2970624
  763.9 149.9 %all-reduce.2 = bf16[2240,5]{0,1:T(8,128)(2,1)S(1)} all-reduce(bf16[2240,5]{0,1:T(8,128)(2,1)S(1)} %convert_element_type.96), channel_id=5, replica_groups=mesh['gx'=32,'gy'=8] {'gx'}, use_global_device_ids=true, to_apply=%region_13.15.clone | all-reduce | flops 11200 | bytes 44800
  916.4 156.4 %all-gather.10.cloned.1.call-done = bf16[32,70,640]{2,1,0:T(8,128)(2,1)} async-done(((bf16[1,70,640]{2,1,0:T(8,128)(2,1)}), bf16[32,70,640]{2,1,0:T(8,128)(2,1)}) %all-gather.10.cloned.1.call-update) | async-done | bytes 2867216 | tf_op jit(solution)/shard_map/all_gather | solution.py:169
  1072.8 2.9 reshape.470
  1077.6 2.3 copy.104
  1079.9 39.9 %reduce-scatter.9.cloned.1.call-done = bf16[280,160]{1,0:T(8,128)(2,1)} async-done(((bf16[2240,160]{1,0:T(8,128)(2,1)}), bf16[280,160]{1,0:T(8,128)(2,1)}) %reduce-scatter.9.cloned.1.call-update) | async-done | bytes 89616
  (193 shorter events, 72.3 us)
Async XLA Ops:
  7.2 100.0 %copy-start = (bf16[160,896]{1,0:T(8,128)(2,1)S(1)}, bf16[160,896]{1,0:T(8,128)(2,1)}, u32[]{:S(2)}) copy-start(bf16[160,896]{1,0:T(8,128)(2,1)} %param.17) | copy-start | bytes 860164
  7.2 425.2 %all-gather.8.cloned.1.call-start = ((), (), s32[]{:S(2)}) async-start(), calls=%async_computation.1 | async-start | bytes 3041280 | tf_op jit(solution)/shard_map/all_gather | solution.py:72
  111.7 134.0 %copy-start.7 = (s32[5]{0:T(128)S(1)}, s32[5]{0:T(128)}, u32[]{:S(2)}) copy-start(s32[5]{0:T(128)} %param.22) | copy-start | bytes 64
  111.7 134.0 %copy-start.9 = (s32[5]{0:T(128)S(1)}, s32[5]{0:T(128)}, u32[]{:S(2)}) copy-start(s32[5]{0:T(128)} %param.23) | copy-start | bytes 64
  111.7 134.1 %copy-start.8 = (bf16[896]{0:T(1024)(128)(2,1)S(1)}, bf16[896]{0:T(1024)(128)(2,1)}, u32[]{:S(2)}) copy-start(bf16[896]{0:T(1024)(128)(2,1)} %param.18) | copy-start | bytes 5380
  111.7 134.1 %copy-start.10 = (u32[256]{0:T(256)S(1)}, u32[256]{0:T(256)}, u32[]{:S(2)}) copy-start(u32[256]{0:T(256)} %constant.106) | copy-start | bytes 3076
  236.1 15.1 %collective-permute-start = (f32[80,896]{1,0:T(8,128)S(1)}, f32[80,896]{1,0:T(8,128)S(1)}, u32[]{:S(2)}, u32[]{:S(2)}) collective-permute-start(f32[80,896]{1,0:T(8,128)S(1)} %fusion.8), channel_id=1, source_target_pairs={{0,8},{8,16},{16,24},{24,32},{32,40},{40,48},{48,56},{56,64},{64,7... | collective-permute-start | bytes 860168
  238.1 13.1 %collective-permute-start.1 = (f32[80,896]{1,0:T(8,128)S(1)}, f32[80,896]{1,0:T(8,128)S(1)}, u32[]{:S(2)}, u32[]{:S(2)}) collective-permute-start(f32[80,896]{1,0:T(8,128)S(1)} %fusion.8), channel_id=1, source_target_pairs={{0,16},{8,24},{16,32},{24,40},{32,48},{40,56},{48,64},{56,72},{64,... | collective-permute-start | bytes 860168
  242.9 8.3 collective-permute-start.2
  244.3 6.9 collective-permute-start.3
  253.4 819.4 %all-gather.10.cloned.1.call-start = ((), (), s32[]{:S(2)}) async-start(), calls=%async_computation.2 | async-start | bytes 3041280 | tf_op jit(solution)/shard_map/all_gather | solution.py:169
  425.1 6.7 copy-start.2
  425.1 6.7 copy-start.3
  657.9 0.7 copy-start.4
  658.7 0.7 copy-start.5
  757.9 156.3 %collective-permute-start.4 = (bf16[80,640]{1,0:T(8,128)(2,1)S(1)}, bf16[80,640]{1,0:T(8,128)(2,1)S(1)}, u32[]{:S(2)}, u32[]{:S(2)}) collective-permute-start(bf16[80,640]{1,0:T(8,128)(2,1)S(1)} %fusion.9), channel_id=1, source_target_pairs={{0,8},{8,16},{16,24},{24,32},{32,40},{40,48},{48,56},{56,64},{64,7... | collective-permute-start | bytes 307208
  759.8 154.3 %collective-permute-start.5 = (bf16[80,640]{1,0:T(8,128)(2,1)S(1)}, bf16[80,640]{1,0:T(8,128)(2,1)S(1)}, u32[]{:S(2)}, u32[]{:S(2)}) collective-permute-start(bf16[80,640]{1,0:T(8,128)(2,1)S(1)} %fusion.9), channel_id=1, source_target_pairs={{0,16},{8,24},{16,32},{24,40},{32,48},{40,56},{48,64},{56,72},{64,... | collective-permute-start | bytes 307208
  761.1 153.1 %collective-permute-start.6 = (bf16[80,640]{1,0:T(8,128)(2,1)S(1)}, bf16[80,640]{1,0:T(8,128)(2,1)S(1)}, u32[]{:S(2)}, u32[]{:S(2)}) collective-permute-start(bf16[80,640]{1,0:T(8,128)(2,1)S(1)} %fusion.9), channel_id=1, source_target_pairs={{0,24},{8,32},{16,40},{24,48},{32,56},{40,64},{48,72},{56,80},{64,... | collective-permute-start | bytes 307208
  762.4 151.7 %collective-permute-start.7 = (bf16[70,640]{1,0:T(8,128)(2,1)S(1)}, bf16[70,640]{1,0:T(8,128)(2,1)S(1)}, u32[]{:S(2)}, u32[]{:S(2)}) collective-permute-start(bf16[70,640]{1,0:T(8,128)(2,1)S(1)} %slice.39), channel_id=1, source_target_pairs={{0,32},{8,40},{16,48},{24,56},{32,64},{40,72},{48,80},{56,88},{64,... | collective-permute-start | bytes 268808
  916.3 159.4 %copy-start.6 = (bf16[640,160]{0,1:T(8,128)(2,1)S(1)}, bf16[640,160]{0,1:T(8,128)(2,1)}, u32[]{:S(2)}) copy-start(bf16[640,160]{0,1:T(8,128)(2,1)} %param.19) | copy-start | bytes 614404
  916.3 203.5 %reduce-scatter.9.cloned.1.call-start = ((), (), s32[]{:S(2)}) async-start(), calls=%async_computation.3 | async-start | bytes 1290240
  1077.6 43.3 %copy-start.1 = (bf16[280,160]{0,1:T(8,128)(2,1)S(1)}, bf16[280,160]{0,1:T(8,128)(2,1)}, u32[]{:S(2)}) copy-start(bf16[280,160]{0,1:T(8,128)(2,1)} %param.15) | copy-start | bytes 268804
Sparse Core Ops, SparseCore 0:
  253.5 159.6 all-gather.7
  916.4 156.2 all-gather.9
  1080.0 39.7 reduce-scatter.8
where the time goes:
time: 1130 us
  blocking collectives  785 us (69%)
  waiting for transfers between devices  200 us (18%)
  local copies, waits for them, and re-layouts  53.9 us (5%)
  matrix products  31.2 us (3%)
  between operations  15.6 us (1%)
  starting transfers between devices  15.3 us (1%)
  loops' own time  13.5 us (1%)
  other arithmetic  13.3 us (1%)
    unnamed x3, blocking collectives  369 us
    all_gather x1, waiting for transfers between devices, per_device(): lax.all_gather(attended, 'gx', axis=0, tiled=True)  156 us
    pmax x1, blocking collectives, per_device(): highest = lax.pmax(highest.astype(jnp.bfloat16), 'gx').astype(highest.dtype)  150 us
    all_gather x1, blocking collectives, share_rows(): lax.all_gather(new_values, 'gx', axis=0, tiled=True)  87.6 us
    all_gather x1, blocking collectives, share_rows(): lax.all_gather(new_keys, 'gx', axis=0, tiled=True)  82.3 us
    psum x1, blocking collectives, per_device(): squares = lax.psum(jnp.sum(hidden_f * hidden_f, axis=1), 'gx')  79 us
    unnamed x12, waiting for transfers between devices  43.9 us
  transfers between devices with their start and end apart: 11, of which 3 were waited for; matrix products, arithmetic and copies ran while one was open for 1% of the time, Pallas kernels for 0%

commit v1 on v0

--- a/solution.py
+++ b/solution.py
@@ -1,6 +1,7 @@
 import jax
 import jax.numpy as jnp
 from jax import lax
+from jax.sharding import Mesh
 from jax.sharding import PartitionSpec as P
 
 HEAD_DIM = 128
@@ -66,12 +67,36 @@
     return jnp.where(is_live[:, :, None], jnp.take(new_rows, source_rows, axis=0), cache)
 
 
+GX = ("y", "zl", "x")
+GY = ("zh", "c")
+
+
+def gather_gx(value):
+    for axis in GX[::-1]:
+        value = lax.all_gather(value, axis, axis=0, tiled=True)
+    return value
+
+
+def psum_gx(value):
+    for axis in GX[::-1]:
+        value = lax.psum(value, axis)
+    return value
+
+
+def pmax_gx(value):
+    for axis in GX[::-1]:
+        value = lax.pmax(value, axis)
+    return value
+
+
 def share_rows(share_sum, cached_len, fresh_len, first_row):
     queries, new_keys, new_values = finish_rows(share_sum, cached_len, fresh_len, first_row)
+    widths = (queries.shape[1], new_keys.shape[1])
+    joined = gather_gx(jnp.concatenate([queries, new_keys, new_values], axis=1))
     return (
-        lax.all_gather(queries, "gx", axis=0, tiled=True),
-        lax.all_gather(new_keys, "gx", axis=0, tiled=True),
-        lax.all_gather(new_values, "gx", axis=0, tiled=True),
+        joined[:, : widths[0]],
+        joined[:, widths[0] : widths[0] + widths[1]],
+        joined[:, widths[0] + widths[1] :],
     )
 
 
@@ -88,25 +113,26 @@
 ):
     scale = HEAD_DIM ** (-0.5)
     token_count = REQUESTS * NEW_TOKENS
-    model_width = hidden.shape[1] * lax.axis_size("gx")
+    gx_size = lax.psum(1, GX)
+    model_width = hidden.shape[1] * gx_size
     hidden_f = hidden.astype(jnp.float32)
-    squares = lax.psum(jnp.sum(hidden_f * hidden_f, axis=1), "gx")
+    squares = psum_gx(jnp.sum(hidden_f * hidden_f, axis=1))
     normed = (
         hidden_f * lax.rsqrt(squares / model_width + NORM_EPS)[:, None] * norm_gain[None, :]
     ).astype(jnp.bfloat16)
-    gathered = lax.all_gather(normed, "gy", axis=0, tiled=True)
+    gathered = lax.all_gather(normed, GY, axis=0, tiled=True)
     bias_f = qkv_bias.astype(jnp.float32)[None, :]
-    row_share = token_count // lax.axis_size("gx")
-    share_start = lax.axis_index("gx") * row_share
+    row_share = token_count // gx_size
+    share_start = lax.axis_index(GX) * row_share
     summed = lax.psum_scatter(
         jnp.dot(gathered, qkv_weight, preferred_element_type=jnp.float32),
-        "gx",
+        GX,
         scatter_dimension=0,
         tiled=True,
     )
     queries, new_keys, new_values = share_rows(summed + bias_f, cached_len, fresh_len, share_start)
     slot_count = key_cache.shape[1]
-    first_slot = lax.axis_index("gx") * slot_count
+    first_slot = lax.axis_index(GX) * slot_count
     key_out = append_rows(key_cache, new_keys, cached_len, fresh_len, first_slot)
     value_out = append_rows(value_cache, new_values, cached_len, fresh_len, first_slot)
     groups_here = key_cache.shape[2] // HEAD_DIM
@@ -133,7 +159,7 @@
         return jnp.max(scores_for(query_req, key_req, visible_for(cached_here, fresh_here)), axis=3)
 
     highest = lax.map(local_top, (query_blocks, key_blocks, cached_len, fresh_len))
-    highest = lax.pmax(highest.astype(jnp.bfloat16), "gx").astype(highest.dtype)
+    highest = pmax_gx(highest.astype(jnp.bfloat16)).astype(highest.dtype)
 
     def local_sums(items):
         query_req, key_req, value_req, cached_here, fresh_here, top_here = items
@@ -154,42 +180,43 @@
     )
     mixed = mixed.reshape(token_count, -1)
     denom = denom.reshape(token_count, -1)
-    mixed, denom = (
-        lax.psum_scatter(mixed.astype(jnp.bfloat16), "gx", scatter_dimension=0, tiled=True).astype(
-            jnp.float32
-        ),
-        lax.psum_scatter(denom.astype(jnp.bfloat16), "gx", scatter_dimension=0, tiled=True).astype(
-            jnp.float32
-        ),
-    )
+    mixed_width = mixed.shape[1]
+    pad = jnp.zeros((token_count, HEAD_DIM - denom.shape[1]), jnp.float32)
+    both = jnp.concatenate([mixed, denom, pad], axis=1).astype(jnp.bfloat16)
+    both = lax.psum_scatter(both, GX, scatter_dimension=0, tiled=True).astype(jnp.float32)
+    mixed = both[:, :mixed_width]
+    denom = both[:, mixed_width : mixed_width + denom.shape[1]]
     unused_pos, is_live = token_positions(cached_len, fresh_len, share_start, row_share)
     ratio = mixed.reshape(row_share, -1, HEAD_DIM) / denom[:, :, None]
     attended = jnp.where(is_live[:, None], ratio.reshape(row_share, -1), 0.0).astype(jnp.bfloat16)
     partial_out = jnp.dot(
-        lax.all_gather(attended, "gx", axis=0, tiled=True),
+        gather_gx(attended),
         out_weight,
         preferred_element_type=jnp.float32,
     )
     summed_out = lax.psum_scatter(
-        partial_out.astype(jnp.bfloat16), "gy", scatter_dimension=0, tiled=True
+        partial_out.astype(jnp.bfloat16), GY, scatter_dimension=0, tiled=True
     ).astype(jnp.float32)
     output = (hidden_f + summed_out).astype(jnp.bfloat16)
     return (output, key_out, value_out)
 
 
 def solution(mesh):
+    sub_mesh = Mesh(
+        mesh.devices.reshape(4, mesh.shape["gx"] // 16, 4, mesh.shape["gy"] // 2, 2), GX + GY
+    )
     in_specs = (
-        P("gy", "gx"),
-        P("gx"),
-        P("gx", "gy"),
-        P("gy"),
-        P("gy", "gx"),
-        P(None, "gx", "gy"),
-        P(None, "gx", "gy"),
+        P(GY, GX),
+        P(GX),
+        P(GX, GY),
+        P(GY),
+        P(GY, GX),
+        P(None, GX, GY),
+        P(None, GX, GY),
         P(),
         P(),
     )
-    out_specs = (P("gy", "gx"), P(None, "gx", "gy"), P(None, "gx", "gy"))
+    out_specs = (P(GY, GX), P(None, GX, GY), P(None, GX, GY))
     return jax.shard_map(
-        per_device, mesh=mesh, in_specs=in_specs, out_specs=out_specs, check_vma=False
-    )
+        per_device, mesh=sub_mesh, in_specs=in_specs, out_specs=out_specs, check_vma=False
+    )

time: 1130 us -> 619 us (0.55)
  blocking collectives: 785 us -> 347 us
  waiting for transfers between devices: 200 us -> 136 us
    unnamed x3 -> x2, blocking collectives: 369 us -> 217 us
    all_gather x3 -> x5, blocking collectives: 188 us -> 66.9 us  [the longest x4 46.4 us: gather_gx(): value = lax.all_gather(value, axis, axis=0, tiled=True)]
    pmax x1 -> x3, blocking collectives: 150 us -> 38.7 us  [pmax_gx(): value = lax.pmax(value, axis)]
    all_gather x2, waiting for transfers between devices: 156 us -> 87.9 us  [gather_gx(): value = lax.all_gather(value, axis, axis=0, tiled=True)]
    psum x1 -> x3, blocking collectives: 79 us -> 24.2 us  [psum_gx(): value = lax.psum(value, axis)]
    unnamed x12 -> x9, waiting for transfers between devices: 43.9 us -> 48.2 us
  transfers between devices with their start and end apart: 11 -> 8, of which waited for: 3 -> 5; matrix products, arithmetic and copies ran while one was open for 1% -> 0% of each run, Pallas kernels for 0% -> 0%
where the time goes in v1:
time: 619 us; the launch traced here: 618 us
  blocking collectives  347 us (56%)
  waiting for transfers between devices  136 us (22%)
  local copies, waits for them, and re-layouts  48.8 us (8%)
  matrix products  32.1 us (5%)
  other arithmetic  16.9 us (3%)
  between operations  15.6 us (3%)
  loops' own time  12.7 us (2%)
  starting transfers between devices  8.65 us (1%)
    unnamed x2, blocking collectives  217 us
    all_gather x2, waiting for transfers between devices, gather_gx(): value = lax.all_gather(value, axis, axis=0, tiled=True)  87.9 us
    unnamed x9, waiting for transfers between devices  48.2 us
    all_gather x4, blocking collectives, gather_gx(): value = lax.all_gather(value, axis, axis=0, tiled=True)  46.4 us
    pmax x3, blocking collectives, pmax_gx(): value = lax.pmax(value, axis)  38.7 us
    psum x3, blocking collectives, psum_gx(): value = lax.psum(value, axis)  24.2 us
    all_gather x1, blocking collectives, per_device(): gathered = lax.all_gather(normed, GY, axis=0, tiled=True)  20.5 us
    dot_general x10, matrix products, scores_for(): jnp.einsum('ikgd,pkd->kgip', query_req, key_req, preferred_element_type=j...  19.2 us
  transfers between devices with their start and end apart: 8, of which 5 were waited for; matrix products, arithmetic and copies ran while one was open for 0% of the time, Pallas kernels for 0%

profile of v1, /device:TPU:2, one launch (start us, length us, event | category | flops | bytes accessed | tf_op | source)
XLA Modules:
  0.0 617.5 jit_solution(14488319229614992455)
XLA Ops:
  8.2 10.0 %psum.21 = f32[280]{0:T(512)S(1)} all-reduce(f32[280]{0:T(512)S(1)} %fusion.40), channel_id=1, replica_groups=mesh['y'=4,'zl'=2,'x'=4,'zh'=4,'c'=2] {'x'}, use_global_device_ids=true, to_apply=%region_2.0 | all-reduce | flops 280 | bytes 2240 | tf_op jit(solution)/shard_map/psum | solution.py:82
  18.2 4.9 psum.22
  23.1 9.4 %psum.23 = f32[280]{0:T(512)S(1)} all-reduce(f32[280]{0:T(512)S(1)} %psum.22), channel_id=1, replica_groups=mesh['y'=4,'zl'=2,'x'=4,'zh'=4,'c'=2] {'y'}, use_global_device_ids=true, to_apply=%region_4.0 | all-reduce | flops 280 | bytes 2240 | tf_op jit(solution)/shard_map/psum | solution.py:82
  33.5 20.5 %all-gather = bf16[8,280,160]{1,2,0:T(8,128)(2,1)S(1)} all-gather(bf16[1,280,160]{1,2,0:T(8,128)(2,1)S(1)} %fusion.46), channel_id=1, replica_groups=mesh['y'=4,'zl'=2,'x'=4,'zh'=4,'c'=2] {'zh','c'}, dimensions={0}, use_global_device_ids=true | all-gather | bytes 806400 | tf_op jit(solution)/shard_map/all_gather | solution.py:123
  55.1 4.5 fusion.63
  59.6 121.5 %fusion.8 = f32[80,896]{1,0:T(8,128)S(1)} fusion(f32[2240,896]{1,0:T(8,128)} %fusion.63), kind=kCustom, calls=%all-reduce-scatter | all-reduce-scatter fusion | flops 2293761 | bytes 8315904
  195.2 15.6 %all-gather.1 = bf16[4,70,896]{2,1,0:T(8,128)(2,1)S(1)} all-gather(bf16[1,70,896]{2,1,0:T(8,128)(2,1)S(1)} %maximum_bitcast_fusion.1), channel_id=1, replica_groups=mesh['y'=4,'zl'=2,'x'=4,'zh'=4,'c'=2] {'x'}, dimensions={0}, use_global_device_ids=true | all-gather | bytes 627200 | tf_op jit(solution)/shard_map/all_gather | solution.py:76
  211.0 11.3 %all_gather.23 = bf16[560,896]{1,0:T(8,128)(2,1)} all-gather(bf16[280,896]{1,0:T(8,128)(2,1)S(1)} %reshape.471), channel_id=1, replica_groups=mesh['y'=4,'zl'=2,'x'=4,'zh'=4,'c'=2] {'zl'}, dimensions={0}, use_global_device_ids=true | all-gather | bytes 1505280 | tf_op jit(solution)/shard_map/all_gather | solution.py:76
  222.8 49.5 %all-gather.6.cloned.1.call-done = bf16[2240,896]{1,0:T(8,128)(2,1)} async-done(((bf16[560,896]{1,0:T(8,128)(2,1)}), bf16[2240,896]{1,0:T(8,128)(2,1)}) %all-gather.6.cloned.1.call-update) | async-done | bytes 4014096 | tf_op jit(solution)/shard_map/all_gather | solution.py:76
  274.1 5.2 reshape.445
  279.3 4.8 copy.68
  291.5 24.8 %while.24 = (s32[]{:T(128)}, bf16[5,1,5,448]{3,2,1,0:T(8,128)(2,1)S(1)}, s32[5]{0:T(128)S(1)}, s32[5]{0:T(128)S(1)}, bf16[5,272,1,128]{3,1,2,0:T(8,128)(2,1)S(1)...) while((s32[]{:T(128)}, bf16[5,1,5,448]{3,2,1,0:T(8,128)(2,1)S(1)}, ...), condition=%wide.region_9.11_spmd.clone, body=%wide.region_7.10_spmd.clone.sunk | while | flops 158046256 | bytes 932525 | solution.py:161
  316.3 14.4 %pmax.21 = bf16[5,1,5,448]{3,2,1,0:T(8,128)(2,1)S(1)} all-reduce(bf16[5,1,5,448]{3,2,1,0:T(8,128)(2,1)S(1)} %get-tuple-element.104), channel_id=1, replica_groups=mesh['y'=4,'zl'=2,'x'=4,'zh'=4,'c'=2] {'x'}, use_global_device_ids=true, to_apply=%region_10.12 | all-reduce | flops 11200 | bytes 44800 | tf_op jit(solution)/shard_map/pmax | solution.py:88
  330.7 8.5 %pmax.22 = bf16[5,1,5,448]{3,2,1,0:T(8,128)(2,1)S(1)} all-reduce(bf16[5,1,5,448]{3,2,1,0:T(8,128)(2,1)S(1)} %pmax.21), channel_id=1, replica_groups=mesh['y'=4,'zl'=2,'x'=4,'zh'=4,'c'=2] {'zl'}, use_global_device_ids=true, to_apply=%region_11.13 | all-reduce | flops 11200 | bytes 44800 | tf_op jit(solution)/shard_map/pmax | solution.py:88
  339.3 15.7 %pmax.23 = bf16[5,1,5,448]{3,2,1,0:T(8,128)(2,1)S(1)} all-reduce(bf16[5,1,5,448]{3,2,1,0:T(8,128)(2,1)S(1)} %pmax.22), channel_id=1, replica_groups=mesh['y'=4,'zl'=2,'x'=4,'zh'=4,'c'=2] {'y'}, use_global_device_ids=true, to_apply=%region_12.14 | all-reduce | flops 11200 | bytes 44800 | tf_op jit(solution)/shard_map/pmax | solution.py:88
  355.0 38.3 %while.25 = (s32[]{:T(128)}, bf16[5,448,640]{1,2,0:T(8,128)(2,1)}, bf16[5,448,5]{1,2,0:T(8,128)(2,1)S(1)}, bf16[5,272,1,128]{3,1,2,0:T(8,128)(2,1)S(1)}, s32[5]{...) while((s32[]{:T(128)}, bf16[5,448,640]{1,2,0:T(8,128)(2,1)}, ...), condition=%wide.region_15.17_spmd.clone, body=%wide.region_13.16_spmd.clone.sunk | while | flops 318286912 | bytes 9364173 | solution.py:178
  394.0 4.3 copy.69
  399.5 3.5 maximum_maximum_fusion
  403.0 95.4 %fusion.9 = bf16[72,768]{1,0:T(8,128)(2,1)S(1)} fusion(bf16[2240,768]{1,0:T(8,128)(2,1)} %maximum_maximum_fusion), kind=kCustom, calls=%all-reduce-scatter.1 | all-reduce-scatter fusion | flops 1769473 | bytes 3552256
  501.2 4.7 collective-permute-done.4
  506.5 11.3 %all-gather.2 = bf16[4,70,640]{2,1,0:T(8,128)(2,1)S(1)} all-gather(bf16[1,70,640]{2,1,0:T(8,128)(2,1)S(1)} %fusion.47), channel_id=1, replica_groups=mesh['y'=4,'zl'=2,'x'=4,'zh'=4,'c'=2] {'x'}, dimensions={0}, use_global_device_ids=true | all-gather | bytes 448000 | tf_op jit(solution)/shard_map/all_gather | solution.py:76
  517.9 8.2 %all_gather.26 = bf16[560,640]{1,0:T(8,128)(2,1)} all-gather(bf16[280,640]{1,0:T(8,128)(2,1)S(1)} %reshape.473), channel_id=1, replica_groups=mesh['y'=4,'zl'=2,'x'=4,'zh'=4,'c'=2] {'zl'}, dimensions={0}, use_global_device_ids=true | all-gather | bytes 1075200 | tf_op jit(solution)/shard_map/all_gather | solution.py:76
  526.2 38.4 %all-gather.8.cloned.1.call-done = bf16[2240,640]{1,0:T(8,128)(2,1)} async-done(((bf16[560,640]{1,0:T(8,128)(2,1)}), bf16[2240,640]{1,0:T(8,128)(2,1)}) %all-gather.8.cloned.1.call-update) | async-done | bytes 2867216 | tf_op jit(solution)/shard_map/all_gather | solution.py:76
  568.9 40.4 %reduce-scatter.8.cloned.1.call-done = bf16[280,160]{1,0:T(8,128)(2,1)} async-done(((bf16[2240,160]{1,0:T(8,128)(2,1)}), bf16[280,160]{1,0:T(8,128)(2,1)}) %reduce-scatter.8.cloned.1.call-update) | async-done | bytes 89616
  (209 shorter events, 87.1 us)
Async XLA Ops:
  7.2 47.9 %copy-start = (bf16[160,896]{1,0:T(8,128)(2,1)S(1)}, bf16[160,896]{1,0:T(8,128)(2,1)}, u32[]{:S(2)}) copy-start(bf16[160,896]{1,0:T(8,128)(2,1)} %param.17) | copy-start | bytes 860164
  7.2 265.1 %all-gather.6.cloned.1.call-start = ((), (), s32[]{:S(2)}) async-start(), calls=%async_computation.1 | async-start | bytes 5017600 | tf_op jit(solution)/shard_map/all_gather | solution.py:76
  59.6 128.1 %copy-start.9 = (s32[5]{0:T(128)S(1)}, s32[5]{0:T(128)}, u32[]{:S(2)}) copy-start(s32[5]{0:T(128)} %param.22) | copy-start | bytes 64
  59.6 128.1 %copy-start.12 = (s32[5]{0:T(128)S(1)}, s32[5]{0:T(128)}, u32[]{:S(2)}) copy-start(s32[5]{0:T(128)} %param.23) | copy-start | bytes 64
  59.6 128.8 %copy-start.11 = (bf16[896]{0:T(1024)(128)(2,1)S(1)}, bf16[896]{0:T(1024)(128)(2,1)}, u32[]{:S(2)}) copy-start(bf16[896]{0:T(1024)(128)(2,1)} %param.18) | copy-start | bytes 5380
  59.6 128.9 %copy-start.15 = (u32[256]{0:T(256)S(1)}, u32[256]{0:T(256)}, u32[]{:S(2)}) copy-start(u32[256]{0:T(256)} %constant.122) | copy-start | bytes 3076
  181.1 11.8 %collective-permute-start = (f32[80,896]{1,0:T(8,128)S(1)}, f32[80,896]{1,0:T(8,128)S(1)}, u32[]{:S(2)}, u32[]{:S(2)}) collective-permute-start(f32[80,896]{1,0:T(8,128)S(1)} %fusion.8), channel_id=1, source_target_pairs={{0,8},{8,16},{16,24},{24,32},{32,40},{40,48},{48,56},{56,64},{64,7... | collective-permute-start | bytes 860168
  183.1 9.9 %collective-permute-start.1 = (f32[80,896]{1,0:T(8,128)S(1)}, f32[80,896]{1,0:T(8,128)S(1)}, u32[]{:S(2)}, u32[]{:S(2)}) collective-permute-start(f32[80,896]{1,0:T(8,128)S(1)} %fusion.8), channel_id=1, source_target_pairs={{0,16},{8,24},{16,32},{24,40},{32,48},{40,56},{48,64},{56,72},{64,... | collective-permute-start | bytes 860168
  184.8 8.2 %collective-permute-start.2 = (f32[80,896]{1,0:T(8,128)S(1)}, f32[80,896]{1,0:T(8,128)S(1)}, u32[]{:S(2)}, u32[]{:S(2)}) collective-permute-start(f32[80,896]{1,0:T(8,128)S(1)} %fusion.8), channel_id=1, source_target_pairs={{0,24},{8,32},{16,40},{24,48},{32,56},{40,64},{48,72},{56,80},{64,... | collective-permute-start | bytes 860168
  186.1 6.9 %collective-permute-start.3 = (f32[70,896]{1,0:T(8,128)S(1)}, f32[70,896]{1,0:T(8,128)S(1)}, u32[]{:S(2)}, u32[]{:S(2)}) collective-permute-start(f32[70,896]{1,0:T(8,128)S(1)} %slice.63), channel_id=1, source_target_pairs={{0,32},{8,40},{16,48},{24,56},{32,64},{40,72},{48,80},{56,88},{64,... | collective-permute-start | bytes 752648
  222.3 342.2 %all-gather.8.cloned.1.call-start = ((), (), s32[]{:S(2)}) async-start(), calls=%async_computation.2 | async-start | bytes 3584000 | tf_op jit(solution)/shard_map/all_gather | solution.py:76
  272.3 1.8 slice-start
  279.3 4.8 copy-start.1
  284.2 6.7 %copy-start.3 = (bf16[5,272,128]{2,1,0:T(8,128)(2,1)S(1)}, bf16[5,272,128]{2,1,0:T(8,128)(2,1)}, u32[]{:S(2)}) copy-start(bf16[5,272,128]{2,1,0:T(8,128)(2,1)} %param.20) | copy-start | bytes 1044484
  284.2 6.7 %copy-start.4 = (bf16[5,272,128]{2,1,0:T(8,128)(2,1)S(1)}, bf16[5,272,128]{2,1,0:T(8,128)(2,1)}, u32[]{:S(2)}) copy-start(bf16[5,272,128]{2,1,0:T(8,128)(2,1)} %param.21) | copy-start | bytes 1044484
  287.5 4.0 copy-start.8
  287.5 4.0 copy-start.10
  287.5 4.0 copy-start.13
  394.0 4.3 copy-start.5
  403.0 97.6 %copy-start.14 = (s32[70]{0:T(128)S(1)}, s32[70]{0:T(128)}, u32[]{:S(2)}) copy-start(s32[70]{0:T(128)} %get-tuple-element.234) | copy-start | bytes 844
  498.5 66.0 %copy-start.7 = (bf16[640,160]{0,1:T(8,128)(2,1)S(1)}, bf16[640,160]{0,1:T(8,128)(2,1)}, u32[]{:S(2)}) copy-start(bf16[640,160]{0,1:T(8,128)(2,1)} %param.19) | copy-start | bytes 614404
  498.5 7.4 %collective-permute-start.4 = (bf16[62,768]{1,0:T(8,128)(2,1)S(1)}, bf16[62,768]{1,0:T(8,128)(2,1)S(1)}, u32[]{:S(2)}, u32[]{:S(2)}) collective-permute-start(bf16[62,768]{1,0:T(8,128)(2,1)S(1)} %slice.64), channel_id=1, source_target_pairs={{0,8},{8,16},{16,24},{24,32},{32,40},{40,48},{48,56},{56,64},{64,7... | collective-permute-start | bytes 285704
  526.1 83.2 %reduce-scatter.8.cloned.1.call-start = ((), (), s32[]{:S(2)}) async-start(), calls=%async_computation.3 | async-start | bytes 1290240
  567.4 42.9 %copy-start.2 = (bf16[280,160]{0,1:T(8,128)(2,1)S(1)}, bf16[280,160]{0,1:T(8,128)(2,1)}, u32[]{:S(2)}) copy-start(bf16[280,160]{0,1:T(8,128)(2,1)} %param.15) | copy-start | bytes 268804
  (1 other events, 0.7 us)
Sparse Core Ops, SparseCore 0:
  222.4 49.7 all-gather.5
  526.2 38.2 all-gather.7
  569.0 40.2 reduce-scatter.7

commit v2 on v1

--- a/solution.py
+++ b/solution.py
@@ -154,17 +154,14 @@
         )
         return jnp.where(visible[None, None], scores, NEG_LARGE)
 
-    def local_top(items):
-        query_req, key_req, cached_here, fresh_here = items
-        return jnp.max(scores_for(query_req, key_req, visible_for(cached_here, fresh_here)), axis=3)
-
-    highest = lax.map(local_top, (query_blocks, key_blocks, cached_len, fresh_len))
-    highest = pmax_gx(highest.astype(jnp.bfloat16)).astype(highest.dtype)
-
     def local_sums(items):
-        query_req, key_req, value_req, cached_here, fresh_here, top_here = items
+        query_req, key_req, value_req, cached_here, fresh_here = items
         visible = visible_for(cached_here, fresh_here)
         scores = scores_for(query_req, key_req, visible)
+        top = jnp.max(scores, axis=3)
+        top_hi = top.astype(jnp.bfloat16)
+        top_lo = (top - top_hi.astype(jnp.float32)).astype(jnp.bfloat16)
+        top_here = top_hi.astype(jnp.float32) + top_lo.astype(jnp.float32)
         weighted = jnp.where(visible[None, None], jnp.exp(scores - top_here[..., None]), 0.0)
         denom = jnp.sum(weighted, axis=3)
         mixed = jnp.einsum(
@@ -173,21 +170,37 @@
             value_req,
             preferred_element_type=jnp.float32,
         )
-        return (mixed.reshape(NEW_TOKENS, -1), denom.reshape(-1, NEW_TOKENS).T)
-
-    mixed, denom = lax.map(
-        local_sums, (query_blocks, key_blocks, value_blocks, cached_len, fresh_len, highest)
-    )
+        stats = jnp.concatenate(
+            [
+                top_hi.astype(jnp.float32).reshape(-1, NEW_TOKENS).T,
+                top_lo.astype(jnp.float32).reshape(-1, NEW_TOKENS).T,
+                denom.reshape(-1, NEW_TOKENS).T,
+            ],
+            axis=1,
+        )
+        return (mixed.reshape(NEW_TOKENS, -1), stats)
+
+    mixed, stats = lax.map(local_sums, (query_blocks, key_blocks, value_blocks, cached_len, fresh_len))
     mixed = mixed.reshape(token_count, -1)
-    denom = denom.reshape(token_count, -1)
+    stats = stats.reshape(token_count, -1)
     mixed_width = mixed.shape[1]
-    pad = jnp.zeros((token_count, HEAD_DIM - denom.shape[1]), jnp.float32)
-    both = jnp.concatenate([mixed, denom, pad], axis=1).astype(jnp.bfloat16)
-    both = lax.psum_scatter(both, GX, scatter_dimension=0, tiled=True).astype(jnp.float32)
-    mixed = both[:, :mixed_width]
-    denom = both[:, mixed_width : mixed_width + denom.shape[1]]
+    heads_here = mixed_width // HEAD_DIM
+    pad = jnp.zeros((token_count, HEAD_DIM - stats.shape[1]), jnp.float32)
+    both = jnp.concatenate([mixed, stats, pad], axis=1).astype(jnp.bfloat16)
+    both = lax.all_to_all(both, GX, 0, 0, tiled=True).astype(jnp.float32)
+    both = both.reshape(gx_size, row_share, -1)
+    parts = both[:, :, :mixed_width].reshape(gx_size, row_share, heads_here, HEAD_DIM)
+    part_top = (
+        both[:, :, mixed_width : mixed_width + heads_here]
+        + both[:, :, mixed_width + heads_here : mixed_width + 2 * heads_here]
+    )
+    part_denom = both[:, :, mixed_width + 2 * heads_here : mixed_width + 3 * heads_here]
+    top_all = jnp.max(part_top, axis=0)
+    scale_k = jnp.exp(part_top - top_all[None])
+    denom = jnp.sum(part_denom * scale_k, axis=0)
+    mixed = jnp.sum(parts * scale_k[..., None], axis=0)
     unused_pos, is_live = token_positions(cached_len, fresh_len, share_start, row_share)
-    ratio = mixed.reshape(row_share, -1, HEAD_DIM) / denom[:, :, None]
+    ratio = mixed / denom[:, :, None]
     attended = jnp.where(is_live[:, None], ratio.reshape(row_share, -1), 0.0).astype(jnp.bfloat16)
     partial_out = jnp.dot(
         gather_gx(attended),

time: 619 us -> 543 us (0.88)
  blocking collectives: 347 us -> 213 us
  waiting for transfers between devices: 136 us -> 180 us
  local copies, waits for them, and re-layouts: 48.8 us -> 64 us
  matrix products: 32.1 us -> 21.6 us
  other arithmetic: 16.9 us -> 27.1 us
    unnamed x2 -> x1, blocking collectives: 217 us -> 122 us
    all_to_all x0 -> x1, waiting for transfers between devices: none -> 47 us  [per_device(): both = lax.all_to_all(both, GX, 0, 0, tiled=True).astype(jnp.float32)]
    pmax x3 -> x0, blocking collectives: 38.7 us -> none  [pmax_gx(): value = lax.pmax(value, axis)]
    mul x0 -> x2, local copies, waits for them, and re-layouts: none -> 14.4 us  [per_device(): mixed = jnp.sum(parts * scale_k[..., None], axis=0)]
    reduce_sum x0 -> x7, other arithmetic: none -> 11.9 us  [the longest x1 7.56 us: per_device(): mixed = jnp.sum(parts * scale_k[..., None], axis=0)]
    dot_general x10 -> x5, matrix products: 19.2 us -> 8.64 us  [scores_for(): jnp.einsum('ikgd,pkd->kgip', query_req, key_req, preferred_element_type=j...]
    all_to_all x0 -> x1, starting transfers between devices: none -> 7.48 us  [per_device(): both = lax.all_to_all(both, GX, 0, 0, tiled=True).astype(jnp.float32)]
    another operation x1 -> x0, loops' own time: 6.31 us -> none  [per_device(): lax.map(local_top, (query_blocks, key_blocks, cached_len, fresh_len))]
where the time goes in v2:
time: 543 us; the launch traced here: 542 us
  blocking collectives  213 us (39%)
  waiting for transfers between devices  180 us (33%)
  local copies, waits for them, and re-layouts  64 us (12%)
  other arithmetic  27.1 us (5%)
  matrix products  21.6 us (4%)
  between operations  14.9 us (3%)
  starting transfers between devices  14.2 us (3%)
  loops' own time  6.66 us (1%)
    unnamed x1, blocking collectives  122 us
    all_gather x2, waiting for transfers between devices, gather_gx(): value = lax.all_gather(value, axis, axis=0, tiled=True)  89.2 us
    all_to_all x1, waiting for transfers between devices, per_device(): both = lax.all_to_all(both, GX, 0, 0, tiled=True).astype(jnp.float32)  47 us
    all_gather x4, blocking collectives, gather_gx(): value = lax.all_gather(value, axis, axis=0, tiled=True)  46.6 us
    unnamed x8, waiting for transfers between devices  44.3 us
    psum x3, blocking collectives, psum_gx(): value = lax.psum(value, axis)  24.2 us
    all_gather x1, blocking collectives, per_device(): gathered = lax.all_gather(normed, GY, axis=0, tiled=True)  20.5 us
    mul x2, local copies, waits for them, and re-layouts, per_device(): mixed = jnp.sum(parts * scale_k[..., None], axis=0)  14.4 us
  transfers between devices with their start and end apart: 8, of which 5 were waited for; matrix products, arithmetic and copies ran while one was open for 0% of the time, Pallas kernels for 0%

profile of v2, /device:TPU:2, one launch (start us, length us, event | category | flops | bytes accessed | tf_op | source)
XLA Modules:
  0.0 541.8 jit_solution(11192574640374812477)
XLA Ops:
  8.2 10.0 %psum.21 = f32[280]{0:T(512)S(1)} all-reduce(f32[280]{0:T(512)S(1)} %fusion.35), channel_id=1, replica_groups=mesh['y'=4,'zl'=2,'x'=4,'zh'=4,'c'=2] {'x'}, use_global_device_ids=true, to_apply=%region_2.0 | all-reduce | flops 280 | bytes 2240 | tf_op jit(solution)/shard_map/psum | solution.py:82
  18.2 4.9 psum.22
  23.1 9.4 %psum.23 = f32[280]{0:T(512)S(1)} all-reduce(f32[280]{0:T(512)S(1)} %psum.22), channel_id=1, replica_groups=mesh['y'=4,'zl'=2,'x'=4,'zh'=4,'c'=2] {'y'}, use_global_device_ids=true, to_apply=%region_4.0 | all-reduce | flops 280 | bytes 2240 | tf_op jit(solution)/shard_map/psum | solution.py:82
  33.5 20.5 %all-gather = bf16[8,280,160]{1,2,0:T(8,128)(2,1)S(1)} all-gather(bf16[1,280,160]{1,2,0:T(8,128)(2,1)S(1)} %fusion.39), channel_id=1, replica_groups=mesh['y'=4,'zl'=2,'x'=4,'zh'=4,'c'=2] {'zh','c'}, dimensions={0}, use_global_device_ids=true | all-gather | bytes 806400 | tf_op jit(solution)/shard_map/all_gather | solution.py:123
  55.1 4.5 fusion.56
  59.6 121.6 %fusion.4 = f32[80,896]{1,0:T(8,128)S(1)} fusion(f32[2240,896]{1,0:T(8,128)} %fusion.56), kind=kCustom, calls=%all-reduce-scatter | all-reduce-scatter fusion | flops 2293761 | bytes 8315904
  189.3 3.8 collective-permute-done.3
  195.4 15.8 %all-gather.1 = bf16[4,70,896]{2,1,0:T(8,128)(2,1)S(1)} all-gather(bf16[1,70,896]{2,1,0:T(8,128)(2,1)S(1)} %maximum_bitcast_fusion.2), channel_id=1, replica_groups=mesh['y'=4,'zl'=2,'x'=4,'zh'=4,'c'=2] {'x'}, dimensions={0}, use_global_device_ids=true | all-gather | bytes 627200 | tf_op jit(solution)/shard_map/all_gather | solution.py:76
  211.3 11.1 %all_gather.23 = bf16[560,896]{1,0:T(8,128)(2,1)} all-gather(bf16[280,896]{1,0:T(8,128)(2,1)S(1)} %reshape.435), channel_id=1, replica_groups=mesh['y'=4,'zl'=2,'x'=4,'zh'=4,'c'=2] {'zl'}, dimensions={0}, use_global_device_ids=true | all-gather | bytes 1505280 | tf_op jit(solution)/shard_map/all_gather | solution.py:76
  222.9 49.6 %all-gather.6.cloned.1.call-done = bf16[2240,896]{1,0:T(8,128)(2,1)} async-done(((bf16[560,896]{1,0:T(8,128)(2,1)}), bf16[2240,896]{1,0:T(8,128)(2,1)}) %all-gather.6.cloned.1.call-update) | async-done | bytes 4014096 | tf_op jit(solution)/shard_map/all_gather | solution.py:76
  274.2 5.2 reshape.411
  279.5 4.8 copy.64
  291.6 40.5 %while.13 = (s32[]{:T(128)}, bf16[5,448,640]{1,2,0:T(8,128)(2,1)}, bf16[5,448,15]{1,2,0:T(8,128)(2,1)S(1)}, bf16[5,272,1,128]{3,1,2,0:T(8,128)(2,1)S(1)}, s32[5]...) while((s32[]{:T(128)}, bf16[5,448,640]{1,2,0:T(8,128)(2,1)}, ...), condition=%wide.region_10.12_spmd.clone, body=%wide.region_7.11_spmd.clone.sunk | while | flops 320177472 | bytes 11967169 | solution.py:183
  333.0 5.5 %copy.65 = bf16[5,448,640]{2,1,0:T(8,128)(2,1)} copy(bf16[5,448,640]{1,2,0:T(8,128)(2,1)} %get-tuple-element.57) | data formatting | bytes 5734400 | tf_op jit(solution)/shard_map/convert.4
  343.1 3.5 maximum_maximum_fusion
  346.6 7.5 %all-to-all-start = ((bf16[32,70,768]{2,1,0:T(8,128)(2,1)}), bf16[32,70,768]{2,1,0:T(8,128)(2,1)}, u32[]{:S(2)}, u32[]{:S(2)}) async-start(bf16[32,70,768]{2,1,0:T(8,128)(2,1)} %maximum_maximum_fusion), calls=%async_computation | async-start | bytes 7077888 | tf_op jit(solution)/shard_map/all_to_all | solution.py:190
  354.4 47.0 %all-to-all-done = bf16[32,70,768]{2,1,0:T(8,128)(2,1)} async-done(((bf16[32,70,768]{2,1,0:T(8,128)(2,1)}), bf16[32,70,768]{2,1,0:T(8,128)(2,1)}, u32[]{:S(2)}, u32[]{:S(2)}) %all-to-all-start) | async-done | bytes 3440672 | tf_op jit(solution)/shard_map/all_to_all | solution.py:190
  407.0 5.4 %mul.186 = f32[32,70,5,128]{3,2,0,1:T(8,128)} broadcast(f32[32,70,5]{2,0,1:T(8,128)S(1)} %copy.68), dimensions={0,1,2} | broadcast | bytes 5779200 | tf_op jit(solution)/shard_map/mul | solution.py:201
  412.5 9.0 %mul.187 = f32[32,70,640]{2,0,1:T(8,128)} reshape(f32[32,70,5,128]{3,2,0,1:T(8,128)} %mul.186) | data formatting | bytes 11468800 | tf_op jit(solution)/shard_map/mul | solution.py:201
  421.5 7.6 %fusion.32 = f32[70,640]{1,0:T(8,128)S(1)} fusion(f32[32,70,768]{2,1,0:T(8,128)} %copy-done.2, f32[32,70,640]{2,0,1:T(8,128)} %mul.187), kind=kLoop, calls=%fused_computation.41 | loop fusion | flops 2822400 | bytes 11648000 | tf_op jit(solution)/shard_map/reduce_sum | solution.py:201
  429.3 11.3 %all-gather.2 = bf16[4,70,640]{2,1,0:T(8,128)(2,1)S(1)} all-gather(bf16[1,70,640]{2,1,0:T(8,128)(2,1)S(1)} %fusion.40), channel_id=1, replica_groups=mesh['y'=4,'zl'=2,'x'=4,'zh'=4,'c'=2] {'x'}, dimensions={0}, use_global_device_ids=true | all-gather | bytes 448000 | tf_op jit(solution)/shard_map/all_gather | solution.py:76
  440.7 8.4 %all_gather.26 = bf16[560,640]{1,0:T(8,128)(2,1)} all-gather(bf16[280,640]{1,0:T(8,128)(2,1)S(1)} %reshape.437), channel_id=1, replica_groups=mesh['y'=4,'zl'=2,'x'=4,'zh'=4,'c'=2] {'zl'}, dimensions={0}, use_global_device_ids=true | all-gather | bytes 1075200 | tf_op jit(solution)/shard_map/all_gather | solution.py:76
  449.2 39.6 %all-gather.8.cloned.1.call-done = bf16[2240,640]{1,0:T(8,128)(2,1)} async-done(((bf16[560,640]{1,0:T(8,128)(2,1)}), bf16[2240,640]{1,0:T(8,128)(2,1)}) %all-gather.8.cloned.1.call-update) | async-done | bytes 2867216 | tf_op jit(solution)/shard_map/all_gather | solution.py:76
  493.2 40.4 %reduce-scatter.6.cloned.1.call-done = bf16[280,160]{1,0:T(8,128)(2,1)} async-done(((bf16[2240,160]{1,0:T(8,128)(2,1)}), bf16[280,160]{1,0:T(8,128)(2,1)}) %reduce-scatter.6.cloned.1.call-update) | async-done | bytes 89616
  (174 shorter events, 73.9 us)
Async XLA Ops:
  7.2 47.9 %copy-start = (bf16[160,896]{1,0:T(8,128)(2,1)S(1)}, bf16[160,896]{1,0:T(8,128)(2,1)}, u32[]{:S(2)}) copy-start(bf16[160,896]{1,0:T(8,128)(2,1)} %param.15) | copy-start | bytes 860164
  7.2 265.3 %all-gather.6.cloned.1.call-start = ((), (), s32[]{:S(2)}) async-start(), calls=%async_computation.2 | async-start | bytes 5017600 | tf_op jit(solution)/shard_map/all_gather | solution.py:76
  59.6 128.1 %copy-start.10 = (s32[5]{0:T(128)S(1)}, s32[5]{0:T(128)}, u32[]{:S(2)}) copy-start(s32[5]{0:T(128)} %param.20) | copy-start | bytes 64
  59.6 128.1 %copy-start.12 = (s32[5]{0:T(128)S(1)}, s32[5]{0:T(128)}, u32[]{:S(2)}) copy-start(s32[5]{0:T(128)} %param.21) | copy-start | bytes 64
  59.6 128.3 %copy-start.11 = (bf16[896]{0:T(1024)(128)(2,1)S(1)}, bf16[896]{0:T(1024)(128)(2,1)}, u32[]{:S(2)}) copy-start(bf16[896]{0:T(1024)(128)(2,1)} %param.16) | copy-start | bytes 5380
  59.6 128.3 %copy-start.13 = (u32[256]{0:T(256)S(1)}, u32[256]{0:T(256)}, u32[]{:S(2)}) copy-start(u32[256]{0:T(256)} %constant.108) | copy-start | bytes 3076
  181.2 11.9 %collective-permute-start = (f32[80,896]{1,0:T(8,128)S(1)}, f32[80,896]{1,0:T(8,128)S(1)}, u32[]{:S(2)}, u32[]{:S(2)}) collective-permute-start(f32[80,896]{1,0:T(8,128)S(1)} %fusion.4), channel_id=1, source_target_pairs={{0,8},{8,16},{16,24},{24,32},{32,40},{40,48},{48,56},{56,64},{64,7... | collective-permute-start | bytes 860168
  183.1 10.0 %collective-permute-start.1 = (f32[80,896]{1,0:T(8,128)S(1)}, f32[80,896]{1,0:T(8,128)S(1)}, u32[]{:S(2)}, u32[]{:S(2)}) collective-permute-start(f32[80,896]{1,0:T(8,128)S(1)} %fusion.4), channel_id=1, source_target_pairs={{0,16},{8,24},{16,32},{24,40},{32,48},{40,56},{48,64},{56,72},{64,... | collective-permute-start | bytes 860168
  184.9 8.2 %collective-permute-start.2 = (f32[80,896]{1,0:T(8,128)S(1)}, f32[80,896]{1,0:T(8,128)S(1)}, u32[]{:S(2)}, u32[]{:S(2)}) collective-permute-start(f32[80,896]{1,0:T(8,128)S(1)} %fusion.4), channel_id=1, source_target_pairs={{0,24},{8,32},{16,40},{24,48},{32,56},{40,64},{48,72},{56,80},{64,... | collective-permute-start | bytes 860168
  186.3 6.9 %collective-permute-start.3 = (f32[70,896]{1,0:T(8,128)S(1)}, f32[70,896]{1,0:T(8,128)S(1)}, u32[]{:S(2)}, u32[]{:S(2)}) collective-permute-start(f32[70,896]{1,0:T(8,128)S(1)} %slice.73), channel_id=1, source_target_pairs={{0,32},{8,40},{16,48},{24,56},{32,64},{40,72},{48,80},{56,88},{64,... | collective-permute-start | bytes 752648
  272.4 1.8 slice-start
  279.5 4.8 copy-start.3
  284.3 6.7 %copy-start.6 = (bf16[5,272,128]{2,1,0:T(8,128)(2,1)S(1)}, bf16[5,272,128]{2,1,0:T(8,128)(2,1)}, u32[]{:S(2)}) copy-start(bf16[5,272,128]{2,1,0:T(8,128)(2,1)} %param.18) | copy-start | bytes 1044484
  284.3 6.7 %copy-start.7 = (bf16[5,272,128]{2,1,0:T(8,128)(2,1)S(1)}, bf16[5,272,128]{2,1,0:T(8,128)(2,1)}, u32[]{:S(2)}) copy-start(bf16[5,272,128]{2,1,0:T(8,128)(2,1)} %param.19) | copy-start | bytes 1044484
  332.1 0.7 copy-start.4
  332.1 0.8 copy-start.8
  346.6 54.8 %all-to-all-start = ((bf16[32,70,768]{2,1,0:T(8,128)(2,1)}), bf16[32,70,768]{2,1,0:T(8,128)(2,1)}, u32[]{:S(2)}, u32[]{:S(2)}) async-start(bf16[32,70,768]{2,1,0:T(8,128)(2,1)} %maximum_maximum_fusion), calls=%async_computation | async-start | bytes 7077888 | tf_op jit(solution)/shard_map/all_to_all | solution.py:190
  354.1 134.7 %all-gather.8.cloned.1.call-start = ((), (), s32[]{:S(2)}) async-start(), calls=%async_computation.3 | async-start | bytes 3584000 | tf_op jit(solution)/shard_map/all_gather | solution.py:76
  403.9 2.9 copy-start.2
  429.0 59.8 %copy-start.9 = (bf16[640,160]{0,1:T(8,128)(2,1)S(1)}, bf16[640,160]{0,1:T(8,128)(2,1)}, u32[]{:S(2)}) copy-start(bf16[640,160]{0,1:T(8,128)(2,1)} %param.17) | copy-start | bytes 614404
  449.1 84.4 %reduce-scatter.6.cloned.1.call-start = ((), (), s32[]{:S(2)}) async-start(), calls=%async_computation.4 | async-start | bytes 1290240
  488.8 46.5 %copy-start.1 = (bf16[160,896]{1,0:T(8,128)(2,1)S(1)}, bf16[160,896]{1,0:T(8,128)(2,1)}, u32[]{:S(2)}) copy-start(bf16[160,896]{1,0:T(8,128)(2,1)} %param.15) | copy-start | bytes 860164
  491.7 42.9 %copy-start.5 = (bf16[280,160]{0,1:T(8,128)(2,1)S(1)}, bf16[280,160]{0,1:T(8,128)(2,1)}, u32[]{:S(2)}) copy-start(bf16[280,160]{0,1:T(8,128)(2,1)} %param.13) | copy-start | bytes 268804
Sparse Core Ops, SparseCore 0:
  222.6 49.7 all-gather.5
  449.2 39.5 all-gather.7
  493.3 40.2 reduce-scatter.5

commit v3 on v2

--- a/solution.py
+++ b/solution.py
@@ -116,20 +116,20 @@
     gx_size = lax.psum(1, GX)
     model_width = hidden.shape[1] * gx_size
     hidden_f = hidden.astype(jnp.float32)
-    squares = psum_gx(jnp.sum(hidden_f * hidden_f, axis=1))
-    normed = (
-        hidden_f * lax.rsqrt(squares / model_width + NORM_EPS)[:, None] * norm_gain[None, :]
-    ).astype(jnp.bfloat16)
-    gathered = lax.all_gather(normed, GY, axis=0, tiled=True)
+    gathered = lax.all_gather(hidden, GY, axis=0, tiled=True).astype(jnp.float32)
+    squares = jnp.sum(gathered * gathered, axis=1, keepdims=True)
+    gained = (gathered * norm_gain[None, :]).astype(jnp.bfloat16)
     bias_f = qkv_bias.astype(jnp.float32)[None, :]
     row_share = token_count // gx_size
     share_start = lax.axis_index(GX) * row_share
-    summed = lax.psum_scatter(
-        jnp.dot(gathered, qkv_weight, preferred_element_type=jnp.float32),
-        GX,
-        scatter_dimension=0,
-        tiled=True,
-    )
+    partial = jnp.dot(gained, qkv_weight, preferred_element_type=jnp.float32)
+    proj_width = partial.shape[1]
+    pad = jnp.zeros((token_count, HEAD_DIM - 1), jnp.float32)
+    payload = jnp.concatenate([partial, squares, pad], axis=1).astype(jnp.bfloat16)
+    payload = lax.all_to_all(payload, GX, 0, 0, tiled=True).astype(jnp.float32)
+    payload = jnp.sum(payload.reshape(gx_size, row_share, -1), axis=0)
+    scale_row = lax.rsqrt(payload[:, proj_width : proj_width + 1] / model_width + NORM_EPS)
+    summed = payload[:, :proj_width] * scale_row
     queries, new_keys, new_values = share_rows(summed + bias_f, cached_len, fresh_len, share_start)
     slot_count = key_cache.shape[1]
     first_slot = lax.axis_index(GX) * slot_count

time: 543 us -> 467 us (0.86)
  blocking collectives: 213 us -> 63.8 us
  waiting for transfers between devices: 180 us -> 240 us
  other arithmetic: 27.1 us -> 34.4 us
  local copies, waits for them, and re-layouts: 64 us -> 70.4 us
    unnamed x1 -> x0, blocking collectives: 122 us -> none
    all_to_all x0 -> x1, waiting for transfers between devices: none -> 65.2 us  [per_device(): payload = lax.all_to_all(payload, GX, 0, 0, tiled=True).astype(jnp.float32)]
    psum x3 -> x0, blocking collectives: 24.2 us -> none  [psum_gx(): value = lax.psum(value, axis)]
    all_to_all x0 -> x1, starting transfers between devices: none -> 8.42 us  [per_device(): payload = lax.all_to_all(payload, GX, 0, 0, tiled=True).astype(jnp.float32)]
    unnamed x5 -> x1, starting transfers between devices: 6.45 us -> 0.04 us
    concatenate x0 -> x3, local copies, waits for them, and re-layouts: none -> 5.72 us  [per_device(): jnp.concatenate([partial, squares, pad], axis=1).astype(jnp.bfloat16)]
    concatenate x0 -> x1, other arithmetic: none -> 5.52 us  [per_device(): jnp.concatenate([partial, squares, pad], axis=1).astype(jnp.bfloat16)]
    unnamed x8 -> x4, waiting for transfers between devices: 44.3 us -> 40.6 us
  transfers between devices with their start and end apart: 8 -> 5, of which waited for: 5 -> 5; matrix products, arithmetic and copies ran while one was open for 0% -> 0% of each run, Pallas kernels for 0% -> 0%
where the time goes in v3:
time: 467 us; the launch traced here: 466 us
  waiting for transfers between devices  240 us (51%)
  local copies, waits for them, and re-layouts  70.4 us (15%)
  blocking collectives  63.8 us (14%)
  other arithmetic  34.4 us (7%)
  matrix products  20.5 us (4%)
  starting transfers between devices  16.2 us (3%)
  between operations  14.2 us (3%)
  loops' own time  6.42 us (1%)
    all_gather x2, waiting for transfers between devices, gather_gx(): value = lax.all_gather(value, axis, axis=0, tiled=True)  87.1 us
    all_to_all x1, waiting for transfers between devices, per_device(): payload = lax.all_to_all(payload, GX, 0, 0, tiled=True).astype(jnp.float32)  65.2 us
    all_to_all x1, waiting for transfers between devices, per_device(): both = lax.all_to_all(both, GX, 0, 0, tiled=True).astype(jnp.float32)  47 us
    all_gather x4, blocking collectives, gather_gx(): value = lax.all_gather(value, axis, axis=0, tiled=True)  43 us
    unnamed x4, waiting for transfers between devices  40.6 us
    all_gather x1, blocking collectives, per_device(): lax.all_gather(hidden, GY, axis=0, tiled=True).astype(jnp.float32)  20.8 us
    mul x2, local copies, waits for them, and re-layouts, per_device(): mixed = jnp.sum(parts * scale_k[..., None], axis=0)  14.4 us
    unnamed x39, local copies, waits for them, and re-layouts  10.4 us
  transfers between devices with their start and end apart: 5, of which 5 were waited for; matrix products, arithmetic and copies ran while one was open for 0% of the time, Pallas kernels for 0%

profile of v3, /device:TPU:2, one launch (start us, length us, event | category | flops | bytes accessed | tf_op | source)
XLA Modules:
  0.0 465.7 jit_solution(7638515817862231481)
XLA Ops:
  7.2 20.8 %all-gather = bf16[8,280,160]{1,2,0:T(8,128)(2,1)S(1)} all-gather(bf16[1,280,160]{1,2,0:T(8,128)(2,1)} %bitcast.141), channel_id=1, replica_groups=mesh['y'=4,'zl'=2,'x'=4,'zh'=4,'c'=2] {'zh','c'}, dimensions={0}, use_global_device_ids=true | all-gather | bytes 806400 | tf_op jit(solution)/shard_map/all_gather | solution.py:119
  31.7 3.4 convolution_convert_fusion
  35.1 5.1 %concatenate.40 = bf16[32,70,896]{2,1,0:T(8,128)(2,1)} reshape(bf16[2240,896]{1,0:T(8,128)(2,1)} %convolution_convert_fusion) | data formatting | bytes 8028160 | tf_op jit(solution)/shard_map/concatenate | solution.py:128
  40.8 5.5 %maximum_maximum_fusion = bf16[32,70,1024]{2,1,0:T(8,128)(2,1)} fusion(bf16[32,70,1]{2,1,0:T(8,128)(2,1)S(1)} %concatenate.51, bf16[32,70,896]{2,1,0:T(8,128)(2,1)} %concatenate.40, bf16[1024]{0:T(1024)(128)(2,1)S(1)} %pad.14.clone), kind=kLoop, calls=%fused_computation.44 | loop fusion | flops 13762560 | bytes 8608128 | tf_op jit(solution)/shard_map/concatenate | solution.py:128
  46.4 8.4 %all-to-all-start = ((bf16[32,70,1024]{2,1,0:T(8,128)(2,1)}), bf16[32,70,1024]{2,1,0:T(8,128)(2,1)}, u32[]{:S(2)}, u32[]{:S(2)}) async-start(bf16[32,70,1024]{2,1,0:T(8,128)(2,1)} %maximum_maximum_fusion), calls=%async_computation | async-start | bytes 9437184 | tf_op jit(solution)/shard_map/all_to_all | solution.py:129
  55.3 65.2 %all-to-all-done = bf16[32,70,1024]{2,1,0:T(8,128)(2,1)} async-done(((bf16[32,70,1024]{2,1,0:T(8,128)(2,1)}), bf16[32,70,1024]{2,1,0:T(8,128)(2,1)}, u32[]{:S(2)}, u32[]{:S(2)}) %all-to-all-start) | async-done | bytes 4587552 | tf_op jit(solution)/shard_map/all_to_all | solution.py:129
  120.5 3.4 convert_reduce_fusion
  125.3 11.9 %all-gather.1 = bf16[4,70,896]{2,1,0:T(8,128)(2,1)S(1)} all-gather(bf16[1,70,896]{2,1,0:T(8,128)(2,1)S(1)} %maximum_bitcast_fusion.2), channel_id=1, replica_groups=mesh['y'=4,'zl'=2,'x'=4,'zh'=4,'c'=2] {'x'}, dimensions={0}, use_global_device_ids=true | all-gather | bytes 627200 | tf_op jit(solution)/shard_map/all_gather | solution.py:76
  137.4 11.4 %all_gather.23 = bf16[560,896]{1,0:T(8,128)(2,1)} all-gather(bf16[280,896]{1,0:T(8,128)(2,1)S(1)} %reshape.443), channel_id=1, replica_groups=mesh['y'=4,'zl'=2,'x'=4,'zh'=4,'c'=2] {'zl'}, dimensions={0}, use_global_device_ids=true | all-gather | bytes 1505280 | tf_op jit(solution)/shard_map/all_gather | solution.py:76
  149.2 47.4 %all-gather.6.cloned.1.call-done = bf16[2240,896]{1,0:T(8,128)(2,1)} async-done(((bf16[560,896]{1,0:T(8,128)(2,1)}), bf16[2240,896]{1,0:T(8,128)(2,1)}) %all-gather.6.cloned.1.call-update) | async-done | bytes 4014096 | tf_op jit(solution)/shard_map/all_gather | solution.py:76
  198.4 5.2 %reshape.419 = bf16[5,448,1,5,128]{4,3,1,0,2:T(8,128)(2,1)} reshape(bf16[2240,640]{1,0:T(8,128)(2,1)S(1)} %slice-done) | data formatting | bytes 5734400 | tf_op jit(solution)/shard_map/reshape | solution.py:139
  203.7 4.8 %copy.94 = bf16[5,448,1,5,128]{4,1,3,2,0:T(8,128)(2,1)} copy(bf16[5,448,1,5,128]{4,3,1,0,2:T(8,128)(2,1)} %reshape.419) | data formatting | bytes 5734400
  215.8 40.1 %while.13 = (s32[]{:T(128)}, bf16[5,448,640]{1,2,0:T(8,128)(2,1)}, bf16[5,448,15]{1,2,0:T(8,128)(2,1)S(1)}, bf16[5,272,1,128]{3,1,2,0:T(8,128)(2,1)S(1)}, s32[5]...) while((s32[]{:T(128)}, bf16[5,448,640]{1,2,0:T(8,128)(2,1)}, ...), condition=%wide.region_7.9_spmd.clone, body=%wide.region_4.8_spmd.clone.sunk | while | flops 320177472 | bytes 11967169 | solution.py:183
  256.7 5.5 %copy.95 = bf16[5,448,640]{2,1,0:T(8,128)(2,1)} copy(bf16[5,448,640]{1,2,0:T(8,128)(2,1)} %get-tuple-element.57) | data formatting | bytes 5734400 | tf_op jit(solution)/shard_map/convert.4
  266.8 3.6 maximum_maximum_fusion.1
  270.4 7.5 %all-to-all-start.1 = ((bf16[32,70,768]{2,1,0:T(8,128)(2,1)}), bf16[32,70,768]{2,1,0:T(8,128)(2,1)}, u32[]{:S(2)}, u32[]{:S(2)}) async-start(bf16[32,70,768]{2,1,0:T(8,128)(2,1)} %maximum_maximum_fusion.1), calls=%async_computation.1 | async-start | bytes 7077888 | tf_op jit(solution)/shard_map/all_to_all | solution.py:190
  278.1 47.0 %all-to-all-done.1 = bf16[32,70,768]{2,1,0:T(8,128)(2,1)} async-done(((bf16[32,70,768]{2,1,0:T(8,128)(2,1)}), bf16[32,70,768]{2,1,0:T(8,128)(2,1)}, u32[]{:S(2)}, u32[]{:S(2)}) %all-to-all-start.1) | async-done | bytes 3440672 | tf_op jit(solution)/shard_map/all_to_all | solution.py:190
  330.8 5.4 %mul.189 = f32[32,70,5,128]{3,2,0,1:T(8,128)} broadcast(f32[32,70,5]{2,0,1:T(8,128)S(1)} %copy.98), dimensions={0,1,2} | broadcast | bytes 5779200 | tf_op jit(solution)/shard_map/mul | solution.py:201
  336.2 9.0 %mul.190 = f32[32,70,640]{2,0,1:T(8,128)} reshape(f32[32,70,5,128]{3,2,0,1:T(8,128)} %mul.189) | data formatting | bytes 11468800 | tf_op jit(solution)/shard_map/mul | solution.py:201
  345.2 7.6 %fusion.31 = f32[70,640]{1,0:T(8,128)S(1)} fusion(f32[32,70,768]{2,1,0:T(8,128)} %copy-done.2, f32[32,70,640]{2,0,1:T(8,128)} %mul.190), kind=kLoop, calls=%fused_computation.42 | loop fusion | flops 2822400 | bytes 11648000 | tf_op jit(solution)/shard_map/reduce_sum | solution.py:201
  353.1 11.3 %all-gather.2 = bf16[4,70,640]{2,1,0:T(8,128)(2,1)S(1)} all-gather(bf16[1,70,640]{2,1,0:T(8,128)(2,1)S(1)} %fusion.36), channel_id=1, replica_groups=mesh['y'=4,'zl'=2,'x'=4,'zh'=4,'c'=2] {'x'}, dimensions={0}, use_global_device_ids=true | all-gather | bytes 448000 | tf_op jit(solution)/shard_map/all_gather | solution.py:76
  364.4 8.4 %all_gather.26 = bf16[560,640]{1,0:T(8,128)(2,1)} all-gather(bf16[280,640]{1,0:T(8,128)(2,1)S(1)} %reshape.445), channel_id=1, replica_groups=mesh['y'=4,'zl'=2,'x'=4,'zh'=4,'c'=2] {'zl'}, dimensions={0}, use_global_device_ids=true | all-gather | bytes 1075200 | tf_op jit(solution)/shard_map/all_gather | solution.py:76
  372.9 39.7 %all-gather.8.cloned.1.call-done = bf16[2240,640]{1,0:T(8,128)(2,1)} async-done(((bf16[560,640]{1,0:T(8,128)(2,1)}), bf16[2240,640]{1,0:T(8,128)(2,1)}) %all-gather.8.cloned.1.call-update) | async-done | bytes 2867216 | tf_op jit(solution)/shard_map/all_gather | solution.py:76
  416.9 40.5 %reduce-scatter.4.cloned.1.call-done = bf16[280,160]{1,0:T(8,128)(2,1)} async-done(((bf16[2240,160]{1,0:T(8,128)(2,1)}), bf16[280,160]{1,0:T(8,128)(2,1)}) %reduce-scatter.4.cloned.1.call-update) | async-done | bytes 89616
  (166 shorter events, 67.1 us)
Async XLA Ops:
  7.2 24.5 %copy-start = (bf16[160,896]{1,0:T(8,128)(2,1)S(1)}, bf16[160,896]{1,0:T(8,128)(2,1)}, u32[]{:S(2)}) copy-start(bf16[160,896]{1,0:T(8,128)(2,1)} %param.15) | copy-start | bytes 860164
  29.6 2.1 copy-start.11
  46.4 8.5 %copy-start.12 = (bf16[896]{0:T(1024)(128)(2,1)S(1)}, bf16[896]{0:T(1024)(128)(2,1)}, u32[]{:S(2)}) copy-start(bf16[896]{0:T(1024)(128)(2,1)} %param.16) | copy-start | bytes 5380
  46.4 8.6 %copy-start.10 = (s32[5]{0:T(128)S(1)}, s32[5]{0:T(128)}, u32[]{:S(2)}) copy-start(s32[5]{0:T(128)} %param.20) | copy-start | bytes 64
  46.4 8.6 %copy-start.13 = (s32[5]{0:T(128)S(1)}, s32[5]{0:T(128)}, u32[]{:S(2)}) copy-start(s32[5]{0:T(128)} %param.21) | copy-start | bytes 64
  46.4 74.1 %all-to-all-start = ((bf16[32,70,1024]{2,1,0:T(8,128)(2,1)}), bf16[32,70,1024]{2,1,0:T(8,128)(2,1)}, u32[]{:S(2)}, u32[]{:S(2)}) async-start(bf16[32,70,1024]{2,1,0:T(8,128)(2,1)} %maximum_maximum_fusion), calls=%async_computation | async-start | bytes 9437184 | tf_op jit(solution)/shard_map/all_to_all | solution.py:129
  54.8 141.8 %all-gather.6.cloned.1.call-start = ((), (), s32[]{:S(2)}) async-start(), calls=%async_computation.3 | async-start | bytes 5017600 | tf_op jit(solution)/shard_map/all_gather | solution.py:76
  196.6 1.8 slice-start
  203.7 4.8 %copy-start.3 = (bf16[2240,896]{1,0:T(8,128)(2,1)S(1)}, bf16[2240,896]{1,0:T(8,128)(2,1)}, u32[]{:S(2)}) copy-start(bf16[2240,896]{1,0:T(8,128)(2,1)} %all-gather.6.cloned.1.call-done) | copy-start | bytes 12042244
  208.5 6.7 %copy-start.6 = (bf16[5,272,128]{2,1,0:T(8,128)(2,1)S(1)}, bf16[5,272,128]{2,1,0:T(8,128)(2,1)}, u32[]{:S(2)}) copy-start(bf16[5,272,128]{2,1,0:T(8,128)(2,1)} %param.18) | copy-start | bytes 1044484
  208.5 6.7 %copy-start.7 = (bf16[5,272,128]{2,1,0:T(8,128)(2,1)S(1)}, bf16[5,272,128]{2,1,0:T(8,128)(2,1)}, u32[]{:S(2)}) copy-start(bf16[5,272,128]{2,1,0:T(8,128)(2,1)} %param.19) | copy-start | bytes 1044484
  255.9 0.7 copy-start.4
  255.9 0.8 copy-start.8
  270.4 54.8 %all-to-all-start.1 = ((bf16[32,70,768]{2,1,0:T(8,128)(2,1)}), bf16[32,70,768]{2,1,0:T(8,128)(2,1)}, u32[]{:S(2)}, u32[]{:S(2)}) async-start(bf16[32,70,768]{2,1,0:T(8,128)(2,1)} %maximum_maximum_fusion.1), calls=%async_computation.1 | async-start | bytes 7077888 | tf_op jit(solution)/shard_map/all_to_all | solution.py:190
  277.9 134.7 %all-gather.8.cloned.1.call-start = ((), (), s32[]{:S(2)}) async-start(), calls=%async_computation.4 | async-start | bytes 3584000 | tf_op jit(solution)/shard_map/all_gather | solution.py:76
  327.7 2.9 copy-start.2
  352.7 59.8 %copy-start.9 = (bf16[640,160]{0,1:T(8,128)(2,1)S(1)}, bf16[640,160]{0,1:T(8,128)(2,1)}, u32[]{:S(2)}) copy-start(bf16[640,160]{0,1:T(8,128)(2,1)} %param.17) | copy-start | bytes 614404
  372.8 84.6 %reduce-scatter.4.cloned.1.call-start = ((), (), s32[]{:S(2)}) async-start(), calls=%async_computation.5 | async-start | bytes 1290240
  412.6 46.6 %copy-start.1 = (bf16[160,896]{1,0:T(8,128)(2,1)S(1)}, bf16[160,896]{1,0:T(8,128)(2,1)}, u32[]{:S(2)}) copy-start(bf16[160,896]{1,0:T(8,128)(2,1)} %param.15) | copy-start | bytes 860164
  415.4 43.1 %copy-start.5 = (bf16[280,160]{0,1:T(8,128)(2,1)S(1)}, bf16[280,160]{0,1:T(8,128)(2,1)}, u32[]{:S(2)}) copy-start(bf16[280,160]{0,1:T(8,128)(2,1)} %param.13) | copy-start | bytes 268804
Sparse Core Ops, SparseCore 0:
  149.0 47.5 all-gather.5
  373.0 39.5 all-gather.7
  417.1 40.3 reduce-scatter.3

commit v4 on v3

--- a/solution.py
+++ b/solution.py
@@ -142,45 +142,39 @@
     slot_pos = first_slot + jnp.arange(slot_count, dtype=jnp.int32)
     query_pos = jnp.arange(NEW_TOKENS, dtype=jnp.int32)
 
-    def visible_for(cached_here, fresh_here):
-        return (slot_pos[None, :] < cached_here + fresh_here) & (
-            slot_pos[None, :] <= cached_here + query_pos[:, None]
-        )
-
-    def scores_for(query_req, key_req, visible):
-        scores = (
-            jnp.einsum("ikgd,pkd->kgip", query_req, key_req, preferred_element_type=jnp.float32)
-            * scale
-        )
-        return jnp.where(visible[None, None], scores, NEG_LARGE)
-
-    def local_sums(items):
-        query_req, key_req, value_req, cached_here, fresh_here = items
-        visible = visible_for(cached_here, fresh_here)
-        scores = scores_for(query_req, key_req, visible)
-        top = jnp.max(scores, axis=3)
-        top_hi = top.astype(jnp.bfloat16)
-        top_lo = (top - top_hi.astype(jnp.float32)).astype(jnp.bfloat16)
-        top_here = top_hi.astype(jnp.float32) + top_lo.astype(jnp.float32)
-        weighted = jnp.where(visible[None, None], jnp.exp(scores - top_here[..., None]), 0.0)
-        denom = jnp.sum(weighted, axis=3)
-        mixed = jnp.einsum(
-            "kgip,pkd->ikgd",
-            weighted.astype(jnp.bfloat16),
-            value_req,
-            preferred_element_type=jnp.float32,
-        )
-        stats = jnp.concatenate(
-            [
-                top_hi.astype(jnp.float32).reshape(-1, NEW_TOKENS).T,
-                top_lo.astype(jnp.float32).reshape(-1, NEW_TOKENS).T,
-                denom.reshape(-1, NEW_TOKENS).T,
-            ],
-            axis=1,
-        )
-        return (mixed.reshape(NEW_TOKENS, -1), stats)
-
-    mixed, stats = lax.map(local_sums, (query_blocks, key_blocks, value_blocks, cached_len, fresh_len))
+    total_len = (cached_len + fresh_len)[:, None, None]
+    visible = (slot_pos[None, None, :] < total_len) & (
+        slot_pos[None, None, :] <= cached_len[:, None, None] + query_pos[None, :, None]
+    )
+    scores = (
+        jnp.einsum("rikgd,rpkd->rkgip", query_blocks, key_blocks, preferred_element_type=jnp.float32)
+        * scale
+    )
+    scores = jnp.where(visible[:, None, None], scores, NEG_LARGE)
+    top = jnp.max(scores, axis=4)
+    top_hi = top.astype(jnp.bfloat16)
+    top_lo = (top - top_hi.astype(jnp.float32)).astype(jnp.bfloat16)
+    top_here = top_hi.astype(jnp.float32) + top_lo.astype(jnp.float32)
+    weighted = jnp.where(visible[:, None, None], jnp.exp(scores - top_here[..., None]), 0.0)
+    denom = jnp.sum(weighted, axis=4)
+    mixed = jnp.einsum(
+        "rkgip,rpkd->rikgd",
+        weighted.astype(jnp.bfloat16),
+        value_blocks,
+        preferred_element_type=jnp.float32,
+    )
+
+    def per_token(stat):
+        return stat.transpose(0, 3, 1, 2).reshape(token_count, -1)
+
+    stats = jnp.concatenate(
+        [
+            per_token(top_hi.astype(jnp.float32)),
+            per_token(top_lo.astype(jnp.float32)),
+            per_token(denom),
+        ],
+        axis=1,
+    )
     mixed = mixed.reshape(token_count, -1)
     stats = stats.reshape(token_count, -1)
     mixed_width = mixed.shape[1]
@@ -207,9 +201,9 @@
         out_weight,
         preferred_element_type=jnp.float32,
     )
-    summed_out = lax.psum_scatter(
-        partial_out.astype(jnp.bfloat16), GY, scatter_dimension=0, tiled=True
-    ).astype(jnp.float32)
+    gy_size = lax.psum(1, GY)
+    summed_out = lax.all_to_all(partial_out.astype(jnp.bfloat16), GY, 0, 0, tiled=True)
+    summed_out = jnp.sum(summed_out.astype(jnp.float32).reshape(gy_size, token_count // gy_size, -1), axis=0)
     output = (hidden_f + summed_out).astype(jnp.bfloat16)
     return (output, key_out, value_out)
 

time: 467 us -> 454 us (0.972)
  waiting for transfers between devices: 240 us -> 198 us
  blocking collectives: 63.8 us -> 98.1 us
  loops' own time: 6.42 us -> 0 us
  matrix products: 20.5 us -> 25.9 us
    unnamed x4 -> x2, waiting for transfers between devices: 40.6 us -> 0.03 us
    all_to_all x0 -> x1, blocking collectives: none -> 34.3 us  [per_device(): lax.all_to_all(partial_out.astype(jnp.bfloat16), GY, 0, 0, tiled=True)]
    concatenate x4 -> x8, local copies, waits for them, and re-layouts: 4.58 us -> 17.3 us  [per_device(): both = jnp.concatenate([mixed, stats, pad], axis=1).astype(jnp.bfloat16)]
    unnamed x39 -> x32, local copies, waits for them, and re-layouts: 10.4 us -> 2.07 us
    another operation x1 -> x0, loops' own time: 6.42 us -> none  [per_device(): lax.map(local_sums, (query_blocks, key_blocks, value_blocks, cached_len,...]
    dynamic_slice x10 -> x0, local copies, waits for them, and re-layouts: 5.79 us -> none  [per_device(): lax.map(local_sums, (query_blocks, key_blocks, value_blocks, cached_len,...]
    dot_general x10 -> x2, matrix products: 14.2 us -> 19.7 us  [the longest x1 9.94 us: per_device(): jnp.einsum('rkgip,rpkd->rikgd', weighted.astype(jnp.bfloat16), value_bloc...]
    reshape x1 -> x0, local copies, waits for them, and re-layouts: 5.25 us -> none  [per_device(): queries.reshape(REQUESTS, NEW_TOKENS, groups_here, GROUP, HEAD_DIM)]
  transfers between devices with their start and end apart: 5 -> 4, of which waited for: 5 -> 4; matrix products, arithmetic and copies ran while one was open for 0% -> 0% of each run, Pallas kernels for 0% -> 0%
where the time goes in v4:
time: 454 us; the launch traced here: 453 us
  waiting for transfers between devices  198 us (44%)
  blocking collectives  98.1 us (22%)
  local copies, waits for them, and re-layouts  65.9 us (15%)
  other arithmetic  34.3 us (8%)
  matrix products  25.9 us (6%)
  starting transfers between devices  16 us (4%)
  between operations  14.5 us (3%)
    all_gather x2, waiting for transfers between devices, gather_gx(): value = lax.all_gather(value, axis, axis=0, tiled=True)  85.7 us
    all_to_all x1, waiting for transfers between devices, per_device(): payload = lax.all_to_all(payload, GX, 0, 0, tiled=True).astype(jnp.float32)  65.2 us
    all_to_all x1, waiting for transfers between devices, per_device(): both = lax.all_to_all(both, GX, 0, 0, tiled=True).astype(jnp.float32)  47.2 us
    all_gather x4, blocking collectives, gather_gx(): value = lax.all_gather(value, axis, axis=0, tiled=True)  43 us
    all_to_all x1, blocking collectives, per_device(): lax.all_to_all(partial_out.astype(jnp.bfloat16), GY, 0, 0, tiled=True)  34.3 us
    all_gather x1, blocking collectives, per_device(): lax.all_gather(hidden, GY, axis=0, tiled=True).astype(jnp.float32)  20.8 us
    concatenate x8, local copies, waits for them, and re-layouts, per_device(): both = jnp.concatenate([mixed, stats, pad], axis=1).astype(jnp.bfloat16)  17.3 us
    mul x2, local copies, waits for them, and re-layouts, per_device(): mixed = jnp.sum(parts * scale_k[..., None], axis=0)  14.4 us
  transfers between devices with their start and end apart: 4, of which 4 were waited for; matrix products, arithmetic and copies ran while one was open for 0% of the time, Pallas kernels for 0%

profile of v4, /device:TPU:2, one launch (start us, length us, event | category | flops | bytes accessed | tf_op | source)
XLA Modules:
  0.0 452.9 jit_solution(15350733865433363649)
XLA Ops:
  7.2 20.8 %all-gather = bf16[8,280,160]{1,2,0:T(8,128)(2,1)S(1)} all-gather(bf16[1,280,160]{1,2,0:T(8,128)(2,1)} %bitcast.104), channel_id=1, replica_groups=mesh['y'=4,'zl'=2,'x'=4,'zh'=4,'c'=2] {'zh','c'}, dimensions={0}, use_global_device_ids=true | all-gather | bytes 806400 | tf_op jit(solution)/shard_map/all_gather | solution.py:119
  35.1 5.1 %concatenate.41 = bf16[32,70,896]{2,1,0:T(8,128)(2,1)} reshape(bf16[2240,896]{1,0:T(8,128)(2,1)} %convolution_convert_fusion) | data formatting | bytes 8028160 | tf_op jit(solution)/shard_map/concatenate | solution.py:128
  40.8 5.5 %maximum_maximum_fusion = bf16[32,70,1024]{2,1,0:T(8,128)(2,1)} fusion(bf16[32,70,1]{2,1,0:T(8,128)(2,1)S(1)} %concatenate.53, bf16[32,70,896]{2,1,0:T(8,128)(2,1)} %concatenate.41, bf16[1024]{0:T(1024)(128)(2,1)S(1)} %pad.8.clone), kind=kLoop, calls=%fused_computation.14 | loop fusion | flops 13762560 | bytes 8608128 | tf_op jit(solution)/shard_map/concatenate | solution.py:128
  46.3 8.4 %all-to-all-start = ((bf16[32,70,1024]{2,1,0:T(8,128)(2,1)}), bf16[32,70,1024]{2,1,0:T(8,128)(2,1)}, u32[]{:S(2)}, u32[]{:S(2)}) async-start(bf16[32,70,1024]{2,1,0:T(8,128)(2,1)} %maximum_maximum_fusion), calls=%async_computation | async-start | bytes 9437184 | tf_op jit(solution)/shard_map/all_to_all | solution.py:129
  55.2 65.2 %all-to-all-done = bf16[32,70,1024]{2,1,0:T(8,128)(2,1)} async-done(((bf16[32,70,1024]{2,1,0:T(8,128)(2,1)}), bf16[32,70,1024]{2,1,0:T(8,128)(2,1)}, u32[]{:S(2)}, u32[]{:S(2)}) %all-to-all-start) | async-done | bytes 4587552 | tf_op jit(solution)/shard_map/all_to_all | solution.py:129
  125.3 11.9 %all-gather.1 = bf16[4,70,896]{2,1,0:T(8,128)(2,1)S(1)} all-gather(bf16[1,70,896]{2,1,0:T(8,128)(2,1)S(1)} %maximum_bitcast_fusion.1), channel_id=1, replica_groups=mesh['y'=4,'zl'=2,'x'=4,'zh'=4,'c'=2] {'x'}, dimensions={0}, use_global_device_ids=true | all-gather | bytes 627200 | tf_op jit(solution)/shard_map/all_gather | solution.py:76
  137.3 11.4 %all_gather.23 = bf16[560,896]{1,0:T(8,128)(2,1)} all-gather(bf16[280,896]{1,0:T(8,128)(2,1)S(1)} %reshape.460), channel_id=1, replica_groups=mesh['y'=4,'zl'=2,'x'=4,'zh'=4,'c'=2] {'zl'}, dimensions={0}, use_global_device_ids=true | all-gather | bytes 1505280 | tf_op jit(solution)/shard_map/all_gather | solution.py:76
  150.6 46.0 %all-gather.6.cloned.1.call-done = bf16[2240,896]{1,0:T(8,128)(2,1)} async-done(((bf16[560,896]{1,0:T(8,128)(2,1)}), bf16[2240,896]{1,0:T(8,128)(2,1)}) %all-gather.6.cloned.1.call-update) | async-done | bytes 4014096 | tf_op jit(solution)/shard_map/all_gather | solution.py:76
  207.1 5.3 %reshape.435 = bf16[5,448,5,128]{3,2,1,0:T(8,128)(2,1)} reshape(bf16[2240,640]{1,0:T(8,128)(2,1)S(1)} %slice-done) | data formatting | bytes 5734400 | tf_op jit(solution)/shard_map/reshape.13
  214.1 9.7 %fusion = (f32[5,5,448]{2,1,0:T(8,128)S(1)}, f32[5,272,448,5]{2,1,3,0:T(8,128)}) fusion(pred[5,448,272]{1,2,0:T(8,128)(4,1)} %compare_and_fusion, bf16[5,448,5,128]{3,2,1,0:T(8,128)(2,1)} %reshape.435, bf16[5,272,128]{2,1,0:T(8,128)(2,1)S(1)} %get-tuple-element.17), kind=kOutput, calls=%fused_computation.4 | convolution fusion | flops 789006400 | bytes 16055040 | tf_op jit(solution)/shard_map/rikgd,rpkd->rkgip/dot_general | solution.py:150
  223.8 8.5 %fusion.1 = bf16[5,5,448]{2,1,0:T(8,128)(2,1)S(1)} fusion(f32[5,272,448,5]{2,1,3,0:T(8,128)} %get-tuple-element.24, f32[5,5,448]{2,1,0:T(8,128)S(1)} %get-tuple-element.13, pred[5,448,272]{1,2,0:T(8,128)(4,1)S(1)} %copy-done.3), kind=kLoop, calls=%fused_computation.5 | loop fusion | flops 15220800 | bytes 12862080 | tf_op jit(solution)/shard_map/reduce_sum | solution.py:159
  233.8 9.9 %convert_bitcast_fusion = bf16[5,448,1,5,128]{4,1,3,0,2:T(8,128)(2,1)S(1)} fusion(f32[5,272,448,5]{2,1,3,0:T(8,128)} %get-tuple-element.24, f32[5,5,448]{2,1,0:T(8,128)S(1)} %get-tuple-element.13, pred[5,448,272]{1,2,0:T(8,128)(4,1)S(1)} %copy-done.3, bf16[5,272,128]{2,1,0:T(8,128)(2,1)S(1)} %get-tuple-element.16), kind=kOutput, calls=%fused_computation.18 | convolution fusion | flops 796544000 | bytes 16055040 | tf_op jit(solution)/shard_map/rkgip,rpkd->rikgd/dot_general | solution.py:160
  243.7 4.1 copy.90
  247.9 6.2 %concatenate.48 = bf16[32,70,640]{2,1,0:T(8,128)(2,1)S(1)} reshape(bf16[5,448,1,5,128]{4,3,1,0,2:T(8,128)(2,1)} %copy.90) | data formatting | bytes 5734400 | tf_op jit(solution)/shard_map/concatenate | solution.py:183
  257.8 6.9 %concatenate.52 = bf16[32,70,768]{2,1,0:T(8,128)(2,1)} concatenate(bf16[32,70,640]{2,1,0:T(8,128)(2,1)S(1)} %concatenate.48, bf16[32,70,5]{2,1,0:T(8,128)(2,1)} %copy.94, bf16[32,70,5]{2,1,0:T(8,128)(2,1)} %copy.95, bf16[32,70,5]{2,1,0:T(8,128)(2,1)} %copy.96, bf16[32,70,113]{2,1,0:T(8,128)(2,1)} %broadcast_in_dim.118), dimensions={2} | concatenate | bytes 6881280 | tf_op jit(solution)/shard_map/concatenate | solution.py:183
  264.7 7.5 %all-to-all-start.1 = ((bf16[32,70,768]{2,1,0:T(8,128)(2,1)}), bf16[32,70,768]{2,1,0:T(8,128)(2,1)}, u32[]{:S(2)}, u32[]{:S(2)}) async-start(bf16[32,70,768]{2,1,0:T(8,128)(2,1)} %concatenate.52), calls=%async_computation.1 | async-start | bytes 7077888 | tf_op jit(solution)/shard_map/all_to_all | solution.py:184
  272.3 47.2 %all-to-all-done.1 = bf16[32,70,768]{2,1,0:T(8,128)(2,1)} async-done(((bf16[32,70,768]{2,1,0:T(8,128)(2,1)}), bf16[32,70,768]{2,1,0:T(8,128)(2,1)}, u32[]{:S(2)}, u32[]{:S(2)}) %all-to-all-start.1) | async-done | bytes 3440672 | tf_op jit(solution)/shard_map/all_to_all | solution.py:184
  324.9 5.4 %mul.196 = f32[32,70,5,128]{3,2,0,1:T(8,128)} broadcast(f32[32,70,5]{2,0,1:T(8,128)S(1)} %copy.97), dimensions={0,1,2} | broadcast | bytes 5779200 | tf_op jit(solution)/shard_map/mul | solution.py:195
  330.3 9.0 %mul.197 = f32[32,70,640]{2,0,1:T(8,128)} reshape(f32[32,70,5,128]{3,2,0,1:T(8,128)} %mul.196) | data formatting | bytes 11468800 | tf_op jit(solution)/shard_map/mul | solution.py:195
  339.3 7.6 %fusion.7 = f32[70,640]{1,0:T(8,128)S(1)} fusion(f32[32,70,768]{2,1,0:T(8,128)} %copy-done.2, f32[32,70,640]{2,0,1:T(8,128)} %mul.197), kind=kLoop, calls=%fused_computation.12 | loop fusion | flops 2822400 | bytes 11648000 | tf_op jit(solution)/shard_map/reduce_sum | solution.py:195
  347.2 11.3 %all-gather.2 = bf16[4,70,640]{2,1,0:T(8,128)(2,1)S(1)} all-gather(bf16[1,70,640]{2,1,0:T(8,128)(2,1)S(1)} %fusion.18), channel_id=1, replica_groups=mesh['y'=4,'zl'=2,'x'=4,'zh'=4,'c'=2] {'x'}, dimensions={0}, use_global_device_ids=true | all-gather | bytes 448000 | tf_op jit(solution)/shard_map/all_gather | solution.py:76
  358.6 8.4 %all_gather.26 = bf16[560,640]{1,0:T(8,128)(2,1)} all-gather(bf16[280,640]{1,0:T(8,128)(2,1)S(1)} %reshape.462), channel_id=1, replica_groups=mesh['y'=4,'zl'=2,'x'=4,'zh'=4,'c'=2] {'zl'}, dimensions={0}, use_global_device_ids=true | all-gather | bytes 1075200 | tf_op jit(solution)/shard_map/all_gather | solution.py:76
  367.0 39.7 %all-gather.8.cloned.1.call-done = bf16[2240,640]{1,0:T(8,128)(2,1)} async-done(((bf16[560,640]{1,0:T(8,128)(2,1)}), bf16[2240,640]{1,0:T(8,128)(2,1)}) %all-gather.8.cloned.1.call-update) | async-done | bytes 2867216 | tf_op jit(solution)/shard_map/all_gather | solution.py:76
  410.9 34.3 %all_to_all.21 = bf16[8,280,160]{1,2,0:T(8,128)(2,1)S(1)} all-to-all(bf16[8,280,160]{1,2,0:T(8,128)(2,1)S(1)} %copy.99), channel_id=1, replica_groups=mesh['y'=4,'zl'=2,'x'=4,'zh'=4,'c'=2] {'zh','c'}, dimensions={0} | all-to-all | bytes 1433600 | tf_op jit(solution)/shard_map/all_to_all | solution.py:205
  (100 shorter events, 42.9 us)
Async XLA Ops:
  7.2 24.5 %copy-start = (bf16[160,896]{1,0:T(8,128)(2,1)S(1)}, bf16[160,896]{1,0:T(8,128)(2,1)}, u32[]{:S(2)}) copy-start(bf16[160,896]{1,0:T(8,128)(2,1)} %param.13) | copy-start | bytes 860164
  7.2 24.5 %copy-start.9 = (f32[160]{0:T(256)S(1)}, f32[160]{0:T(256)}, u32[]{:S(2)}) copy-start(f32[160]{0:T(256)} %param.12) | copy-start | bytes 1924
  46.3 8.5 %copy-start.10 = (bf16[896]{0:T(1024)(128)(2,1)S(1)}, bf16[896]{0:T(1024)(128)(2,1)}, u32[]{:S(2)}) copy-start(bf16[896]{0:T(1024)(128)(2,1)} %param.14) | copy-start | bytes 5380
  46.3 8.6 %copy-start.8 = (s32[5]{0:T(128)S(1)}, s32[5]{0:T(128)}, u32[]{:S(2)}) copy-start(s32[5]{0:T(128)} %param.18) | copy-start | bytes 64
  46.3 8.6 %copy-start.11 = (s32[5]{0:T(128)S(1)}, s32[5]{0:T(128)}, u32[]{:S(2)}) copy-start(s32[5]{0:T(128)} %param.19) | copy-start | bytes 64
  46.3 74.1 %all-to-all-start = ((bf16[32,70,1024]{2,1,0:T(8,128)(2,1)}), bf16[32,70,1024]{2,1,0:T(8,128)(2,1)}, u32[]{:S(2)}, u32[]{:S(2)}) async-start(bf16[32,70,1024]{2,1,0:T(8,128)(2,1)} %maximum_maximum_fusion), calls=%async_computation | async-start | bytes 9437184 | tf_op jit(solution)/shard_map/all_to_all | solution.py:129
  54.7 141.9 %all-gather.6.cloned.1.call-start = ((), (), s32[]{:S(2)}) async-start(), calls=%async_computation.3 | async-start | bytes 5017600 | tf_op jit(solution)/shard_map/all_gather | solution.py:76
  205.3 1.8 slice-start
  214.0 9.8 %copy-start.4 = (bf16[5,272,128]{2,1,0:T(8,128)(2,1)}, bf16[5,272,128]{2,1,0:T(8,128)(2,1)S(1)}, u32[]{:S(2)}) copy-start(bf16[5,272,128]{2,1,0:T(8,128)(2,1)S(1)} %get-tuple-element.17) | copy-start | bytes 1044484
  214.0 19.8 %copy-start.6 = (bf16[5,272,128]{2,1,0:T(8,128)(2,1)}, bf16[5,272,128]{2,1,0:T(8,128)(2,1)S(1)}, u32[]{:S(2)}) copy-start(bf16[5,272,128]{2,1,0:T(8,128)(2,1)S(1)} %get-tuple-element.16) | copy-start | bytes 1044484
  214.1 9.8 %copy-start.3 = (pred[5,448,272]{1,2,0:T(8,128)(4,1)S(1)}, pred[5,448,272]{1,2,0:T(8,128)(4,1)}, u32[]{:S(2)}) copy-start(pred[5,448,272]{1,2,0:T(8,128)(4,1)} %compare_and_fusion) | copy-start | bytes 1827844
  264.7 54.7 %all-to-all-start.1 = ((bf16[32,70,768]{2,1,0:T(8,128)(2,1)}), bf16[32,70,768]{2,1,0:T(8,128)(2,1)}, u32[]{:S(2)}, u32[]{:S(2)}) async-start(bf16[32,70,768]{2,1,0:T(8,128)(2,1)} %concatenate.52), calls=%async_computation.1 | async-start | bytes 7077888 | tf_op jit(solution)/shard_map/all_to_all | solution.py:184
  272.2 134.5 %all-gather.8.cloned.1.call-start = ((), (), s32[]{:S(2)}) async-start(), calls=%async_computation.4 | async-start | bytes 3584000 | tf_op jit(solution)/shard_map/all_gather | solution.py:76
  322.0 2.9 copy-start.2
  346.9 59.8 %copy-start.7 = (bf16[640,160]{0,1:T(8,128)(2,1)S(1)}, bf16[640,160]{0,1:T(8,128)(2,1)}, u32[]{:S(2)}) copy-start(bf16[640,160]{0,1:T(8,128)(2,1)} %param.15) | copy-start | bytes 614404
  406.7 39.3 %copy-start.1 = (bf16[160,896]{1,0:T(8,128)(2,1)S(1)}, bf16[160,896]{1,0:T(8,128)(2,1)}, u32[]{:S(2)}) copy-start(bf16[160,896]{1,0:T(8,128)(2,1)} %param.13) | copy-start | bytes 860164
  409.6 35.8 %copy-start.5 = (bf16[280,160]{0,1:T(8,128)(2,1)S(1)}, bf16[280,160]{0,1:T(8,128)(2,1)}, u32[]{:S(2)}) copy-start(bf16[280,160]{0,1:T(8,128)(2,1)} %param.11) | copy-start | bytes 268804
Sparse Core Ops, SparseCore 0:
  148.9 47.6 all-gather.5
  367.1 39.5 all-gather.7

commit v5 on v4

--- a/solution.py
+++ b/solution.py
@@ -124,8 +124,10 @@
     share_start = lax.axis_index(GX) * row_share
     partial = jnp.dot(gained, qkv_weight, preferred_element_type=jnp.float32)
     proj_width = partial.shape[1]
-    pad = jnp.zeros((token_count, HEAD_DIM - 1), jnp.float32)
-    payload = jnp.concatenate([partial, squares, pad], axis=1).astype(jnp.bfloat16)
+    pad = jnp.zeros((token_count, HEAD_DIM - 1), jnp.bfloat16)
+    payload = jnp.concatenate(
+        [partial.astype(jnp.bfloat16), squares.astype(jnp.bfloat16), pad], axis=1
+    )
     payload = lax.all_to_all(payload, GX, 0, 0, tiled=True).astype(jnp.float32)
     payload = jnp.sum(payload.reshape(gx_size, row_share, -1), axis=0)
     scale_row = lax.rsqrt(payload[:, proj_width : proj_width + 1] / model_width + NORM_EPS)
@@ -179,8 +181,10 @@
     stats = stats.reshape(token_count, -1)
     mixed_width = mixed.shape[1]
     heads_here = mixed_width // HEAD_DIM
-    pad = jnp.zeros((token_count, HEAD_DIM - stats.shape[1]), jnp.float32)
-    both = jnp.concatenate([mixed, stats, pad], axis=1).astype(jnp.bfloat16)
+    pad = jnp.zeros((token_count, HEAD_DIM - stats.shape[1]), jnp.bfloat16)
+    both = jnp.concatenate(
+        [mixed.astype(jnp.bfloat16), stats.astype(jnp.bfloat16), pad], axis=1
+    )
     both = lax.all_to_all(both, GX, 0, 0, tiled=True).astype(jnp.float32)
     both = both.reshape(gx_size, row_share, -1)
     parts = both[:, :, :mixed_width].reshape(gx_size, row_share, heads_here, HEAD_DIM)

time: 454 us -> 454 us (level)
    convert_element_type x0 -> x3, local copies, waits for them, and re-layouts: none -> 10.8 us  [the longest x2 10.3 us: per_device(): mixed.astype(jnp.bfloat16)]
    concatenate x11 -> x9, local copies, waits for them, and re-layouts: 23 us -> 16.3 us  [the longest x1 6.95 us: per_device(): jnp.concatenate([mixed.astype(jnp.bfloat16), stats.astype(jnp.bfloat16),...]
where the time goes in v5:
time: 454 us; the launch traced here: 453 us
  waiting for transfers between devices  198 us (44%)
  blocking collectives  98.1 us (22%)
  local copies, waits for them, and re-layouts  65.9 us (15%)
  other arithmetic  34.3 us (8%)
  matrix products  25.9 us (6%)
  starting transfers between devices  16 us (4%)
  between operations  14.5 us (3%)
    all_gather x2, waiting for transfers between devices, gather_gx(): value = lax.all_gather(value, axis, axis=0, tiled=True)  85.7 us
    all_to_all x1, waiting for transfers between devices, per_device(): payload = lax.all_to_all(payload, GX, 0, 0, tiled=True).astype(jnp.float32)  65.2 us
    all_to_all x1, waiting for transfers between devices, per_device(): both = lax.all_to_all(both, GX, 0, 0, tiled=True).astype(jnp.float32)  47.2 us
    all_gather x4, blocking collectives, gather_gx(): value = lax.all_gather(value, axis, axis=0, tiled=True)  43 us
    all_to_all x1, blocking collectives, per_device(): lax.all_to_all(partial_out.astype(jnp.bfloat16), GY, 0, 0, tiled=True)  34.3 us
    all_gather x1, blocking collectives, per_device(): lax.all_gather(hidden, GY, axis=0, tiled=True).astype(jnp.float32)  20.8 us
    mul x2, local copies, waits for them, and re-layouts, per_device(): mixed = jnp.sum(parts * scale_k[..., None], axis=0)  14.4 us
    convert_element_type x2, local copies, waits for them, and re-layouts, per_device(): mixed.astype(jnp.bfloat16)  10.3 us
  transfers between devices with their start and end apart: 4, of which 4 were waited for; matrix products, arithmetic and copies ran while one was open for 0% of the time, Pallas kernels for 0%

profile of v5, /device:TPU:2, one launch (start us, length us, event | category | flops | bytes accessed | tf_op | source)
XLA Modules:
  0.0 452.9 jit_solution(15350733865433363649)
XLA Ops:
  7.2 20.8 %all-gather = bf16[8,280,160]{1,2,0:T(8,128)(2,1)S(1)} all-gather(bf16[1,280,160]{1,2,0:T(8,128)(2,1)} %bitcast.104), channel_id=1, replica_groups=mesh['y'=4,'zl'=2,'x'=4,'zh'=4,'c'=2] {'zh','c'}, dimensions={0}, use_global_device_ids=true | all-gather | bytes 806400 | tf_op jit(solution)/shard_map/all_gather | solution.py:119
  35.1 5.1 %concatenate.39 = bf16[32,70,896]{2,1,0:T(8,128)(2,1)} reshape(bf16[2240,896]{1,0:T(8,128)(2,1)} %convolution_convert_fusion) | data formatting | bytes 8028160 | tf_op jit(solution)/shard_map/concatenate | solution.py:128
  40.8 5.5 %maximum_maximum_fusion = bf16[32,70,1024]{2,1,0:T(8,128)(2,1)} fusion(bf16[32,70,1]{2,1,0:T(8,128)(2,1)S(1)} %convert_element_type.215, bf16[32,70,896]{2,1,0:T(8,128)(2,1)} %concatenate.39, bf16[1024]{0:T(1024)(128)(2,1)S(1)} %pad.8.clone), kind=kLoop, calls=%fused_computation.14 | loop fusion | flops 13762560 | bytes 8608128 | tf_op jit(solution)/shard_map/concatenate | solution.py:128
  46.3 8.4 %all-to-all-start = ((bf16[32,70,1024]{2,1,0:T(8,128)(2,1)}), bf16[32,70,1024]{2,1,0:T(8,128)(2,1)}, u32[]{:S(2)}, u32[]{:S(2)}) async-start(bf16[32,70,1024]{2,1,0:T(8,128)(2,1)} %maximum_maximum_fusion), calls=%async_computation | async-start | bytes 9437184 | tf_op jit(solution)/shard_map/all_to_all | solution.py:131
  55.2 65.2 %all-to-all-done = bf16[32,70,1024]{2,1,0:T(8,128)(2,1)} async-done(((bf16[32,70,1024]{2,1,0:T(8,128)(2,1)}), bf16[32,70,1024]{2,1,0:T(8,128)(2,1)}, u32[]{:S(2)}, u32[]{:S(2)}) %all-to-all-start) | async-done | bytes 4587552 | tf_op jit(solution)/shard_map/all_to_all | solution.py:131
  125.3 11.9 %all-gather.1 = bf16[4,70,896]{2,1,0:T(8,128)(2,1)S(1)} all-gather(bf16[1,70,896]{2,1,0:T(8,128)(2,1)S(1)} %maximum_bitcast_fusion.1), channel_id=1, replica_groups=mesh['y'=4,'zl'=2,'x'=4,'zh'=4,'c'=2] {'x'}, dimensions={0}, use_global_device_ids=true | all-gather | bytes 627200 | tf_op jit(solution)/shard_map/all_gather | solution.py:76
  137.3 11.4 %all_gather.23 = bf16[560,896]{1,0:T(8,128)(2,1)} all-gather(bf16[280,896]{1,0:T(8,128)(2,1)S(1)} %reshape.471), channel_id=1, replica_groups=mesh['y'=4,'zl'=2,'x'=4,'zh'=4,'c'=2] {'zl'}, dimensions={0}, use_global_device_ids=true | all-gather | bytes 1505280 | tf_op jit(solution)/shard_map/all_gather | solution.py:76
  150.6 46.0 %all-gather.6.cloned.1.call-done = bf16[2240,896]{1,0:T(8,128)(2,1)} async-done(((bf16[560,896]{1,0:T(8,128)(2,1)}), bf16[2240,896]{1,0:T(8,128)(2,1)}) %all-gather.6.cloned.1.call-update) | async-done | bytes 4014096 | tf_op jit(solution)/shard_map/all_gather | solution.py:76
  207.1 5.3 %reshape.446 = bf16[5,448,5,128]{3,2,1,0:T(8,128)(2,1)} reshape(bf16[2240,640]{1,0:T(8,128)(2,1)S(1)} %slice-done) | data formatting | bytes 5734400 | tf_op jit(solution)/shard_map/reshape.13
  214.1 9.7 %fusion = (f32[5,5,448]{2,1,0:T(8,128)S(1)}, f32[5,272,448,5]{2,1,3,0:T(8,128)}) fusion(pred[5,448,272]{1,2,0:T(8,128)(4,1)} %compare_and_fusion, bf16[5,448,5,128]{3,2,1,0:T(8,128)(2,1)} %reshape.446, bf16[5,272,128]{2,1,0:T(8,128)(2,1)S(1)} %get-tuple-element.17), kind=kOutput, calls=%fused_computation.4 | convolution fusion | flops 789006400 | bytes 16055040 | tf_op jit(solution)/shard_map/rikgd,rpkd->rkgip/dot_general | solution.py:152
  223.8 8.5 %fusion.1 = bf16[5,5,448]{2,1,0:T(8,128)(2,1)S(1)} fusion(f32[5,272,448,5]{2,1,3,0:T(8,128)} %get-tuple-element.24, f32[5,5,448]{2,1,0:T(8,128)S(1)} %get-tuple-element.13, pred[5,448,272]{1,2,0:T(8,128)(4,1)S(1)} %copy-done.3), kind=kLoop, calls=%fused_computation.5 | loop fusion | flops 15220800 | bytes 12862080 | tf_op jit(solution)/shard_map/reduce_sum | solution.py:161
  233.8 9.9 %convert_bitcast_fusion = bf16[5,448,1,5,128]{4,1,3,0,2:T(8,128)(2,1)S(1)} fusion(f32[5,272,448,5]{2,1,3,0:T(8,128)} %get-tuple-element.24, f32[5,5,448]{2,1,0:T(8,128)S(1)} %get-tuple-element.13, pred[5,448,272]{1,2,0:T(8,128)(4,1)S(1)} %copy-done.3, bf16[5,272,128]{2,1,0:T(8,128)(2,1)S(1)} %get-tuple-element.16), kind=kOutput, calls=%fused_computation.18 | convolution fusion | flops 796544000 | bytes 16055040 | tf_op jit(solution)/shard_map/rkgip,rpkd->rikgd/dot_general | solution.py:162
  243.7 4.1 copy.90
  247.9 6.2 %convert_element_type.205 = bf16[32,70,640]{2,1,0:T(8,128)(2,1)S(1)} reshape(bf16[5,448,1,5,128]{4,3,1,0,2:T(8,128)(2,1)} %copy.90) | data formatting | bytes 5734400 | tf_op jit(solution)/shard_map/convert_element_type | solution.py:186
  257.8 6.9 %concatenate.48 = bf16[32,70,768]{2,1,0:T(8,128)(2,1)} concatenate(bf16[32,70,640]{2,1,0:T(8,128)(2,1)S(1)} %convert_element_type.205, bf16[32,70,5]{2,1,0:T(8,128)(2,1)} %copy.94, bf16[32,70,5]{2,1,0:T(8,128)(2,1)} %copy.95, bf16[32,70,5]{2,1,0:T(8,128)(2,1)} %copy.96, bf16[32,70,113]{2,1,0:T(8,128)(2,1)} %broadcast_in_dim.118), dimensions={2} | concatenate | bytes 6881280 | tf_op jit(solution)/shard_map/concatenate | solution.py:185
  264.7 7.5 %all-to-all-start.1 = ((bf16[32,70,768]{2,1,0:T(8,128)(2,1)}), bf16[32,70,768]{2,1,0:T(8,128)(2,1)}, u32[]{:S(2)}, u32[]{:S(2)}) async-start(bf16[32,70,768]{2,1,0:T(8,128)(2,1)} %concatenate.48), calls=%async_computation.1 | async-start | bytes 7077888 | tf_op jit(solution)/shard_map/all_to_all | solution.py:188
  272.3 47.2 %all-to-all-done.1 = bf16[32,70,768]{2,1,0:T(8,128)(2,1)} async-done(((bf16[32,70,768]{2,1,0:T(8,128)(2,1)}), bf16[32,70,768]{2,1,0:T(8,128)(2,1)}, u32[]{:S(2)}, u32[]{:S(2)}) %all-to-all-start.1) | async-done | bytes 3440672 | tf_op jit(solution)/shard_map/all_to_all | solution.py:188
  324.9 5.4 %mul.196 = f32[32,70,5,128]{3,2,0,1:T(8,128)} broadcast(f32[32,70,5]{2,0,1:T(8,128)S(1)} %copy.97), dimensions={0,1,2} | broadcast | bytes 5779200 | tf_op jit(solution)/shard_map/mul | solution.py:199
  330.3 9.0 %mul.197 = f32[32,70,640]{2,0,1:T(8,128)} reshape(f32[32,70,5,128]{3,2,0,1:T(8,128)} %mul.196) | data formatting | bytes 11468800 | tf_op jit(solution)/shard_map/mul | solution.py:199
  339.3 7.6 %fusion.7 = f32[70,640]{1,0:T(8,128)S(1)} fusion(f32[32,70,768]{2,1,0:T(8,128)} %copy-done.2, f32[32,70,640]{2,0,1:T(8,128)} %mul.197), kind=kLoop, calls=%fused_computation.12 | loop fusion | flops 2822400 | bytes 11648000 | tf_op jit(solution)/shard_map/reduce_sum | solution.py:199
  347.2 11.3 %all-gather.2 = bf16[4,70,640]{2,1,0:T(8,128)(2,1)S(1)} all-gather(bf16[1,70,640]{2,1,0:T(8,128)(2,1)S(1)} %fusion.18), channel_id=1, replica_groups=mesh['y'=4,'zl'=2,'x'=4,'zh'=4,'c'=2] {'x'}, dimensions={0}, use_global_device_ids=true | all-gather | bytes 448000 | tf_op jit(solution)/shard_map/all_gather | solution.py:76
  358.6 8.4 %all_gather.26 = bf16[560,640]{1,0:T(8,128)(2,1)} all-gather(bf16[280,640]{1,0:T(8,128)(2,1)S(1)} %reshape.473), channel_id=1, replica_groups=mesh['y'=4,'zl'=2,'x'=4,'zh'=4,'c'=2] {'zl'}, dimensions={0}, use_global_device_ids=true | all-gather | bytes 1075200 | tf_op jit(solution)/shard_map/all_gather | solution.py:76
  367.0 39.7 %all-gather.8.cloned.1.call-done = bf16[2240,640]{1,0:T(8,128)(2,1)} async-done(((bf16[560,640]{1,0:T(8,128)(2,1)}), bf16[2240,640]{1,0:T(8,128)(2,1)}) %all-gather.8.cloned.1.call-update) | async-done | bytes 2867216 | tf_op jit(solution)/shard_map/all_gather | solution.py:76
  410.9 34.3 %all_to_all.21 = bf16[8,280,160]{1,2,0:T(8,128)(2,1)S(1)} all-to-all(bf16[8,280,160]{1,2,0:T(8,128)(2,1)S(1)} %copy.99), channel_id=1, replica_groups=mesh['y'=4,'zl'=2,'x'=4,'zh'=4,'c'=2] {'zh','c'}, dimensions={0} | all-to-all | bytes 1433600 | tf_op jit(solution)/shard_map/all_to_all | solution.py:209
  (100 shorter events, 42.9 us)
Async XLA Ops:
  7.2 24.5 %copy-start = (bf16[160,896]{1,0:T(8,128)(2,1)S(1)}, bf16[160,896]{1,0:T(8,128)(2,1)}, u32[]{:S(2)}) copy-start(bf16[160,896]{1,0:T(8,128)(2,1)} %param.13) | copy-start | bytes 860164
  7.2 24.5 %copy-start.9 = (f32[160]{0:T(256)S(1)}, f32[160]{0:T(256)}, u32[]{:S(2)}) copy-start(f32[160]{0:T(256)} %param.12) | copy-start | bytes 1924
  46.3 8.5 %copy-start.10 = (bf16[896]{0:T(1024)(128)(2,1)S(1)}, bf16[896]{0:T(1024)(128)(2,1)}, u32[]{:S(2)}) copy-start(bf16[896]{0:T(1024)(128)(2,1)} %param.14) | copy-start | bytes 5380
  46.3 8.6 %copy-start.8 = (s32[5]{0:T(128)S(1)}, s32[5]{0:T(128)}, u32[]{:S(2)}) copy-start(s32[5]{0:T(128)} %param.18) | copy-start | bytes 64
  46.3 8.6 %copy-start.11 = (s32[5]{0:T(128)S(1)}, s32[5]{0:T(128)}, u32[]{:S(2)}) copy-start(s32[5]{0:T(128)} %param.19) | copy-start | bytes 64
  46.3 74.1 %all-to-all-start = ((bf16[32,70,1024]{2,1,0:T(8,128)(2,1)}), bf16[32,70,1024]{2,1,0:T(8,128)(2,1)}, u32[]{:S(2)}, u32[]{:S(2)}) async-start(bf16[32,70,1024]{2,1,0:T(8,128)(2,1)} %maximum_maximum_fusion), calls=%async_computation | async-start | bytes 9437184 | tf_op jit(solution)/shard_map/all_to_all | solution.py:131
  54.7 141.9 %all-gather.6.cloned.1.call-start = ((), (), s32[]{:S(2)}) async-start(), calls=%async_computation.3 | async-start | bytes 5017600 | tf_op jit(solution)/shard_map/all_gather | solution.py:76
  205.3 1.8 slice-start
  214.0 9.8 %copy-start.4 = (bf16[5,272,128]{2,1,0:T(8,128)(2,1)}, bf16[5,272,128]{2,1,0:T(8,128)(2,1)S(1)}, u32[]{:S(2)}) copy-start(bf16[5,272,128]{2,1,0:T(8,128)(2,1)S(1)} %get-tuple-element.17) | copy-start | bytes 1044484
  214.0 19.8 %copy-start.6 = (bf16[5,272,128]{2,1,0:T(8,128)(2,1)}, bf16[5,272,128]{2,1,0:T(8,128)(2,1)S(1)}, u32[]{:S(2)}) copy-start(bf16[5,272,128]{2,1,0:T(8,128)(2,1)S(1)} %get-tuple-element.16) | copy-start | bytes 1044484
  214.1 9.8 %copy-start.3 = (pred[5,448,272]{1,2,0:T(8,128)(4,1)S(1)}, pred[5,448,272]{1,2,0:T(8,128)(4,1)}, u32[]{:S(2)}) copy-start(pred[5,448,272]{1,2,0:T(8,128)(4,1)} %compare_and_fusion) | copy-start | bytes 1827844
  264.7 54.7 %all-to-all-start.1 = ((bf16[32,70,768]{2,1,0:T(8,128)(2,1)}), bf16[32,70,768]{2,1,0:T(8,128)(2,1)}, u32[]{:S(2)}, u32[]{:S(2)}) async-start(bf16[32,70,768]{2,1,0:T(8,128)(2,1)} %concatenate.48), calls=%async_computation.1 | async-start | bytes 7077888 | tf_op jit(solution)/shard_map/all_to_all | solution.py:188
  272.2 134.5 %all-gather.8.cloned.1.call-start = ((), (), s32[]{:S(2)}) async-start(), calls=%async_computation.4 | async-start | bytes 3584000 | tf_op jit(solution)/shard_map/all_gather | solution.py:76
  322.0 2.9 copy-start.2
  346.9 59.8 %copy-start.7 = (bf16[640,160]{0,1:T(8,128)(2,1)S(1)}, bf16[640,160]{0,1:T(8,128)(2,1)}, u32[]{:S(2)}) copy-start(bf16[640,160]{0,1:T(8,128)(2,1)} %param.15) | copy-start | bytes 614404
  406.7 39.3 %copy-start.1 = (bf16[160,896]{1,0:T(8,128)(2,1)S(1)}, bf16[160,896]{1,0:T(8,128)(2,1)}, u32[]{:S(2)}) copy-start(bf16[160,896]{1,0:T(8,128)(2,1)} %param.13) | copy-start | bytes 860164
  409.6 35.8 %copy-start.5 = (bf16[280,160]{0,1:T(8,128)(2,1)S(1)}, bf16[280,160]{0,1:T(8,128)(2,1)}, u32[]{:S(2)}) copy-start(bf16[280,160]{0,1:T(8,128)(2,1)} %param.11) | copy-start | bytes 268804
Sparse Core Ops, SparseCore 0:
  148.9 47.6 all-gather.5
  367.1 39.5 all-gather.7

commit v6 on v4

--- a/solution.py
+++ b/solution.py
@@ -181,20 +181,19 @@
     heads_here = mixed_width // HEAD_DIM
     pad = jnp.zeros((token_count, HEAD_DIM - stats.shape[1]), jnp.float32)
     both = jnp.concatenate([mixed, stats, pad], axis=1).astype(jnp.bfloat16)
-    both = lax.all_to_all(both, GX, 0, 0, tiled=True).astype(jnp.float32)
+    both = lax.all_to_all(both, GX, 0, 0, tiled=True)
     both = both.reshape(gx_size, row_share, -1)
-    parts = both[:, :, :mixed_width].reshape(gx_size, row_share, heads_here, HEAD_DIM)
-    part_top = (
-        both[:, :, mixed_width : mixed_width + heads_here]
-        + both[:, :, mixed_width + heads_here : mixed_width + 2 * heads_here]
-    )
-    part_denom = both[:, :, mixed_width + 2 * heads_here : mixed_width + 3 * heads_here]
+    part_stats = both[:, :, mixed_width : mixed_width + 3 * heads_here].astype(jnp.float32)
+    part_top = part_stats[:, :, :heads_here] + part_stats[:, :, heads_here : 2 * heads_here]
+    part_denom = part_stats[:, :, 2 * heads_here :]
     top_all = jnp.max(part_top, axis=0)
     scale_k = jnp.exp(part_top - top_all[None])
     denom = jnp.sum(part_denom * scale_k, axis=0)
-    mixed = jnp.sum(parts * scale_k[..., None], axis=0)
+    weight_k = scale_k / denom[None]
+    parts = both[:, :, :mixed_width].reshape(gx_size, row_share, heads_here, HEAD_DIM)
+    mixed = jnp.sum(parts.astype(jnp.float32) * weight_k[..., None], axis=0)
     unused_pos, is_live = token_positions(cached_len, fresh_len, share_start, row_share)
-    ratio = mixed / denom[:, :, None]
+    ratio = mixed
     attended = jnp.where(is_live[:, None], ratio.reshape(row_share, -1), 0.0).astype(jnp.bfloat16)
     partial_out = jnp.dot(
         gather_gx(attended),

time: 454 us -> 451 us (level)
  no operation moved by 1% of the time
where the time goes in v6:
time: 451 us; the launch traced here: 449 us
  waiting for transfers between devices  198 us (44%)
  blocking collectives  98.1 us (22%)
  local copies, waits for them, and re-layouts  64.2 us (14%)
  other arithmetic  32.4 us (7%)
  matrix products  25.9 us (6%)
  starting transfers between devices  16 us (4%)
  between operations  14.5 us (3%)
    all_gather x2, waiting for transfers between devices, gather_gx(): value = lax.all_gather(value, axis, axis=0, tiled=True)  85.7 us
    all_to_all x1, waiting for transfers between devices, per_device(): payload = lax.all_to_all(payload, GX, 0, 0, tiled=True).astype(jnp.float32)  65.3 us
    all_to_all x1, waiting for transfers between devices, per_device(): both = lax.all_to_all(both, GX, 0, 0, tiled=True)  47.2 us
    all_gather x4, blocking collectives, gather_gx(): value = lax.all_gather(value, axis, axis=0, tiled=True)  43 us
    all_to_all x1, blocking collectives, per_device(): lax.all_to_all(partial_out.astype(jnp.bfloat16), GY, 0, 0, tiled=True)  34.3 us
    all_gather x1, blocking collectives, per_device(): lax.all_gather(hidden, GY, axis=0, tiled=True).astype(jnp.float32)  20.8 us
    concatenate x8, local copies, waits for them, and re-layouts, per_device(): both = jnp.concatenate([mixed, stats, pad], axis=1).astype(jnp.bfloat16)  17.3 us
    mul x2, local copies, waits for them, and re-layouts, per_device(): mixed = jnp.sum(parts.astype(jnp.float32) * weight_k[..., None], axis=0)  14.4 us
  transfers between devices with their start and end apart: 4, of which 4 were waited for; matrix products, arithmetic and copies ran while one was open for 0% of the time, Pallas kernels for 0%

profile of v6, /device:TPU:2, one launch (start us, length us, event | category | flops | bytes accessed | tf_op | source)
XLA Modules:
  0.0 449.2 jit_solution(6982341711671658384)
XLA Ops:
  7.2 20.8 %all-gather = bf16[8,280,160]{1,2,0:T(8,128)(2,1)S(1)} all-gather(bf16[1,280,160]{1,2,0:T(8,128)(2,1)} %bitcast.99), channel_id=1, replica_groups=mesh['y'=4,'zl'=2,'x'=4,'zh'=4,'c'=2] {'zh','c'}, dimensions={0}, use_global_device_ids=true | all-gather | bytes 806400 | tf_op jit(solution)/shard_map/all_gather | solution.py:119
  35.0 5.1 %concatenate.41 = bf16[32,70,896]{2,1,0:T(8,128)(2,1)} reshape(bf16[2240,896]{1,0:T(8,128)(2,1)} %convolution_convert_fusion) | data formatting | bytes 8028160 | tf_op jit(solution)/shard_map/concatenate | solution.py:128
  40.8 5.5 %maximum_maximum_fusion = bf16[32,70,1024]{2,1,0:T(8,128)(2,1)} fusion(bf16[32,70,1]{2,1,0:T(8,128)(2,1)S(1)} %concatenate.53, bf16[32,70,896]{2,1,0:T(8,128)(2,1)} %concatenate.41, bf16[1024]{0:T(1024)(128)(2,1)S(1)} %pad.8.clone), kind=kLoop, calls=%fused_computation.14 | loop fusion | flops 13762560 | bytes 8608128 | tf_op jit(solution)/shard_map/concatenate | solution.py:128
  46.3 8.4 %all-to-all-start = ((bf16[32,70,1024]{2,1,0:T(8,128)(2,1)}), bf16[32,70,1024]{2,1,0:T(8,128)(2,1)}, u32[]{:S(2)}, u32[]{:S(2)}) async-start(bf16[32,70,1024]{2,1,0:T(8,128)(2,1)} %maximum_maximum_fusion), calls=%async_computation | async-start | bytes 9437184 | tf_op jit(solution)/shard_map/all_to_all | solution.py:129
  55.2 65.3 %all-to-all-done = bf16[32,70,1024]{2,1,0:T(8,128)(2,1)} async-done(((bf16[32,70,1024]{2,1,0:T(8,128)(2,1)}), bf16[32,70,1024]{2,1,0:T(8,128)(2,1)}, u32[]{:S(2)}, u32[]{:S(2)}) %all-to-all-start) | async-done | bytes 4587552 | tf_op jit(solution)/shard_map/all_to_all | solution.py:129
  125.3 11.9 %all-gather.1 = bf16[4,70,896]{2,1,0:T(8,128)(2,1)S(1)} all-gather(bf16[1,70,896]{2,1,0:T(8,128)(2,1)S(1)} %maximum_bitcast_fusion.1), channel_id=1, replica_groups=mesh['y'=4,'zl'=2,'x'=4,'zh'=4,'c'=2] {'x'}, dimensions={0}, use_global_device_ids=true | all-gather | bytes 627200 | tf_op jit(solution)/shard_map/all_gather | solution.py:76
  137.3 11.4 %all_gather.23 = bf16[560,896]{1,0:T(8,128)(2,1)} all-gather(bf16[280,896]{1,0:T(8,128)(2,1)S(1)} %reshape.459), channel_id=1, replica_groups=mesh['y'=4,'zl'=2,'x'=4,'zh'=4,'c'=2] {'zl'}, dimensions={0}, use_global_device_ids=true | all-gather | bytes 1505280 | tf_op jit(solution)/shard_map/all_gather | solution.py:76
  150.6 46.0 %all-gather.6.cloned.1.call-done = bf16[2240,896]{1,0:T(8,128)(2,1)} async-done(((bf16[560,896]{1,0:T(8,128)(2,1)}), bf16[2240,896]{1,0:T(8,128)(2,1)}) %all-gather.6.cloned.1.call-update) | async-done | bytes 4014096 | tf_op jit(solution)/shard_map/all_gather | solution.py:76
  207.1 5.3 %reshape.434 = bf16[5,448,5,128]{3,2,1,0:T(8,128)(2,1)} reshape(bf16[2240,640]{1,0:T(8,128)(2,1)S(1)} %slice-done) | data formatting | bytes 5734400 | tf_op jit(solution)/shard_map/reshape.13
  214.0 9.7 %fusion = (f32[5,5,448]{2,1,0:T(8,128)S(1)}, f32[5,272,448,5]{2,1,3,0:T(8,128)}) fusion(pred[5,448,272]{1,2,0:T(8,128)(4,1)} %compare_and_fusion, bf16[5,448,5,128]{3,2,1,0:T(8,128)(2,1)} %reshape.434, bf16[5,272,128]{2,1,0:T(8,128)(2,1)S(1)} %get-tuple-element.15), kind=kOutput, calls=%fused_computation.4 | convolution fusion | flops 789006400 | bytes 16055040 | tf_op jit(solution)/shard_map/rikgd,rpkd->rkgip/dot_general | solution.py:150
  223.8 8.5 %fusion.1 = bf16[5,5,448]{2,1,0:T(8,128)(2,1)S(1)} fusion(f32[5,272,448,5]{2,1,3,0:T(8,128)} %get-tuple-element.22, f32[5,5,448]{2,1,0:T(8,128)S(1)} %get-tuple-element.11, pred[5,448,272]{1,2,0:T(8,128)(4,1)S(1)} %copy-done.2), kind=kLoop, calls=%fused_computation.5 | loop fusion | flops 15220800 | bytes 12862080 | tf_op jit(solution)/shard_map/reduce_sum | solution.py:159
  233.8 9.9 %convert_bitcast_fusion = bf16[5,448,1,5,128]{4,1,3,0,2:T(8,128)(2,1)S(1)} fusion(f32[5,272,448,5]{2,1,3,0:T(8,128)} %get-tuple-element.22, f32[5,5,448]{2,1,0:T(8,128)S(1)} %get-tuple-element.11, pred[5,448,272]{1,2,0:T(8,128)(4,1)S(1)} %copy-done.2, bf16[5,272,128]{2,1,0:T(8,128)(2,1)S(1)} %get-tuple-element.14), kind=kOutput, calls=%fused_computation.18 | convolution fusion | flops 796544000 | bytes 16055040 | tf_op jit(solution)/shard_map/rkgip,rpkd->rikgd/dot_general | solution.py:160
  243.7 4.1 copy.90
  247.8 6.2 %concatenate.48 = bf16[32,70,640]{2,1,0:T(8,128)(2,1)S(1)} reshape(bf16[5,448,1,5,128]{4,3,1,0,2:T(8,128)(2,1)} %copy.90) | data formatting | bytes 5734400 | tf_op jit(solution)/shard_map/concatenate | solution.py:183
  257.7 6.9 %concatenate.52 = bf16[32,70,768]{2,1,0:T(8,128)(2,1)} concatenate(bf16[32,70,640]{2,1,0:T(8,128)(2,1)S(1)} %concatenate.48, bf16[32,70,5]{2,1,0:T(8,128)(2,1)} %copy.94, bf16[32,70,5]{2,1,0:T(8,128)(2,1)} %copy.95, bf16[32,70,5]{2,1,0:T(8,128)(2,1)} %copy.96, bf16[32,70,113]{2,1,0:T(8,128)(2,1)} %broadcast_in_dim.118), dimensions={2} | concatenate | bytes 6881280 | tf_op jit(solution)/shard_map/concatenate | solution.py:183
  264.7 7.5 %all-to-all-start.1 = ((bf16[32,70,768]{2,1,0:T(8,128)(2,1)}), bf16[32,70,768]{2,1,0:T(8,128)(2,1)}, u32[]{:S(2)}, u32[]{:S(2)}) async-start(bf16[32,70,768]{2,1,0:T(8,128)(2,1)} %concatenate.52), calls=%async_computation.1 | async-start | bytes 7077888 | tf_op jit(solution)/shard_map/all_to_all | solution.py:184
  272.2 47.2 %all-to-all-done.1 = bf16[32,70,768]{2,1,0:T(8,128)(2,1)} async-done(((bf16[32,70,768]{2,1,0:T(8,128)(2,1)}), bf16[32,70,768]{2,1,0:T(8,128)(2,1)}, u32[]{:S(2)}, u32[]{:S(2)}) %all-to-all-start.1) | async-done | bytes 3440672 | tf_op jit(solution)/shard_map/all_to_all | solution.py:184
  322.3 5.5 %mul.197 = f32[32,70,5,128]{3,2,0,1:T(8,128)} broadcast(f32[32,70,5]{2,0,1:T(8,128)S(1)} %copy.97), dimensions={0,1,2} | broadcast | bytes 5779200 | tf_op jit(solution)/shard_map/mul | solution.py:194
  327.7 9.0 %mul.198 = f32[32,70,640]{2,0,1:T(8,128)} reshape(f32[32,70,5,128]{3,2,0,1:T(8,128)} %mul.197) | data formatting | bytes 11468800 | tf_op jit(solution)/shard_map/mul | solution.py:194
  336.7 6.7 %fusion.7 = bf16[70,640]{1,0:T(8,128)(2,1)S(1)} fusion(f32[32,70,640]{2,0,1:T(8,128)} %mul.198, bf16[32,70,768]{2,1,0:T(8,128)(2,1)} %all-to-all-done.1), kind=kLoop, calls=%fused_computation.12 | loop fusion | flops 4256000 | bytes 8691200 | tf_op jit(solution)/shard_map/reduce_sum | solution.py:194
  343.5 11.3 %all-gather.2 = bf16[4,70,640]{2,1,0:T(8,128)(2,1)S(1)} all-gather(bf16[1,70,640]{2,1,0:T(8,128)(2,1)S(1)} %fusion.18), channel_id=1, replica_groups=mesh['y'=4,'zl'=2,'x'=4,'zh'=4,'c'=2] {'x'}, dimensions={0}, use_global_device_ids=true | all-gather | bytes 448000 | tf_op jit(solution)/shard_map/all_gather | solution.py:76
  354.9 8.4 %all_gather.26 = bf16[560,640]{1,0:T(8,128)(2,1)} all-gather(bf16[280,640]{1,0:T(8,128)(2,1)S(1)} %reshape.461), channel_id=1, replica_groups=mesh['y'=4,'zl'=2,'x'=4,'zh'=4,'c'=2] {'zl'}, dimensions={0}, use_global_device_ids=true | all-gather | bytes 1075200 | tf_op jit(solution)/shard_map/all_gather | solution.py:76
  363.3 39.7 %all-gather.8.cloned.1.call-done = bf16[2240,640]{1,0:T(8,128)(2,1)} async-done(((bf16[560,640]{1,0:T(8,128)(2,1)}), bf16[2240,640]{1,0:T(8,128)(2,1)}) %all-gather.8.cloned.1.call-update) | async-done | bytes 2867216 | tf_op jit(solution)/shard_map/all_gather | solution.py:76
  407.2 34.3 %all_to_all.21 = bf16[8,280,160]{1,2,0:T(8,128)(2,1)S(1)} all-to-all(bf16[8,280,160]{1,2,0:T(8,128)(2,1)S(1)} %copy.99), channel_id=1, replica_groups=mesh['y'=4,'zl'=2,'x'=4,'zh'=4,'c'=2] {'zh','c'}, dimensions={0} | all-to-all | bytes 1433600 | tf_op jit(solution)/shard_map/all_to_all | solution.py:204
  (96 shorter events, 40.0 us)
Async XLA Ops:
  7.2 24.5 %copy-start = (bf16[160,896]{1,0:T(8,128)(2,1)S(1)}, bf16[160,896]{1,0:T(8,128)(2,1)}, u32[]{:S(2)}) copy-start(bf16[160,896]{1,0:T(8,128)(2,1)} %param.13) | copy-start | bytes 860164
  28.0 3.7 copy-start.8
  46.3 8.5 %copy-start.9 = (bf16[896]{0:T(1024)(128)(2,1)S(1)}, bf16[896]{0:T(1024)(128)(2,1)}, u32[]{:S(2)}) copy-start(bf16[896]{0:T(1024)(128)(2,1)} %param.14) | copy-start | bytes 5380
  46.3 8.6 %copy-start.7 = (s32[5]{0:T(128)S(1)}, s32[5]{0:T(128)}, u32[]{:S(2)}) copy-start(s32[5]{0:T(128)} %param.18) | copy-start | bytes 64
  46.3 8.6 %copy-start.10 = (s32[5]{0:T(128)S(1)}, s32[5]{0:T(128)}, u32[]{:S(2)}) copy-start(s32[5]{0:T(128)} %param.19) | copy-start | bytes 64
  46.3 74.2 %all-to-all-start = ((bf16[32,70,1024]{2,1,0:T(8,128)(2,1)}), bf16[32,70,1024]{2,1,0:T(8,128)(2,1)}, u32[]{:S(2)}, u32[]{:S(2)}) async-start(bf16[32,70,1024]{2,1,0:T(8,128)(2,1)} %maximum_maximum_fusion), calls=%async_computation | async-start | bytes 9437184 | tf_op jit(solution)/shard_map/all_to_all | solution.py:129
  54.7 141.9 %all-gather.6.cloned.1.call-start = ((), (), s32[]{:S(2)}) async-start(), calls=%async_computation.3 | async-start | bytes 5017600 | tf_op jit(solution)/shard_map/all_gather | solution.py:76
  205.3 1.8 slice-start
  214.0 9.8 %copy-start.3 = (bf16[5,272,128]{2,1,0:T(8,128)(2,1)}, bf16[5,272,128]{2,1,0:T(8,128)(2,1)S(1)}, u32[]{:S(2)}) copy-start(bf16[5,272,128]{2,1,0:T(8,128)(2,1)S(1)} %get-tuple-element.15) | copy-start | bytes 1044484
  214.0 19.8 %copy-start.5 = (bf16[5,272,128]{2,1,0:T(8,128)(2,1)}, bf16[5,272,128]{2,1,0:T(8,128)(2,1)S(1)}, u32[]{:S(2)}) copy-start(bf16[5,272,128]{2,1,0:T(8,128)(2,1)S(1)} %get-tuple-element.14) | copy-start | bytes 1044484
  214.0 9.8 %copy-start.2 = (pred[5,448,272]{1,2,0:T(8,128)(4,1)S(1)}, pred[5,448,272]{1,2,0:T(8,128)(4,1)}, u32[]{:S(2)}) copy-start(pred[5,448,272]{1,2,0:T(8,128)(4,1)} %compare_and_fusion) | copy-start | bytes 1827844
  264.7 54.8 %all-to-all-start.1 = ((bf16[32,70,768]{2,1,0:T(8,128)(2,1)}), bf16[32,70,768]{2,1,0:T(8,128)(2,1)}, u32[]{:S(2)}, u32[]{:S(2)}) async-start(bf16[32,70,768]{2,1,0:T(8,128)(2,1)} %concatenate.52), calls=%async_computation.1 | async-start | bytes 7077888 | tf_op jit(solution)/shard_map/all_to_all | solution.py:184
  272.2 130.9 %all-gather.8.cloned.1.call-start = ((), (), s32[]{:S(2)}) async-start(), calls=%async_computation.4 | async-start | bytes 3584000 | tf_op jit(solution)/shard_map/all_gather | solution.py:76
  336.7 66.3 %copy-start.6 = (bf16[640,160]{0,1:T(8,128)(2,1)S(1)}, bf16[640,160]{0,1:T(8,128)(2,1)}, u32[]{:S(2)}) copy-start(bf16[640,160]{0,1:T(8,128)(2,1)} %param.15) | copy-start | bytes 614404
  403.0 39.3 %copy-start.1 = (bf16[160,896]{1,0:T(8,128)(2,1)S(1)}, bf16[160,896]{1,0:T(8,128)(2,1)}, u32[]{:S(2)}) copy-start(bf16[160,896]{1,0:T(8,128)(2,1)} %param.13) | copy-start | bytes 860164
  405.9 35.8 %copy-start.4 = (bf16[280,160]{0,1:T(8,128)(2,1)S(1)}, bf16[280,160]{0,1:T(8,128)(2,1)}, u32[]{:S(2)}) copy-start(bf16[280,160]{0,1:T(8,128)(2,1)} %param.11) | copy-start | bytes 268804
Sparse Core Ops, SparseCore 0:
  148.9 47.6 all-gather.5
  363.5 39.5 all-gather.7

commit v7 on v6

--- a/solution.py
+++ b/solution.py
@@ -72,9 +72,9 @@
 
 
 def gather_gx(value):
-    for axis in GX[::-1]:
-        value = lax.all_gather(value, axis, axis=0, tiled=True)
-    return value
+    copies = lax.psum(1, GX)
+    tiled = jnp.tile(value, (copies,) + (1,) * (value.ndim - 1))
+    return lax.all_to_all(tiled, GX, 0, 0, tiled=True)
 
 
 def psum_gx(value):

time: 451 us -> 439 us (0.973); the launches traced: 449 us -> 431 us
  waiting for transfers between devices: 198 us -> 166 us
  starting transfers between devices: 16 us -> 33.6 us
  local copies, waits for them, and re-layouts: 64.2 us -> 79 us
  between operations: 14.5 us -> 1.51 us
    all_gather x2 -> x0, waiting for transfers between devices: 85.7 us -> none  [gather_gx(): value = lax.all_gather(value, axis, axis=0, tiled=True)]
    all_to_all x0 -> x1, waiting for transfers between devices: none -> 53.4 us  [gather_gx(): return lax.all_to_all(tiled, GX, 0, 0, tiled=True)]
    all_to_all x0 -> x1, blocking collectives: none -> 43.8 us  [gather_gx(): return lax.all_to_all(tiled, GX, 0, 0, tiled=True)]
    all_gather x4 -> x0, blocking collectives: 43 us -> none  [gather_gx(): value = lax.all_gather(value, axis, axis=0, tiled=True)]
    all_to_all x0 -> x1, starting transfers between devices: none -> 18.4 us  [gather_gx(): return lax.all_to_all(tiled, GX, 0, 0, tiled=True)]
    all_to_all x0 -> x2, local copies, waits for them, and re-layouts: none -> 7.95 us  [gather_gx(): return lax.all_to_all(tiled, GX, 0, 0, tiled=True)]
    another operation x1 -> x3, local copies, waits for them, and re-layouts: 5.26 us -> 10 us
  transfers between devices with their start and end apart: 4 -> 3, of which waited for: 4 -> 3; matrix products, arithmetic and copies ran while one was open for 0% -> 0% of each run, Pallas kernels for 0% -> 0%
where the time goes in v7:
time: 439 us; the launch traced here: 431 us
  waiting for transfers between devices  166 us (38%)
  blocking collectives  96.7 us (22%)
  local copies, waits for them, and re-layouts  79 us (18%)
  starting transfers between devices  33.6 us (8%)
  other arithmetic  30.3 us (7%)
  matrix products  24.7 us (6%)
    all_to_all x1, waiting for transfers between devices, per_device(): payload = lax.all_to_all(payload, GX, 0, 0, tiled=True).astype(jnp.float32)  65.3 us
    all_to_all x1, waiting for transfers between devices, gather_gx(): return lax.all_to_all(tiled, GX, 0, 0, tiled=True)  53.4 us
    all_to_all x1, waiting for transfers between devices, per_device(): both = lax.all_to_all(both, GX, 0, 0, tiled=True)  46.8 us
    all_to_all x1, blocking collectives, gather_gx(): return lax.all_to_all(tiled, GX, 0, 0, tiled=True)  43.8 us
    all_to_all x1, blocking collectives, per_device(): lax.all_to_all(partial_out.astype(jnp.bfloat16), GY, 0, 0, tiled=True)  32 us
    all_gather x1, blocking collectives, per_device(): lax.all_gather(hidden, GY, axis=0, tiled=True).astype(jnp.float32)  20.8 us
    all_to_all x1, starting transfers between devices, gather_gx(): return lax.all_to_all(tiled, GX, 0, 0, tiled=True)  18.4 us
    concatenate x8, local copies, waits for them, and re-layouts, per_device(): both = jnp.concatenate([mixed, stats, pad], axis=1).astype(jnp.bfloat16)  17.3 us
  transfers between devices with their start and end apart: 3, of which 3 were waited for; matrix products, arithmetic and copies ran while one was open for 0% of the time, Pallas kernels for 0%

profile of v7, /device:TPU:2, one launch (start us, length us, event | category | flops | bytes accessed | tf_op | source)
XLA Modules:
  0.0 431.3 jit_solution(1444909132222585485)
XLA Ops:
  0.6 20.8 %all-gather = bf16[8,280,160]{1,2,0:T(8,128)(2,1)S(1)} all-gather(bf16[1,280,160]{1,2,0:T(8,128)(2,1)} %bitcast.95), channel_id=1, replica_groups=mesh['y'=4,'zl'=2,'x'=4,'zh'=4,'c'=2] {'zh','c'}, dimensions={0}, use_global_device_ids=true | all-gather | bytes 806400 | tf_op jit(solution)/shard_map/all_gather | solution.py:119
  28.5 5.1 %concatenate.41 = bf16[32,70,896]{2,1,0:T(8,128)(2,1)} reshape(bf16[2240,896]{1,0:T(8,128)(2,1)} %convolution_convert_fusion) | data formatting | bytes 8028160 | tf_op jit(solution)/shard_map/concatenate | solution.py:128
  34.2 5.5 %maximum_maximum_fusion = bf16[32,70,1024]{2,1,0:T(8,128)(2,1)} fusion(bf16[32,70,1]{2,1,0:T(8,128)(2,1)S(1)} %concatenate.53, bf16[32,70,896]{2,1,0:T(8,128)(2,1)} %concatenate.41, bf16[1024]{0:T(1024)(128)(2,1)S(1)} %pad.8.clone), kind=kLoop, calls=%fused_computation.14 | loop fusion | flops 13762560 | bytes 8608128 | tf_op jit(solution)/shard_map/concatenate | solution.py:128
  39.7 8.4 %all-to-all-start = ((bf16[32,70,1024]{2,1,0:T(8,128)(2,1)}), bf16[32,70,1024]{2,1,0:T(8,128)(2,1)}, u32[]{:S(2)}, u32[]{:S(2)}) async-start(bf16[32,70,1024]{2,1,0:T(8,128)(2,1)} %maximum_maximum_fusion), calls=%async_computation | async-start | bytes 9437184 | tf_op jit(solution)/shard_map/all_to_all | solution.py:129
  48.6 65.3 %all-to-all-done = bf16[32,70,1024]{2,1,0:T(8,128)(2,1)} async-done(((bf16[32,70,1024]{2,1,0:T(8,128)(2,1)}), bf16[32,70,1024]{2,1,0:T(8,128)(2,1)}, u32[]{:S(2)}, u32[]{:S(2)}) %all-to-all-start) | async-done | bytes 4587552 | tf_op jit(solution)/shard_map/all_to_all | solution.py:129
  113.9 3.4 convert_reduce_fusion
  121.0 18.4 %all-to-all-start.1 = ((bf16[32,70,896]{2,1,0:T(8,128)(2,1)}), bf16[32,70,896]{2,1,0:T(8,128)(2,1)}, u32[]{:S(2)}, u32[]{:S(2)}) async-start(bf16[32,70,896]{2,1,0:T(8,128)(2,1)} %tile.4), calls=%async_computation.1 | async-start | bytes 8257536 | tf_op jit(solution)/shard_map/all_to_all | solution.py:77
  140.3 53.4 %all-to-all-done.1 = bf16[32,70,896]{2,1,0:T(8,128)(2,1)} async-done(((bf16[32,70,896]{2,1,0:T(8,128)(2,1)}), bf16[32,70,896]{2,1,0:T(8,128)(2,1)}, u32[]{:S(2)}, u32[]{:S(2)}) %all-to-all-start.1) | async-done | bytes 4014112 | tf_op jit(solution)/shard_map/all_to_all | solution.py:77
  193.7 5.0 %all_to_all.28 = bf16[2240,896]{1,0:T(8,128)(2,1)} reshape(bf16[32,70,896]{2,1,0:T(8,128)(2,1)} %all-to-all-done.1) | data formatting | bytes 8028160 | tf_op jit(solution)/shard_map/all_to_all | solution.py:77
  200.0 3.6 slice.82
  210.3 7.6 %reshape.462 = bf16[5,448,5,128]{3,2,1,0:T(8,128)(2,1)} reshape(bf16[2240,640]{1,0:T(8,128)(2,1)} %slice.82) | data formatting | bytes 5734400 | tf_op jit(solution)/shard_map/reshape.14
  218.5 9.5 %fusion = (f32[5,5,448]{2,1,0:T(8,128)S(1)}, f32[5,272,448,5]{2,1,3,0:T(8,128)}) fusion(pred[5,448,272]{1,2,0:T(8,128)(4,1)S(1)} %compare_and_fusion, bf16[5,448,5,128]{3,2,1,0:T(8,128)(2,1)} %reshape.462, bf16[5,272,128]{2,1,0:T(8,128)(2,1)S(1)} %get-tuple-element.15), kind=kOutput, calls=%fused_computation.4 | convolution fusion | flops 789006400 | bytes 16055040 | tf_op jit(solution)/shard_map/rikgd,rpkd->rkgip/dot_general | solution.py:150
  228.1 8.5 %fusion.1 = bf16[5,5,448]{2,1,0:T(8,128)(2,1)S(1)} fusion(f32[5,272,448,5]{2,1,3,0:T(8,128)} %get-tuple-element.22, f32[5,5,448]{2,1,0:T(8,128)S(1)} %get-tuple-element.11, pred[5,448,272]{1,2,0:T(8,128)(4,1)S(1)} %compare_and_fusion), kind=kLoop, calls=%fused_computation.5 | loop fusion | flops 15220800 | bytes 12862080 | tf_op jit(solution)/shard_map/reduce_sum | solution.py:159
  238.0 9.9 %convert_bitcast_fusion = bf16[5,448,1,5,128]{4,1,3,0,2:T(8,128)(2,1)S(1)} fusion(f32[5,272,448,5]{2,1,3,0:T(8,128)} %get-tuple-element.22, f32[5,5,448]{2,1,0:T(8,128)S(1)} %get-tuple-element.11, pred[5,448,272]{1,2,0:T(8,128)(4,1)S(1)} %compare_and_fusion, bf16[5,272,128]{2,1,0:T(8,128)(2,1)S(1)} %get-tuple-element.14), kind=kOutput, calls=%fused_computation.18 | convolution fusion | flops 796544000 | bytes 16055040 | tf_op jit(solution)/shard_map/rkgip,rpkd->rikgd/dot_general | solution.py:160
  248.0 4.1 copy.104
  252.1 6.2 %concatenate.48 = bf16[32,70,640]{2,1,0:T(8,128)(2,1)S(1)} reshape(bf16[5,448,1,5,128]{4,3,1,0,2:T(8,128)(2,1)} %copy.104) | data formatting | bytes 5734400 | tf_op jit(solution)/shard_map/concatenate | solution.py:183
  262.0 6.9 %concatenate.52 = bf16[32,70,768]{2,1,0:T(8,128)(2,1)} concatenate(bf16[32,70,640]{2,1,0:T(8,128)(2,1)S(1)} %concatenate.48, bf16[32,70,5]{2,1,0:T(8,128)(2,1)} %copy.108, bf16[32,70,5]{2,1,0:T(8,128)(2,1)} %copy.109, bf16[32,70,5]{2,1,0:T(8,128)(2,1)} %copy.110, bf16[32,70,113]{2,1,0:T(8,128)(2,1)} %broadcast_in_dim.118), dimensions={2} | concatenate | bytes 6881280 | tf_op jit(solution)/shard_map/concatenate | solution.py:183
  269.0 6.7 %all-to-all-start.2 = ((bf16[32,70,768]{2,1,0:T(8,128)(2,1)}), bf16[32,70,768]{2,1,0:T(8,128)(2,1)}, u32[]{:S(2)}, u32[]{:S(2)}) async-start(bf16[32,70,768]{2,1,0:T(8,128)(2,1)} %concatenate.52), calls=%async_computation.2 | async-start | bytes 7077888 | tf_op jit(solution)/shard_map/all_to_all | solution.py:184
  275.7 46.8 %all-to-all-done.2 = bf16[32,70,768]{2,1,0:T(8,128)(2,1)} async-done(((bf16[32,70,768]{2,1,0:T(8,128)(2,1)}), bf16[32,70,768]{2,1,0:T(8,128)(2,1)}, u32[]{:S(2)}, u32[]{:S(2)}) %all-to-all-start.2) | async-done | bytes 3440672 | tf_op jit(solution)/shard_map/all_to_all | solution.py:184
  325.3 5.5 %mul.197 = f32[32,70,5,128]{3,2,0,1:T(8,128)} broadcast(f32[32,70,5]{2,0,1:T(8,128)S(1)} %copy.111), dimensions={0,1,2} | broadcast | bytes 5779200 | tf_op jit(solution)/shard_map/mul | solution.py:194
  330.8 9.0 %mul.198 = f32[32,70,640]{2,0,1:T(8,128)} reshape(f32[32,70,5,128]{3,2,0,1:T(8,128)} %mul.197) | data formatting | bytes 11468800 | tf_op jit(solution)/shard_map/mul | solution.py:194
  339.8 6.7 %fusion.7 = bf16[70,640]{1,0:T(8,128)(2,1)S(1)} fusion(f32[32,70,640]{2,0,1:T(8,128)} %mul.198, bf16[32,70,768]{2,1,0:T(8,128)(2,1)} %all-to-all-done.2), kind=kLoop, calls=%fused_computation.12 | loop fusion | flops 4256000 | bytes 8691200 | tf_op jit(solution)/shard_map/reduce_sum | solution.py:194
  346.8 43.8 %all_to_all.39 = bf16[32,70,640]{2,1,0:T(8,128)(2,1)} all-to-all(bf16[32,70,640]{2,1,0:T(8,128)(2,1)S(1)} %tile.5), channel_id=1, replica_groups=mesh['y'=4,'zl'=2,'x'=4,'zh'=4,'c'=2] {'y','zl','x'}, dimensions={0} | all-to-all | bytes 5734400 | tf_op jit(solution)/shard_map/all_to_all | solution.py:77
  398.0 32.0 %all_to_all.40 = bf16[8,280,160]{1,2,0:T(8,128)(2,1)S(1)} all-to-all(bf16[8,280,160]{1,2,0:T(8,128)(2,1)S(1)} %copy.113), channel_id=1, replica_groups=mesh['y'=4,'zl'=2,'x'=4,'zh'=4,'c'=2] {'zh','c'}, dimensions={0} | all-to-all | bytes 1433600 | tf_op jit(solution)/shard_map/all_to_all | solution.py:204
  (92 shorter events, 37.3 us)
Async XLA Ops:
  0.6 24.5 %copy-start = (bf16[160,896]{1,0:T(8,128)(2,1)S(1)}, bf16[160,896]{1,0:T(8,128)(2,1)}, u32[]{:S(2)}) copy-start(bf16[160,896]{1,0:T(8,128)(2,1)} %param.13) | copy-start | bytes 860164
  21.4 3.7 copy-start.9
  39.7 8.4 %copy-start.10 = (bf16[896]{0:T(1024)(128)(2,1)S(1)}, bf16[896]{0:T(1024)(128)(2,1)}, u32[]{:S(2)}) copy-start(bf16[896]{0:T(1024)(128)(2,1)} %param.14) | copy-start | bytes 5380
  39.7 8.5 %copy-start.8 = (s32[5]{0:T(128)S(1)}, s32[5]{0:T(128)}, u32[]{:S(2)}) copy-start(s32[5]{0:T(128)} %param.18) | copy-start | bytes 64
  39.7 8.5 %copy-start.11 = (s32[5]{0:T(128)S(1)}, s32[5]{0:T(128)}, u32[]{:S(2)}) copy-start(s32[5]{0:T(128)} %param.19) | copy-start | bytes 64
  39.7 74.1 %all-to-all-start = ((bf16[32,70,1024]{2,1,0:T(8,128)(2,1)}), bf16[32,70,1024]{2,1,0:T(8,128)(2,1)}, u32[]{:S(2)}, u32[]{:S(2)}) async-start(bf16[32,70,1024]{2,1,0:T(8,128)(2,1)} %maximum_maximum_fusion), calls=%async_computation | async-start | bytes 9437184 | tf_op jit(solution)/shard_map/all_to_all | solution.py:129
  121.0 72.7 %all-to-all-start.1 = ((bf16[32,70,896]{2,1,0:T(8,128)(2,1)}), bf16[32,70,896]{2,1,0:T(8,128)(2,1)}, u32[]{:S(2)}, u32[]{:S(2)}) async-start(bf16[32,70,896]{2,1,0:T(8,128)(2,1)} %tile.4), calls=%async_computation.1 | async-start | bytes 8257536 | tf_op jit(solution)/shard_map/all_to_all | solution.py:77
  210.3 7.6 %copy-start.4 = (bf16[5,272,128]{2,1,0:T(8,128)(2,1)S(1)}, bf16[5,272,128]{2,1,0:T(8,128)(2,1)}, u32[]{:S(2)}) copy-start(bf16[5,272,128]{2,1,0:T(8,128)(2,1)} %param.17) | copy-start | bytes 1044484
  210.3 7.6 %copy-start.5 = (bf16[5,272,128]{2,1,0:T(8,128)(2,1)S(1)}, bf16[5,272,128]{2,1,0:T(8,128)(2,1)}, u32[]{:S(2)}) copy-start(bf16[5,272,128]{2,1,0:T(8,128)(2,1)} %param.16) | copy-start | bytes 1044484
  218.5 9.6 %copy-start.2 = (bf16[5,272,128]{2,1,0:T(8,128)(2,1)}, bf16[5,272,128]{2,1,0:T(8,128)(2,1)S(1)}, u32[]{:S(2)}) copy-start(bf16[5,272,128]{2,1,0:T(8,128)(2,1)S(1)} %get-tuple-element.15) | copy-start | bytes 1044484
  218.5 19.6 %copy-start.6 = (bf16[5,272,128]{2,1,0:T(8,128)(2,1)}, bf16[5,272,128]{2,1,0:T(8,128)(2,1)S(1)}, u32[]{:S(2)}) copy-start(bf16[5,272,128]{2,1,0:T(8,128)(2,1)S(1)} %get-tuple-element.14) | copy-start | bytes 1044484
  269.0 53.5 %all-to-all-start.2 = ((bf16[32,70,768]{2,1,0:T(8,128)(2,1)}), bf16[32,70,768]{2,1,0:T(8,128)(2,1)}, u32[]{:S(2)}, u32[]{:S(2)}) async-start(bf16[32,70,768]{2,1,0:T(8,128)(2,1)} %concatenate.52), calls=%async_computation.2 | async-start | bytes 7077888 | tf_op jit(solution)/shard_map/all_to_all | solution.py:184
  390.6 2.9 copy-start.7
  393.6 37.3 %copy-start.1 = (bf16[160,896]{1,0:T(8,128)(2,1)S(1)}, bf16[160,896]{1,0:T(8,128)(2,1)}, u32[]{:S(2)}) copy-start(bf16[160,896]{1,0:T(8,128)(2,1)} %param.13) | copy-start | bytes 860164
  395.5 34.7 %copy-start.3 = (bf16[280,160]{0,1:T(8,128)(2,1)S(1)}, bf16[280,160]{0,1:T(8,128)(2,1)}, u32[]{:S(2)}) copy-start(bf16[280,160]{0,1:T(8,128)(2,1)} %param.11) | copy-start | bytes 268804

commit v8 on v7

--- a/solution.py
+++ b/solution.py
@@ -71,6 +71,12 @@
 GY = ("zh", "c")
 
 
+def gather_gx_chain(value):
+    for axis in GX[::-1]:
+        value = lax.all_gather(value, axis, axis=0, tiled=True)
+    return value
+
+
 def gather_gx(value):
     copies = lax.psum(1, GX)
     tiled = jnp.tile(value, (copies,) + (1,) * (value.ndim - 1))
@@ -92,7 +98,7 @@
 def share_rows(share_sum, cached_len, fresh_len, first_row):
     queries, new_keys, new_values = finish_rows(share_sum, cached_len, fresh_len, first_row)
     widths = (queries.shape[1], new_keys.shape[1])
-    joined = gather_gx(jnp.concatenate([queries, new_keys, new_values], axis=1))
+    joined = gather_gx_chain(jnp.concatenate([queries, new_keys, new_values], axis=1))
     return (
         joined[:, : widths[0]],
         joined[:, widths[0] : widths[0] + widths[1]],

time: 439 us -> 437 us (level); the launches traced: 431 us -> 435 us
  blocking collectives: 96.7 us -> 121 us
  starting transfers between devices: 33.6 us -> 15.9 us
  between operations: 1.51 us -> 14.5 us
  local copies, waits for them, and re-layouts: 79 us -> 68.5 us
  waiting for transfers between devices: 166 us -> 158 us
    all_to_all x1 -> x0, waiting for transfers between devices: 53.4 us -> none  [gather_gx(): return lax.all_to_all(tiled, GX, 0, 0, tiled=True)]
    all_gather x0 -> x1, waiting for transfers between devices: none -> 46 us  [gather_gx_chain(): value = lax.all_gather(value, axis, axis=0, tiled=True)]
    all_gather x0 -> x2, blocking collectives: none -> 23.3 us  [gather_gx_chain(): value = lax.all_gather(value, axis, axis=0, tiled=True)]
    all_to_all x1 -> x0, starting transfers between devices: 18.4 us -> none  [gather_gx(): return lax.all_to_all(tiled, GX, 0, 0, tiled=True)]
    all_to_all x2 -> x1, local copies, waits for them, and re-layouts: 7.95 us -> 2.93 us  [gather_gx(): return lax.all_to_all(tiled, GX, 0, 0, tiled=True)]
where the time goes in v8:
time: 437 us; the launch traced here: 435 us
  waiting for transfers between devices  158 us (36%)
  blocking collectives  121 us (28%)
  local copies, waits for them, and re-layouts  68.5 us (16%)
  other arithmetic  32.4 us (7%)
  matrix products  24.9 us (6%)
  starting transfers between devices  15.9 us (4%)
  between operations  14.5 us (3%)
    all_to_all x1, waiting for transfers between devices, per_device(): payload = lax.all_to_all(payload, GX, 0, 0, tiled=True).astype(jnp.float32)  65.3 us
    all_to_all x1, waiting for transfers between devices, per_device(): both = lax.all_to_all(both, GX, 0, 0, tiled=True)  47.2 us
    all_gather x1, waiting for transfers between devices, gather_gx_chain(): value = lax.all_gather(value, axis, axis=0, tiled=True)  46 us
    all_to_all x1, blocking collectives, gather_gx(): return lax.all_to_all(tiled, GX, 0, 0, tiled=True)  43 us
    all_to_all x1, blocking collectives, per_device(): lax.all_to_all(partial_out.astype(jnp.bfloat16), GY, 0, 0, tiled=True)  33.4 us
    all_gather x2, blocking collectives, gather_gx_chain(): value = lax.all_gather(value, axis, axis=0, tiled=True)  23.3 us
    all_gather x1, blocking collectives, per_device(): lax.all_gather(hidden, GY, axis=0, tiled=True).astype(jnp.float32)  20.8 us
    concatenate x8, local copies, waits for them, and re-layouts, per_device(): both = jnp.concatenate([mixed, stats, pad], axis=1).astype(jnp.bfloat16)  17.3 us
  transfers between devices with their start and end apart: 3, of which 3 were waited for; matrix products, arithmetic and copies ran while one was open for 0% of the time, Pallas kernels for 0%

profile of v8, /device:TPU:2, one launch (start us, length us, event | category | flops | bytes accessed | tf_op | source)
XLA Modules:
  0.0 435.2 jit_solution(11458317250035112213)
XLA Ops:
  7.2 20.8 %all-gather = bf16[8,280,160]{1,2,0:T(8,128)(2,1)S(1)} all-gather(bf16[1,280,160]{1,2,0:T(8,128)(2,1)} %bitcast.97), channel_id=1, replica_groups=mesh['y'=4,'zl'=2,'x'=4,'zh'=4,'c'=2] {'zh','c'}, dimensions={0}, use_global_device_ids=true | all-gather | bytes 806400 | tf_op jit(solution)/shard_map/all_gather | solution.py:125
  35.0 5.1 %concatenate.41 = bf16[32,70,896]{2,1,0:T(8,128)(2,1)} reshape(bf16[2240,896]{1,0:T(8,128)(2,1)} %convolution_convert_fusion) | data formatting | bytes 8028160 | tf_op jit(solution)/shard_map/concatenate | solution.py:134
  40.8 5.5 %maximum_maximum_fusion = bf16[32,70,1024]{2,1,0:T(8,128)(2,1)} fusion(bf16[32,70,1]{2,1,0:T(8,128)(2,1)S(1)} %concatenate.53, bf16[32,70,896]{2,1,0:T(8,128)(2,1)} %concatenate.41, bf16[1024]{0:T(1024)(128)(2,1)S(1)} %pad.8.clone), kind=kLoop, calls=%fused_computation.14 | loop fusion | flops 13762560 | bytes 8608128 | tf_op jit(solution)/shard_map/concatenate | solution.py:134
  46.3 8.4 %all-to-all-start = ((bf16[32,70,1024]{2,1,0:T(8,128)(2,1)}), bf16[32,70,1024]{2,1,0:T(8,128)(2,1)}, u32[]{:S(2)}, u32[]{:S(2)}) async-start(bf16[32,70,1024]{2,1,0:T(8,128)(2,1)} %maximum_maximum_fusion), calls=%async_computation | async-start | bytes 9437184 | tf_op jit(solution)/shard_map/all_to_all | solution.py:135
  55.2 65.3 %all-to-all-done = bf16[32,70,1024]{2,1,0:T(8,128)(2,1)} async-done(((bf16[32,70,1024]{2,1,0:T(8,128)(2,1)}), bf16[32,70,1024]{2,1,0:T(8,128)(2,1)}, u32[]{:S(2)}, u32[]{:S(2)}) %all-to-all-start) | async-done | bytes 4587552 | tf_op jit(solution)/shard_map/all_to_all | solution.py:135
  120.5 3.4 convert_reduce_fusion
  125.3 11.9 %all-gather.1 = bf16[4,70,896]{2,1,0:T(8,128)(2,1)S(1)} all-gather(bf16[1,70,896]{2,1,0:T(8,128)(2,1)S(1)} %maximum_bitcast_fusion.1), channel_id=1, replica_groups=mesh['y'=4,'zl'=2,'x'=4,'zh'=4,'c'=2] {'x'}, dimensions={0}, use_global_device_ids=true | all-gather | bytes 627200 | tf_op jit(solution)/shard_map/all_gather | solution.py:76
  137.3 11.4 %all_gather.14 = bf16[560,896]{1,0:T(8,128)(2,1)} all-gather(bf16[280,896]{1,0:T(8,128)(2,1)S(1)} %reshape.480), channel_id=1, replica_groups=mesh['y'=4,'zl'=2,'x'=4,'zh'=4,'c'=2] {'zl'}, dimensions={0}, use_global_device_ids=true | all-gather | bytes 1505280 | tf_op jit(solution)/shard_map/all_gather | solution.py:76
  150.6 46.0 %all-gather.4.cloned.1.call-done = bf16[2240,896]{1,0:T(8,128)(2,1)} async-done(((bf16[560,896]{1,0:T(8,128)(2,1)}), bf16[2240,896]{1,0:T(8,128)(2,1)}) %all-gather.4.cloned.1.call-update) | async-done | bytes 4014096 | tf_op jit(solution)/shard_map/all_gather | solution.py:76
  201.2 4.0 gather_fusion.1
  207.1 5.3 %reshape.455 = bf16[5,448,5,128]{3,2,1,0:T(8,128)(2,1)} reshape(bf16[2240,640]{1,0:T(8,128)(2,1)S(1)} %slice-done) | data formatting | bytes 5734400 | tf_op jit(solution)/shard_map/reshape.13
  214.0 9.7 %fusion = (f32[5,5,448]{2,1,0:T(8,128)S(1)}, f32[5,272,448,5]{2,1,3,0:T(8,128)}) fusion(pred[5,448,272]{1,2,0:T(8,128)(4,1)} %compare_and_fusion, bf16[5,448,5,128]{3,2,1,0:T(8,128)(2,1)} %reshape.455, bf16[5,272,128]{2,1,0:T(8,128)(2,1)S(1)} %get-tuple-element.15), kind=kOutput, calls=%fused_computation.4 | convolution fusion | flops 789006400 | bytes 16055040 | tf_op jit(solution)/shard_map/rikgd,rpkd->rkgip/dot_general | solution.py:156
  223.8 8.5 %fusion.1 = bf16[5,5,448]{2,1,0:T(8,128)(2,1)S(1)} fusion(f32[5,272,448,5]{2,1,3,0:T(8,128)} %get-tuple-element.22, f32[5,5,448]{2,1,0:T(8,128)S(1)} %get-tuple-element.11, pred[5,448,272]{1,2,0:T(8,128)(4,1)S(1)} %copy-done.2), kind=kLoop, calls=%fused_computation.5 | loop fusion | flops 15220800 | bytes 12862080 | tf_op jit(solution)/shard_map/reduce_sum | solution.py:165
  233.8 9.9 %convert_bitcast_fusion = bf16[5,448,1,5,128]{4,1,3,0,2:T(8,128)(2,1)S(1)} fusion(f32[5,272,448,5]{2,1,3,0:T(8,128)} %get-tuple-element.22, f32[5,5,448]{2,1,0:T(8,128)S(1)} %get-tuple-element.11, pred[5,448,272]{1,2,0:T(8,128)(4,1)S(1)} %copy-done.2, bf16[5,272,128]{2,1,0:T(8,128)(2,1)S(1)} %get-tuple-element.14), kind=kOutput, calls=%fused_computation.18 | convolution fusion | flops 796544000 | bytes 16055040 | tf_op jit(solution)/shard_map/rkgip,rpkd->rikgd/dot_general | solution.py:166
  243.7 4.1 copy.90
  247.8 6.2 %concatenate.48 = bf16[32,70,640]{2,1,0:T(8,128)(2,1)S(1)} reshape(bf16[5,448,1,5,128]{4,3,1,0,2:T(8,128)(2,1)} %copy.90) | data formatting | bytes 5734400 | tf_op jit(solution)/shard_map/concatenate | solution.py:189
  257.7 6.9 %concatenate.52 = bf16[32,70,768]{2,1,0:T(8,128)(2,1)} concatenate(bf16[32,70,640]{2,1,0:T(8,128)(2,1)S(1)} %concatenate.48, bf16[32,70,5]{2,1,0:T(8,128)(2,1)} %copy.94, bf16[32,70,5]{2,1,0:T(8,128)(2,1)} %copy.95, bf16[32,70,5]{2,1,0:T(8,128)(2,1)} %copy.96, bf16[32,70,113]{2,1,0:T(8,128)(2,1)} %broadcast_in_dim.118), dimensions={2} | concatenate | bytes 6881280 | tf_op jit(solution)/shard_map/concatenate | solution.py:189
  264.7 7.5 %all-to-all-start.1 = ((bf16[32,70,768]{2,1,0:T(8,128)(2,1)}), bf16[32,70,768]{2,1,0:T(8,128)(2,1)}, u32[]{:S(2)}, u32[]{:S(2)}) async-start(bf16[32,70,768]{2,1,0:T(8,128)(2,1)} %concatenate.52), calls=%async_computation.1 | async-start | bytes 7077888 | tf_op jit(solution)/shard_map/all_to_all | solution.py:190
  272.2 47.2 %all-to-all-done.1 = bf16[32,70,768]{2,1,0:T(8,128)(2,1)} async-done(((bf16[32,70,768]{2,1,0:T(8,128)(2,1)}), bf16[32,70,768]{2,1,0:T(8,128)(2,1)}, u32[]{:S(2)}, u32[]{:S(2)}) %all-to-all-start.1) | async-done | bytes 3440672 | tf_op jit(solution)/shard_map/all_to_all | solution.py:190
  322.3 5.5 %mul.197 = f32[32,70,5,128]{3,2,0,1:T(8,128)} broadcast(f32[32,70,5]{2,0,1:T(8,128)S(1)} %copy.97), dimensions={0,1,2} | broadcast | bytes 5779200 | tf_op jit(solution)/shard_map/mul | solution.py:200
  327.7 9.0 %mul.198 = f32[32,70,640]{2,0,1:T(8,128)} reshape(f32[32,70,5,128]{3,2,0,1:T(8,128)} %mul.197) | data formatting | bytes 11468800 | tf_op jit(solution)/shard_map/mul | solution.py:200
  336.7 6.7 %fusion.7 = bf16[70,640]{1,0:T(8,128)(2,1)S(1)} fusion(f32[32,70,640]{2,0,1:T(8,128)} %mul.198, bf16[32,70,768]{2,1,0:T(8,128)(2,1)} %all-to-all-done.1), kind=kLoop, calls=%fused_computation.12 | loop fusion | flops 4256000 | bytes 8691200 | tf_op jit(solution)/shard_map/reduce_sum | solution.py:200
  343.7 43.0 %all_to_all.30 = bf16[32,70,640]{2,1,0:T(8,128)(2,1)} all-to-all(bf16[32,70,640]{2,1,0:T(8,128)(2,1)S(1)} %tile.2), channel_id=1, replica_groups=mesh['y'=4,'zl'=2,'x'=4,'zh'=4,'c'=2] {'y','zl','x'}, dimensions={0} | all-to-all | bytes 5734400 | tf_op jit(solution)/shard_map/all_to_all | solution.py:83
  394.1 33.4 %all_to_all.31 = bf16[8,280,160]{1,2,0:T(8,128)(2,1)S(1)} all-to-all(bf16[8,280,160]{1,2,0:T(8,128)(2,1)S(1)} %copy.99), channel_id=1, replica_groups=mesh['y'=4,'zl'=2,'x'=4,'zh'=4,'c'=2] {'zh','c'}, dimensions={0} | all-to-all | bytes 1433600 | tf_op jit(solution)/shard_map/all_to_all | solution.py:210
  (93 shorter events, 35.8 us)
Async XLA Ops:
  7.2 24.5 %copy-start = (bf16[160,896]{1,0:T(8,128)(2,1)S(1)}, bf16[160,896]{1,0:T(8,128)(2,1)}, u32[]{:S(2)}) copy-start(bf16[160,896]{1,0:T(8,128)(2,1)} %param.13) | copy-start | bytes 860164
  28.0 3.7 copy-start.8
  46.3 8.5 %copy-start.9 = (bf16[896]{0:T(1024)(128)(2,1)S(1)}, bf16[896]{0:T(1024)(128)(2,1)}, u32[]{:S(2)}) copy-start(bf16[896]{0:T(1024)(128)(2,1)} %param.14) | copy-start | bytes 5380
  46.3 8.6 %copy-start.7 = (s32[5]{0:T(128)S(1)}, s32[5]{0:T(128)}, u32[]{:S(2)}) copy-start(s32[5]{0:T(128)} %param.18) | copy-start | bytes 64
  46.3 8.6 %copy-start.10 = (s32[5]{0:T(128)S(1)}, s32[5]{0:T(128)}, u32[]{:S(2)}) copy-start(s32[5]{0:T(128)} %param.19) | copy-start | bytes 64
  46.3 74.2 %all-to-all-start = ((bf16[32,70,1024]{2,1,0:T(8,128)(2,1)}), bf16[32,70,1024]{2,1,0:T(8,128)(2,1)}, u32[]{:S(2)}, u32[]{:S(2)}) async-start(bf16[32,70,1024]{2,1,0:T(8,128)(2,1)} %maximum_maximum_fusion), calls=%async_computation | async-start | bytes 9437184 | tf_op jit(solution)/shard_map/all_to_all | solution.py:135
  54.7 141.9 %all-gather.4.cloned.1.call-start = ((), (), s32[]{:S(2)}) async-start(), calls=%async_computation.4 | async-start | bytes 5017600 | tf_op jit(solution)/shard_map/all_gather | solution.py:76
  205.3 1.8 slice-start
  214.0 9.8 %copy-start.3 = (bf16[5,272,128]{2,1,0:T(8,128)(2,1)}, bf16[5,272,128]{2,1,0:T(8,128)(2,1)S(1)}, u32[]{:S(2)}) copy-start(bf16[5,272,128]{2,1,0:T(8,128)(2,1)S(1)} %get-tuple-element.15) | copy-start | bytes 1044484
  214.0 19.8 %copy-start.5 = (bf16[5,272,128]{2,1,0:T(8,128)(2,1)}, bf16[5,272,128]{2,1,0:T(8,128)(2,1)S(1)}, u32[]{:S(2)}) copy-start(bf16[5,272,128]{2,1,0:T(8,128)(2,1)S(1)} %get-tuple-element.14) | copy-start | bytes 1044484
  214.0 9.8 %copy-start.2 = (pred[5,448,272]{1,2,0:T(8,128)(4,1)S(1)}, pred[5,448,272]{1,2,0:T(8,128)(4,1)}, u32[]{:S(2)}) copy-start(pred[5,448,272]{1,2,0:T(8,128)(4,1)} %compare_and_fusion) | copy-start | bytes 1827844
  264.7 54.8 %all-to-all-start.1 = ((bf16[32,70,768]{2,1,0:T(8,128)(2,1)}), bf16[32,70,768]{2,1,0:T(8,128)(2,1)}, u32[]{:S(2)}, u32[]{:S(2)}) async-start(bf16[32,70,768]{2,1,0:T(8,128)(2,1)} %concatenate.52), calls=%async_computation.1 | async-start | bytes 7077888 | tf_op jit(solution)/shard_map/all_to_all | solution.py:190
  386.8 2.9 copy-start.6
  389.7 38.7 %copy-start.1 = (bf16[160,896]{1,0:T(8,128)(2,1)S(1)}, bf16[160,896]{1,0:T(8,128)(2,1)}, u32[]{:S(2)}) copy-start(bf16[160,896]{1,0:T(8,128)(2,1)} %param.13) | copy-start | bytes 860164
  391.6 36.1 %copy-start.4 = (bf16[280,160]{0,1:T(8,128)(2,1)S(1)}, bf16[280,160]{0,1:T(8,128)(2,1)}, u32[]{:S(2)}) copy-start(bf16[280,160]{0,1:T(8,128)(2,1)} %param.11) | copy-start | bytes 268804
Sparse Core Ops, SparseCore 0:
  148.9 47.6 all-gather.3

commit v9 on v8

--- a/solution.py
+++ b/solution.py
@@ -72,9 +72,11 @@
 
 
 def gather_gx_chain(value):
-    for axis in GX[::-1]:
+    for axis in GX[:0:-1]:
         value = lax.all_gather(value, axis, axis=0, tiled=True)
-    return value
+    copies = lax.psum(1, GX[0])
+    tiled = jnp.tile(value, (copies,) + (1,) * (value.ndim - 1))
+    return lax.all_to_all(tiled, GX[0], 0, 0, tiled=True)
 
 
 def gather_gx(value):

time: 437 us -> 440 us (level); the launches traced: 435 us -> 432 us
  starting transfers between devices: 15.9 us -> 32.6 us
  between operations: 14.5 us -> 1.52 us
  waiting for transfers between devices: 158 us -> 152 us
  local copies, waits for them, and re-layouts: 68.5 us -> 74.1 us
    all_gather x1 -> x0, waiting for transfers between devices: 46 us -> none  [gather_gx_chain(): value = lax.all_gather(value, axis, axis=0, tiled=True)]
    all_to_all x0 -> x1, waiting for transfers between devices: none -> 42.2 us  [gather_gx_chain(): return lax.all_to_all(tiled, GX[0], 0, 0, tiled=True)]
    all_to_all x0 -> x1, starting transfers between devices: none -> 16 us  [gather_gx_chain(): return lax.all_to_all(tiled, GX[0], 0, 0, tiled=True)]
    another operation x1 -> x2, local copies, waits for them, and re-layouts: 5.26 us -> 9.77 us
where the time goes in v9:
time: 440 us; the launch traced here: 432 us
  waiting for transfers between devices  152 us (35%)
  blocking collectives  118 us (27%)
  local copies, waits for them, and re-layouts  74.1 us (17%)
  starting transfers between devices  32.6 us (7%)
  other arithmetic  30.3 us (7%)
  matrix products  24.7 us (6%)
    all_to_all x1, waiting for transfers between devices, per_device(): payload = lax.all_to_all(payload, GX, 0, 0, tiled=True).astype(jnp.float32)  65.3 us
    all_to_all x1, waiting for transfers between devices, per_device(): both = lax.all_to_all(both, GX, 0, 0, tiled=True)  44.2 us
    all_to_all x1, waiting for transfers between devices, gather_gx_chain(): return lax.all_to_all(tiled, GX[0], 0, 0, tiled=True)  42.2 us
    all_to_all x1, blocking collectives, gather_gx(): return lax.all_to_all(tiled, GX, 0, 0, tiled=True)  41.7 us
    all_to_all x1, blocking collectives, per_device(): lax.all_to_all(partial_out.astype(jnp.bfloat16), GY, 0, 0, tiled=True)  32 us
    all_gather x2, blocking collectives, gather_gx_chain(): value = lax.all_gather(value, axis, axis=0, tiled=True)  23.1 us
    all_gather x1, blocking collectives, per_device(): lax.all_gather(hidden, GY, axis=0, tiled=True).astype(jnp.float32)  20.8 us
    concatenate x8, local copies, waits for them, and re-layouts, per_device(): both = jnp.concatenate([mixed, stats, pad], axis=1).astype(jnp.bfloat16)  17.3 us
  transfers between devices with their start and end apart: 3, of which 3 were waited for; matrix products, arithmetic and copies ran while one was open for 0% of the time, Pallas kernels for 0%

profile of v9, /device:TPU:2, one launch (start us, length us, event | category | flops | bytes accessed | tf_op | source)
XLA Modules:
  0.0 432.4 jit_solution(6210786904337374558)
XLA Ops:
  0.6 20.8 %all-gather = bf16[8,280,160]{1,2,0:T(8,128)(2,1)S(1)} all-gather(bf16[1,280,160]{1,2,0:T(8,128)(2,1)} %bitcast.98), channel_id=1, replica_groups=mesh['y'=4,'zl'=2,'x'=4,'zh'=4,'c'=2] {'zh','c'}, dimensions={0}, use_global_device_ids=true | all-gather | bytes 806400 | tf_op jit(solution)/shard_map/all_gather | solution.py:127
  28.5 5.1 %concatenate.41 = bf16[32,70,896]{2,1,0:T(8,128)(2,1)} reshape(bf16[2240,896]{1,0:T(8,128)(2,1)} %convolution_convert_fusion) | data formatting | bytes 8028160 | tf_op jit(solution)/shard_map/concatenate | solution.py:136
  34.2 5.5 %maximum_maximum_fusion = bf16[32,70,1024]{2,1,0:T(8,128)(2,1)} fusion(bf16[32,70,1]{2,1,0:T(8,128)(2,1)S(1)} %concatenate.53, bf16[32,70,896]{2,1,0:T(8,128)(2,1)} %concatenate.41, bf16[1024]{0:T(1024)(128)(2,1)S(1)} %pad.8.clone), kind=kLoop, calls=%fused_computation.14 | loop fusion | flops 13762560 | bytes 8608128 | tf_op jit(solution)/shard_map/concatenate | solution.py:136
  39.7 8.4 %all-to-all-start = ((bf16[32,70,1024]{2,1,0:T(8,128)(2,1)}), bf16[32,70,1024]{2,1,0:T(8,128)(2,1)}, u32[]{:S(2)}, u32[]{:S(2)}) async-start(bf16[32,70,1024]{2,1,0:T(8,128)(2,1)} %maximum_maximum_fusion), calls=%async_computation | async-start | bytes 9437184 | tf_op jit(solution)/shard_map/all_to_all | solution.py:137
  48.6 65.3 %all-to-all-done = bf16[32,70,1024]{2,1,0:T(8,128)(2,1)} async-done(((bf16[32,70,1024]{2,1,0:T(8,128)(2,1)}), bf16[32,70,1024]{2,1,0:T(8,128)(2,1)}, u32[]{:S(2)}, u32[]{:S(2)}) %all-to-all-start) | async-done | bytes 4587552 | tf_op jit(solution)/shard_map/all_to_all | solution.py:137
  118.7 11.9 %all-gather.1 = bf16[4,70,896]{2,1,0:T(8,128)(2,1)S(1)} all-gather(bf16[1,70,896]{2,1,0:T(8,128)(2,1)S(1)} %maximum_bitcast_fusion.1), channel_id=1, replica_groups=mesh['y'=4,'zl'=2,'x'=4,'zh'=4,'c'=2] {'x'}, dimensions={0}, use_global_device_ids=true | all-gather | bytes 627200 | tf_op jit(solution)/shard_map/all_gather | solution.py:76
  130.8 11.2 %all_gather.11 = bf16[560,896]{1,0:T(8,128)(2,1)S(1)} all-gather(bf16[280,896]{1,0:T(8,128)(2,1)S(1)} %reshape.487), channel_id=1, replica_groups=mesh['y'=4,'zl'=2,'x'=4,'zh'=4,'c'=2] {'zl'}, dimensions={0}, use_global_device_ids=true | all-gather | bytes 1505280 | tf_op jit(solution)/shard_map/all_gather | solution.py:76
  144.1 16.0 %all-to-all-start.1 = ((bf16[4,560,896]{2,1,0:T(8,128)(2,1)}), bf16[4,560,896]{2,1,0:T(8,128)(2,1)}, u32[]{:S(2)}, u32[]{:S(2)}) async-start(bf16[4,560,896]{2,1,0:T(8,128)(2,1)} %tile.4), calls=%async_computation.1 | async-start | bytes 8028160 | tf_op jit(solution)/shard_map/all_to_all | solution.py:79
  161.1 42.2 %all-to-all-done.1 = bf16[4,560,896]{2,1,0:T(8,128)(2,1)} async-done(((bf16[4,560,896]{2,1,0:T(8,128)(2,1)}), bf16[4,560,896]{2,1,0:T(8,128)(2,1)}, u32[]{:S(2)}, u32[]{:S(2)}) %all-to-all-start.1) | async-done | bytes 4014112 | tf_op jit(solution)/shard_map/all_to_all | solution.py:79
  204.6 3.7 slice.82
  214.9 7.6 %reshape.462 = bf16[5,448,5,128]{3,2,1,0:T(8,128)(2,1)} reshape(bf16[2240,640]{1,0:T(8,128)(2,1)} %slice.82) | data formatting | bytes 5734400 | tf_op jit(solution)/shard_map/reshape.14
  223.1 9.5 %fusion = (f32[5,5,448]{2,1,0:T(8,128)S(1)}, f32[5,272,448,5]{2,1,3,0:T(8,128)}) fusion(pred[5,448,272]{1,2,0:T(8,128)(4,1)S(1)} %compare_and_fusion, bf16[5,448,5,128]{3,2,1,0:T(8,128)(2,1)} %reshape.462, bf16[5,272,128]{2,1,0:T(8,128)(2,1)S(1)} %get-tuple-element.15), kind=kOutput, calls=%fused_computation.4 | convolution fusion | flops 789006400 | bytes 16055040 | tf_op jit(solution)/shard_map/rikgd,rpkd->rkgip/dot_general | solution.py:158
  232.7 8.5 %fusion.1 = bf16[5,5,448]{2,1,0:T(8,128)(2,1)S(1)} fusion(f32[5,272,448,5]{2,1,3,0:T(8,128)} %get-tuple-element.22, f32[5,5,448]{2,1,0:T(8,128)S(1)} %get-tuple-element.11, pred[5,448,272]{1,2,0:T(8,128)(4,1)S(1)} %compare_and_fusion), kind=kLoop, calls=%fused_computation.5 | loop fusion | flops 15220800 | bytes 12862080 | tf_op jit(solution)/shard_map/reduce_sum | solution.py:167
  242.6 9.9 %convert_bitcast_fusion = bf16[5,448,1,5,128]{4,1,3,0,2:T(8,128)(2,1)S(1)} fusion(f32[5,272,448,5]{2,1,3,0:T(8,128)} %get-tuple-element.22, f32[5,5,448]{2,1,0:T(8,128)S(1)} %get-tuple-element.11, pred[5,448,272]{1,2,0:T(8,128)(4,1)S(1)} %compare_and_fusion, bf16[5,272,128]{2,1,0:T(8,128)(2,1)S(1)} %get-tuple-element.14), kind=kOutput, calls=%fused_computation.18 | convolution fusion | flops 796544000 | bytes 16055040 | tf_op jit(solution)/shard_map/rkgip,rpkd->rikgd/dot_general | solution.py:168
  252.6 4.1 copy.87
  256.7 6.2 %concatenate.48 = bf16[32,70,640]{2,1,0:T(8,128)(2,1)S(1)} reshape(bf16[5,448,1,5,128]{4,3,1,0,2:T(8,128)(2,1)} %copy.87) | data formatting | bytes 5734400 | tf_op jit(solution)/shard_map/concatenate | solution.py:191
  266.6 6.9 %concatenate.52 = bf16[32,70,768]{2,1,0:T(8,128)(2,1)} concatenate(bf16[32,70,640]{2,1,0:T(8,128)(2,1)S(1)} %concatenate.48, bf16[32,70,5]{2,1,0:T(8,128)(2,1)} %copy.91, bf16[32,70,5]{2,1,0:T(8,128)(2,1)} %copy.92, bf16[32,70,5]{2,1,0:T(8,128)(2,1)} %copy.93, bf16[32,70,113]{2,1,0:T(8,128)(2,1)} %broadcast_in_dim.118), dimensions={2} | concatenate | bytes 6881280 | tf_op jit(solution)/shard_map/concatenate | solution.py:191
  273.6 8.1 %all-to-all-start.2 = ((bf16[32,70,768]{2,1,0:T(8,128)(2,1)}), bf16[32,70,768]{2,1,0:T(8,128)(2,1)}, u32[]{:S(2)}, u32[]{:S(2)}) async-start(bf16[32,70,768]{2,1,0:T(8,128)(2,1)} %concatenate.52), calls=%async_computation.2 | async-start | bytes 7077888 | tf_op jit(solution)/shard_map/all_to_all | solution.py:192
  281.7 44.2 %all-to-all-done.2 = bf16[32,70,768]{2,1,0:T(8,128)(2,1)} async-done(((bf16[32,70,768]{2,1,0:T(8,128)(2,1)}), bf16[32,70,768]{2,1,0:T(8,128)(2,1)}, u32[]{:S(2)}, u32[]{:S(2)}) %all-to-all-start.2) | async-done | bytes 3440672 | tf_op jit(solution)/shard_map/all_to_all | solution.py:192
  328.7 5.5 %mul.197 = f32[32,70,5,128]{3,2,0,1:T(8,128)} broadcast(f32[32,70,5]{2,0,1:T(8,128)S(1)} %copy.94), dimensions={0,1,2} | broadcast | bytes 5779200 | tf_op jit(solution)/shard_map/mul | solution.py:202
  334.2 9.0 %mul.198 = f32[32,70,640]{2,0,1:T(8,128)} reshape(f32[32,70,5,128]{3,2,0,1:T(8,128)} %mul.197) | data formatting | bytes 11468800 | tf_op jit(solution)/shard_map/mul | solution.py:202
  343.1 6.7 %fusion.7 = bf16[70,640]{1,0:T(8,128)(2,1)S(1)} fusion(f32[32,70,640]{2,0,1:T(8,128)} %mul.198, bf16[32,70,768]{2,1,0:T(8,128)(2,1)} %all-to-all-done.2), kind=kLoop, calls=%fused_computation.12 | loop fusion | flops 4256000 | bytes 8691200 | tf_op jit(solution)/shard_map/reduce_sum | solution.py:202
  350.2 41.7 %all_to_all.39 = bf16[32,70,640]{2,1,0:T(8,128)(2,1)} all-to-all(bf16[32,70,640]{2,1,0:T(8,128)(2,1)S(1)} %tile.5), channel_id=1, replica_groups=mesh['y'=4,'zl'=2,'x'=4,'zh'=4,'c'=2] {'y','zl','x'}, dimensions={0} | all-to-all | bytes 5734400 | tf_op jit(solution)/shard_map/all_to_all | solution.py:85
  399.2 32.0 %all_to_all.40 = bf16[8,280,160]{1,2,0:T(8,128)(2,1)S(1)} all-to-all(bf16[8,280,160]{1,2,0:T(8,128)(2,1)S(1)} %copy.96), channel_id=1, replica_groups=mesh['y'=4,'zl'=2,'x'=4,'zh'=4,'c'=2] {'zh','c'}, dimensions={0} | all-to-all | bytes 1433600 | tf_op jit(solution)/shard_map/all_to_all | solution.py:212
  (94 shorter events, 40.8 us)
Async XLA Ops:
  0.6 24.5 %copy-start = (bf16[160,896]{1,0:T(8,128)(2,1)S(1)}, bf16[160,896]{1,0:T(8,128)(2,1)}, u32[]{:S(2)}) copy-start(bf16[160,896]{1,0:T(8,128)(2,1)} %param.13) | copy-start | bytes 860164
  21.4 3.7 copy-start.9
  39.7 8.4 %copy-start.10 = (bf16[896]{0:T(1024)(128)(2,1)S(1)}, bf16[896]{0:T(1024)(128)(2,1)}, u32[]{:S(2)}) copy-start(bf16[896]{0:T(1024)(128)(2,1)} %param.14) | copy-start | bytes 5380
  39.7 8.5 %copy-start.8 = (s32[5]{0:T(128)S(1)}, s32[5]{0:T(128)}, u32[]{:S(2)}) copy-start(s32[5]{0:T(128)} %param.18) | copy-start | bytes 64
  39.7 8.5 %copy-start.11 = (s32[5]{0:T(128)S(1)}, s32[5]{0:T(128)}, u32[]{:S(2)}) copy-start(s32[5]{0:T(128)} %param.19) | copy-start | bytes 64
  39.7 74.1 %all-to-all-start = ((bf16[32,70,1024]{2,1,0:T(8,128)(2,1)}), bf16[32,70,1024]{2,1,0:T(8,128)(2,1)}, u32[]{:S(2)}, u32[]{:S(2)}) async-start(bf16[32,70,1024]{2,1,0:T(8,128)(2,1)} %maximum_maximum_fusion), calls=%async_computation | async-start | bytes 9437184 | tf_op jit(solution)/shard_map/all_to_all | solution.py:137
  144.1 59.2 %all-to-all-start.1 = ((bf16[4,560,896]{2,1,0:T(8,128)(2,1)}), bf16[4,560,896]{2,1,0:T(8,128)(2,1)}, u32[]{:S(2)}, u32[]{:S(2)}) async-start(bf16[4,560,896]{2,1,0:T(8,128)(2,1)} %tile.4), calls=%async_computation.1 | async-start | bytes 8028160 | tf_op jit(solution)/shard_map/all_to_all | solution.py:79
  214.9 7.6 %copy-start.4 = (bf16[5,272,128]{2,1,0:T(8,128)(2,1)S(1)}, bf16[5,272,128]{2,1,0:T(8,128)(2,1)}, u32[]{:S(2)}) copy-start(bf16[5,272,128]{2,1,0:T(8,128)(2,1)} %param.17) | copy-start | bytes 1044484
  214.9 7.6 %copy-start.5 = (bf16[5,272,128]{2,1,0:T(8,128)(2,1)S(1)}, bf16[5,272,128]{2,1,0:T(8,128)(2,1)}, u32[]{:S(2)}) copy-start(bf16[5,272,128]{2,1,0:T(8,128)(2,1)} %param.16) | copy-start | bytes 1044484
  223.1 9.6 %copy-start.2 = (bf16[5,272,128]{2,1,0:T(8,128)(2,1)}, bf16[5,272,128]{2,1,0:T(8,128)(2,1)S(1)}, u32[]{:S(2)}) copy-start(bf16[5,272,128]{2,1,0:T(8,128)(2,1)S(1)} %get-tuple-element.15) | copy-start | bytes 1044484
  223.1 19.6 %copy-start.6 = (bf16[5,272,128]{2,1,0:T(8,128)(2,1)}, bf16[5,272,128]{2,1,0:T(8,128)(2,1)S(1)}, u32[]{:S(2)}) copy-start(bf16[5,272,128]{2,1,0:T(8,128)(2,1)S(1)} %get-tuple-element.14) | copy-start | bytes 1044484
  273.6 52.3 %all-to-all-start.2 = ((bf16[32,70,768]{2,1,0:T(8,128)(2,1)}), bf16[32,70,768]{2,1,0:T(8,128)(2,1)}, u32[]{:S(2)}, u32[]{:S(2)}) async-start(bf16[32,70,768]{2,1,0:T(8,128)(2,1)} %concatenate.52), calls=%async_computation.2 | async-start | bytes 7077888 | tf_op jit(solution)/shard_map/all_to_all | solution.py:192
  391.9 2.9 copy-start.7
  394.8 37.2 %copy-start.1 = (bf16[160,896]{1,0:T(8,128)(2,1)S(1)}, bf16[160,896]{1,0:T(8,128)(2,1)}, u32[]{:S(2)}) copy-start(bf16[160,896]{1,0:T(8,128)(2,1)} %param.13) | copy-start | bytes 860164
  396.7 34.6 %copy-start.3 = (bf16[280,160]{0,1:T(8,128)(2,1)S(1)}, bf16[280,160]{0,1:T(8,128)(2,1)}, u32[]{:S(2)}) copy-start(bf16[280,160]{0,1:T(8,128)(2,1)} %param.11) | copy-start | bytes 268804

commit v10 on v8

--- a/solution.py
+++ b/solution.py
@@ -122,7 +122,9 @@
     gx_size = lax.psum(1, GX)
     model_width = hidden.shape[1] * gx_size
     hidden_f = hidden.astype(jnp.float32)
-    gathered = lax.all_gather(hidden, GY, axis=0, tiled=True).astype(jnp.float32)
+    gy_copies = lax.psum(1, GY)
+    gathered = lax.all_to_all(jnp.tile(hidden, (gy_copies, 1)), GY, 0, 0, tiled=True)
+    gathered = gathered.astype(jnp.float32)
     squares = jnp.sum(gathered * gathered, axis=1, keepdims=True)
     gained = (gathered * norm_gain[None, :]).astype(jnp.bfloat16)
     bias_f = qkv_bias.astype(jnp.float32)[None, :]

time: 437 us -> 443 us (1.014)
  waiting for transfers between devices: 158 us -> 182 us
  blocking collectives: 121 us -> 98.7 us
  starting transfers between devices: 15.9 us -> 24.2 us
    all_to_all x0 -> x1, waiting for transfers between devices: none -> 27.8 us  [per_device(): lax.all_to_all(jnp.tile(hidden, (gy_copies, 1)), GY, 0, 0, tiled=True)]
    all_gather x1 -> x0, blocking collectives: 20.8 us -> none  [per_device(): lax.all_gather(hidden, GY, axis=0, tiled=True).astype(jnp.float32)]
    all_to_all x0 -> x1, starting transfers between devices: none -> 8.47 us  [per_device(): lax.all_to_all(jnp.tile(hidden, (gy_copies, 1)), GY, 0, 0, tiled=True)]
    concatenate x3 -> x2, local copies, waits for them, and re-layouts: 5.71 us -> 0.6 us  [per_device(): jnp.concatenate([partial, squares, pad], axis=1).astype(jnp.bfloat16)]
  transfers between devices with their start and end apart: 3 -> 4, of which waited for: 3 -> 4; matrix products, arithmetic and copies ran while one was open for 0% -> 1% of each run, Pallas kernels for 0% -> 0%
where the time goes in v10:
time: 443 us; the launch traced here: 442 us
  waiting for transfers between devices  182 us (41%)
  blocking collectives  98.7 us (22%)
  local copies, waits for them, and re-layouts  66.9 us (15%)
  other arithmetic  31.9 us (7%)
  starting transfers between devices  24.2 us (5%)
  matrix products  23.1 us (5%)
  between operations  14.5 us (3%)
    all_to_all x1, waiting for transfers between devices, per_device(): payload = lax.all_to_all(payload, GX, 0, 0, tiled=True).astype(jnp.float32)  61.8 us
    all_to_all x1, waiting for transfers between devices, per_device(): both = lax.all_to_all(both, GX, 0, 0, tiled=True)  47.2 us
    all_gather x1, waiting for transfers between devices, gather_gx_chain(): value = lax.all_gather(value, axis, axis=0, tiled=True)  45.4 us
    all_to_all x1, blocking collectives, gather_gx(): return lax.all_to_all(tiled, GX, 0, 0, tiled=True)  43 us
    all_to_all x1, blocking collectives, per_device(): lax.all_to_all(partial_out.astype(jnp.bfloat16), GY, 0, 0, tiled=True)  33.4 us
    all_to_all x1, waiting for transfers between devices, per_device(): lax.all_to_all(jnp.tile(hidden, (gy_copies, 1)), GY, 0, 0, tiled=True)  27.8 us
    all_gather x2, blocking collectives, gather_gx_chain(): value = lax.all_gather(value, axis, axis=0, tiled=True)  22.3 us
    concatenate x8, local copies, waits for them, and re-layouts, per_device(): both = jnp.concatenate([mixed, stats, pad], axis=1).astype(jnp.bfloat16)  17.3 us
  transfers between devices with their start and end apart: 4, of which 4 were waited for; matrix products, arithmetic and copies ran while one was open for 1% of the time, Pallas kernels for 0%

profile of v10, /device:TPU:2, one launch (start us, length us, event | category | flops | bytes accessed | tf_op | source)
XLA Modules:
  0.0 441.5 jit_solution(12867908451235652783)
XLA Ops:
  9.2 8.5 %all-to-all-start = ((bf16[8,280,160]{1,2,0:T(8,128)(2,1)}), bf16[8,280,160]{1,2,0:T(8,128)(2,1)S(1)}, u32[]{:S(2)}, u32[]{:S(2)}) async-start(bf16[8,280,160]{1,2,0:T(8,128)(2,1)} %tile.4), calls=%async_computation | async-start | bytes 1966080 | tf_op jit(solution)/shard_map/all_to_all | solution.py:126
  17.7 27.8 %all-to-all-done = bf16[8,280,160]{1,2,0:T(8,128)(2,1)S(1)} async-done(((bf16[8,280,160]{1,2,0:T(8,128)(2,1)}), bf16[8,280,160]{1,2,0:T(8,128)(2,1)S(1)}, u32[]{:S(2)}, u32[]{:S(2)}) %all-to-all-start) | async-done | bytes 716832 | tf_op jit(solution)/shard_map/all_to_all | solution.py:126
  54.5 3.4 maximum_maximum_fusion
  57.9 8.2 %all-to-all-start.1 = ((bf16[32,70,1024]{2,1,0:T(8,128)(2,1)}), bf16[32,70,1024]{2,1,0:T(8,128)(2,1)}, u32[]{:S(2)}, u32[]{:S(2)}) async-start(bf16[32,70,1024]{2,1,0:T(8,128)(2,1)} %maximum_maximum_fusion), calls=%async_computation.1 | async-start | bytes 9437184 | tf_op jit(solution)/shard_map/all_to_all | solution.py:137
  66.5 61.8 %all-to-all-done.1 = bf16[32,70,1024]{2,1,0:T(8,128)(2,1)} async-done(((bf16[32,70,1024]{2,1,0:T(8,128)(2,1)}), bf16[32,70,1024]{2,1,0:T(8,128)(2,1)}, u32[]{:S(2)}, u32[]{:S(2)}) %all-to-all-start.1) | async-done | bytes 4587552 | tf_op jit(solution)/shard_map/all_to_all | solution.py:137
  128.3 3.4 convert_reduce_fusion
  133.1 11.6 %all-gather = bf16[4,70,896]{2,1,0:T(8,128)(2,1)S(1)} all-gather(bf16[1,70,896]{2,1,0:T(8,128)(2,1)S(1)} %maximum_bitcast_fusion.1), channel_id=1, replica_groups=mesh['y'=4,'zl'=2,'x'=4,'zh'=4,'c'=2] {'x'}, dimensions={0}, use_global_device_ids=true | all-gather | bytes 627200 | tf_op jit(solution)/shard_map/all_gather | solution.py:76
  144.9 10.7 %all_gather.10 = bf16[560,896]{1,0:T(8,128)(2,1)} all-gather(bf16[280,896]{1,0:T(8,128)(2,1)S(1)} %reshape.495), channel_id=1, replica_groups=mesh['y'=4,'zl'=2,'x'=4,'zh'=4,'c'=2] {'zl'}, dimensions={0}, use_global_device_ids=true | all-gather | bytes 1505280 | tf_op jit(solution)/shard_map/all_gather | solution.py:76
  157.4 45.4 %all-gather.3.cloned.1.call-done = bf16[2240,896]{1,0:T(8,128)(2,1)} async-done(((bf16[560,896]{1,0:T(8,128)(2,1)}), bf16[2240,896]{1,0:T(8,128)(2,1)}) %all-gather.3.cloned.1.call-update) | async-done | bytes 4014096 | tf_op jit(solution)/shard_map/all_gather | solution.py:76
  207.5 4.0 gather_fusion.1
  213.4 5.3 %reshape.471 = bf16[5,448,5,128]{3,2,1,0:T(8,128)(2,1)} reshape(bf16[2240,640]{1,0:T(8,128)(2,1)S(1)} %slice-done) | data formatting | bytes 5734400 | tf_op jit(solution)/shard_map/reshape.14
  220.3 9.7 %fusion = (f32[5,5,448]{2,1,0:T(8,128)S(1)}, f32[5,272,448,5]{2,1,3,0:T(8,128)}) fusion(pred[5,448,272]{1,2,0:T(8,128)(4,1)} %compare_and_fusion, bf16[5,448,5,128]{3,2,1,0:T(8,128)(2,1)} %reshape.471, bf16[5,272,128]{2,1,0:T(8,128)(2,1)S(1)} %get-tuple-element.15), kind=kOutput, calls=%fused_computation.4 | convolution fusion | flops 789006400 | bytes 16055040 | tf_op jit(solution)/shard_map/rikgd,rpkd->rkgip/dot_general | solution.py:158
  230.1 8.5 %fusion.1 = bf16[5,5,448]{2,1,0:T(8,128)(2,1)S(1)} fusion(f32[5,272,448,5]{2,1,3,0:T(8,128)} %get-tuple-element.22, f32[5,5,448]{2,1,0:T(8,128)S(1)} %get-tuple-element.11, pred[5,448,272]{1,2,0:T(8,128)(4,1)S(1)} %copy-done.2), kind=kLoop, calls=%fused_computation.5 | loop fusion | flops 15220800 | bytes 12862080 | tf_op jit(solution)/shard_map/reduce_sum | solution.py:167
  240.0 9.9 %convert_bitcast_fusion = bf16[5,448,1,5,128]{4,1,3,0,2:T(8,128)(2,1)S(1)} fusion(f32[5,272,448,5]{2,1,3,0:T(8,128)} %get-tuple-element.22, f32[5,5,448]{2,1,0:T(8,128)S(1)} %get-tuple-element.11, pred[5,448,272]{1,2,0:T(8,128)(4,1)S(1)} %copy-done.2, bf16[5,272,128]{2,1,0:T(8,128)(2,1)S(1)} %get-tuple-element.14), kind=kOutput, calls=%fused_computation.17 | convolution fusion | flops 796544000 | bytes 16055040 | tf_op jit(solution)/shard_map/rkgip,rpkd->rikgd/dot_general | solution.py:168
  250.0 4.1 copy.94
  254.1 6.2 %concatenate.45 = bf16[32,70,640]{2,1,0:T(8,128)(2,1)S(1)} reshape(bf16[5,448,1,5,128]{4,3,1,0,2:T(8,128)(2,1)} %copy.94) | data formatting | bytes 5734400 | tf_op jit(solution)/shard_map/concatenate | solution.py:191
  264.0 6.9 %concatenate.49 = bf16[32,70,768]{2,1,0:T(8,128)(2,1)} concatenate(bf16[32,70,640]{2,1,0:T(8,128)(2,1)S(1)} %concatenate.45, bf16[32,70,5]{2,1,0:T(8,128)(2,1)} %copy.98, bf16[32,70,5]{2,1,0:T(8,128)(2,1)} %copy.99, bf16[32,70,5]{2,1,0:T(8,128)(2,1)} %copy.100, bf16[32,70,113]{2,1,0:T(8,128)(2,1)} %broadcast_in_dim.118), dimensions={2} | concatenate | bytes 6881280 | tf_op jit(solution)/shard_map/concatenate | solution.py:191
  270.9 7.5 %all-to-all-start.2 = ((bf16[32,70,768]{2,1,0:T(8,128)(2,1)}), bf16[32,70,768]{2,1,0:T(8,128)(2,1)}, u32[]{:S(2)}, u32[]{:S(2)}) async-start(bf16[32,70,768]{2,1,0:T(8,128)(2,1)} %concatenate.49), calls=%async_computation.2 | async-start | bytes 7077888 | tf_op jit(solution)/shard_map/all_to_all | solution.py:192
  278.5 47.2 %all-to-all-done.2 = bf16[32,70,768]{2,1,0:T(8,128)(2,1)} async-done(((bf16[32,70,768]{2,1,0:T(8,128)(2,1)}), bf16[32,70,768]{2,1,0:T(8,128)(2,1)}, u32[]{:S(2)}, u32[]{:S(2)}) %all-to-all-start.2) | async-done | bytes 3440672 | tf_op jit(solution)/shard_map/all_to_all | solution.py:192
  328.5 5.5 %mul.199 = f32[32,70,5,128]{3,2,0,1:T(8,128)} broadcast(f32[32,70,5]{2,0,1:T(8,128)S(1)} %copy.101), dimensions={0,1,2} | broadcast | bytes 5779200 | tf_op jit(solution)/shard_map/mul | solution.py:202
  334.0 9.0 %mul.200 = f32[32,70,640]{2,0,1:T(8,128)} reshape(f32[32,70,5,128]{3,2,0,1:T(8,128)} %mul.199) | data formatting | bytes 11468800 | tf_op jit(solution)/shard_map/mul | solution.py:202
  343.0 6.7 %fusion.7 = bf16[70,640]{1,0:T(8,128)(2,1)S(1)} fusion(f32[32,70,640]{2,0,1:T(8,128)} %mul.200, bf16[32,70,768]{2,1,0:T(8,128)(2,1)} %all-to-all-done.2), kind=kLoop, calls=%fused_computation.12 | loop fusion | flops 4256000 | bytes 8691200 | tf_op jit(solution)/shard_map/reduce_sum | solution.py:202
  350.0 43.0 %all_to_all.36 = bf16[32,70,640]{2,1,0:T(8,128)(2,1)} all-to-all(bf16[32,70,640]{2,1,0:T(8,128)(2,1)S(1)} %tile.5), channel_id=1, replica_groups=mesh['y'=4,'zl'=2,'x'=4,'zh'=4,'c'=2] {'y','zl','x'}, dimensions={0} | all-to-all | bytes 5734400 | tf_op jit(solution)/shard_map/all_to_all | solution.py:83
  400.4 33.4 %all_to_all.37 = bf16[8,280,160]{1,2,0:T(8,128)(2,1)S(1)} all-to-all(bf16[8,280,160]{1,2,0:T(8,128)(2,1)S(1)} %copy.103), channel_id=1, replica_groups=mesh['y'=4,'zl'=2,'x'=4,'zh'=4,'c'=2] {'zh','c'}, dimensions={0} | all-to-all | bytes 1433600 | tf_op jit(solution)/shard_map/all_to_all | solution.py:212
  (97 shorter events, 39.2 us)
Async XLA Ops:
  7.2 45.7 %copy-start = (bf16[160,896]{1,0:T(8,128)(2,1)S(1)}, bf16[160,896]{1,0:T(8,128)(2,1)}, u32[]{:S(2)}) copy-start(bf16[160,896]{1,0:T(8,128)(2,1)} %param.13) | copy-start | bytes 860164
  9.2 36.3 %all-to-all-start = ((bf16[8,280,160]{1,2,0:T(8,128)(2,1)}), bf16[8,280,160]{1,2,0:T(8,128)(2,1)S(1)}, u32[]{:S(2)}, u32[]{:S(2)}) async-start(bf16[8,280,160]{1,2,0:T(8,128)(2,1)} %tile.4), calls=%async_computation | async-start | bytes 1966080 | tf_op jit(solution)/shard_map/all_to_all | solution.py:126
  45.5 1.0 copy-start.3
  48.0 4.5 %copy-start.11 = (f32[160]{0:T(256)S(1)}, f32[160]{0:T(256)}, u32[]{:S(2)}) copy-start(f32[160]{0:T(256)} %param.12) | copy-start | bytes 1924
  57.9 8.3 %copy-start.9 = (bf16[896]{0:T(1024)(128)(2,1)S(1)}, bf16[896]{0:T(1024)(128)(2,1)}, u32[]{:S(2)}) copy-start(bf16[896]{0:T(1024)(128)(2,1)} %param.14) | copy-start | bytes 5380
  57.9 8.3 %copy-start.8 = (s32[5]{0:T(128)S(1)}, s32[5]{0:T(128)}, u32[]{:S(2)}) copy-start(s32[5]{0:T(128)} %param.18) | copy-start | bytes 64
  57.9 8.4 %copy-start.10 = (s32[5]{0:T(128)S(1)}, s32[5]{0:T(128)}, u32[]{:S(2)}) copy-start(s32[5]{0:T(128)} %param.19) | copy-start | bytes 64
  57.9 70.4 %all-to-all-start.1 = ((bf16[32,70,1024]{2,1,0:T(8,128)(2,1)}), bf16[32,70,1024]{2,1,0:T(8,128)(2,1)}, u32[]{:S(2)}, u32[]{:S(2)}) async-start(bf16[32,70,1024]{2,1,0:T(8,128)(2,1)} %maximum_maximum_fusion), calls=%async_computation.1 | async-start | bytes 9437184 | tf_op jit(solution)/shard_map/all_to_all | solution.py:137
  66.1 136.8 %all-gather.3.cloned.1.call-start = ((), (), s32[]{:S(2)}) async-start(), calls=%async_computation.5 | async-start | bytes 5017600 | tf_op jit(solution)/shard_map/all_gather | solution.py:76
  211.5 1.8 slice-start
  220.3 9.8 %copy-start.4 = (bf16[5,272,128]{2,1,0:T(8,128)(2,1)}, bf16[5,272,128]{2,1,0:T(8,128)(2,1)S(1)}, u32[]{:S(2)}) copy-start(bf16[5,272,128]{2,1,0:T(8,128)(2,1)S(1)} %get-tuple-element.15) | copy-start | bytes 1044484
  220.3 19.8 %copy-start.6 = (bf16[5,272,128]{2,1,0:T(8,128)(2,1)}, bf16[5,272,128]{2,1,0:T(8,128)(2,1)S(1)}, u32[]{:S(2)}) copy-start(bf16[5,272,128]{2,1,0:T(8,128)(2,1)S(1)} %get-tuple-element.14) | copy-start | bytes 1044484
  220.3 9.8 %copy-start.2 = (pred[5,448,272]{1,2,0:T(8,128)(4,1)S(1)}, pred[5,448,272]{1,2,0:T(8,128)(4,1)}, u32[]{:S(2)}) copy-start(pred[5,448,272]{1,2,0:T(8,128)(4,1)} %compare_and_fusion) | copy-start | bytes 1827844
  270.9 54.7 %all-to-all-start.2 = ((bf16[32,70,768]{2,1,0:T(8,128)(2,1)}), bf16[32,70,768]{2,1,0:T(8,128)(2,1)}, u32[]{:S(2)}, u32[]{:S(2)}) async-start(bf16[32,70,768]{2,1,0:T(8,128)(2,1)} %concatenate.49), calls=%async_computation.2 | async-start | bytes 7077888 | tf_op jit(solution)/shard_map/all_to_all | solution.py:192
  393.0 2.9 copy-start.7
  396.0 38.7 %copy-start.1 = (bf16[160,896]{1,0:T(8,128)(2,1)S(1)}, bf16[160,896]{1,0:T(8,128)(2,1)}, u32[]{:S(2)}) copy-start(bf16[160,896]{1,0:T(8,128)(2,1)} %param.13) | copy-start | bytes 860164
  397.9 36.1 %copy-start.5 = (bf16[280,160]{0,1:T(8,128)(2,1)S(1)}, bf16[280,160]{0,1:T(8,128)(2,1)}, u32[]{:S(2)}) copy-start(bf16[280,160]{0,1:T(8,128)(2,1)} %param.11) | copy-start | bytes 268804
Sparse Core Ops, SparseCore 0:
  155.7 47.0 all-gather.2

commit v11 on v8

--- a/solution.py
+++ b/solution.py
@@ -207,8 +207,13 @@
         preferred_element_type=jnp.float32,
     )
     gy_size = lax.psum(1, GY)
-    summed_out = lax.all_to_all(partial_out.astype(jnp.bfloat16), GY, 0, 0, tiled=True)
-    summed_out = jnp.sum(summed_out.astype(jnp.float32).reshape(gy_size, token_count // gy_size, -1), axis=0)
+    core_size = lax.psum(1, GY[1])
+    out_rows = token_count // gy_size
+    staged = partial_out.reshape(gy_size // core_size, core_size, out_rows, -1).transpose(1, 0, 2, 3)
+    staged = lax.all_to_all(staged.astype(jnp.bfloat16), GY[1], 0, 0, tiled=True)
+    staged = jnp.sum(staged.astype(jnp.float32), axis=0)
+    staged = lax.all_to_all(staged.astype(jnp.bfloat16), GY[0], 0, 0, tiled=True)
+    summed_out = jnp.sum(staged.astype(jnp.float32), axis=0)
     output = (hidden_f + summed_out).astype(jnp.bfloat16)
     return (output, key_out, value_out)
 

time: 437 us -> 428 us (0.979)
  blocking collectives: 121 us -> 113 us
    all_to_all x1 -> x2, blocking collectives: 33.4 us -> 26.5 us  [the longest x1 21.9 us: per_device(): lax.all_to_all(staged.astype(jnp.bfloat16), GY[0], 0, 0, tiled=True)]
    all_to_all x3 -> x0, local copies, waits for them, and re-layouts: 5.44 us -> none  [the longest x1 2.93 us: gather_gx(): return lax.all_to_all(tiled, GX, 0, 0, tiled=True)]
  transfers between devices with their start and end apart: 3 -> 3, of which waited for: 3 -> 3; matrix products, arithmetic and copies ran while one was open for 0% -> 1% of each run, Pallas kernels for 0% -> 0%
where the time goes in v11:
time: 428 us; the launch traced here: 427 us
  waiting for transfers between devices  158 us (37%)
  blocking collectives  113 us (26%)
  local copies, waits for them, and re-layouts  65.5 us (15%)
  other arithmetic  32.8 us (8%)
  matrix products  26.2 us (6%)
  starting transfers between devices  15.9 us (4%)
  between operations  14.5 us (3%)
    all_to_all x1, waiting for transfers between devices, per_device(): payload = lax.all_to_all(payload, GX, 0, 0, tiled=True).astype(jnp.float32)  65.3 us
    all_to_all x1, waiting for transfers between devices, per_device(): both = lax.all_to_all(both, GX, 0, 0, tiled=True)  47.2 us
    all_gather x1, waiting for transfers between devices, gather_gx_chain(): value = lax.all_gather(value, axis, axis=0, tiled=True)  46 us
    all_to_all x1, blocking collectives, gather_gx(): return lax.all_to_all(tiled, GX, 0, 0, tiled=True)  42.9 us
    all_gather x2, blocking collectives, gather_gx_chain(): value = lax.all_gather(value, axis, axis=0, tiled=True)  23.3 us
    all_to_all x1, blocking collectives, per_device(): lax.all_to_all(staged.astype(jnp.bfloat16), GY[0], 0, 0, tiled=True)  21.9 us
    all_gather x1, blocking collectives, per_device(): lax.all_gather(hidden, GY, axis=0, tiled=True).astype(jnp.float32)  20.8 us
    concatenate x8, local copies, waits for them, and re-layouts, per_device(): both = jnp.concatenate([mixed, stats, pad], axis=1).astype(jnp.bfloat16)  17.3 us
  transfers between devices with their start and end apart: 3, of which 3 were waited for; matrix products, arithmetic and copies ran while one was open for 1% of the time, Pallas kernels for 0%

profile of v11, /device:TPU:2, one launch (start us, length us, event | category | flops | bytes accessed | tf_op | source)
XLA Modules:
  0.0 426.8 jit_solution(9029610081938853302)
XLA Ops:
  7.2 20.8 %all-gather = bf16[8,280,160]{1,2,0:T(8,128)(2,1)S(1)} all-gather(bf16[1,280,160]{1,2,0:T(8,128)(2,1)} %bitcast.101), channel_id=1, replica_groups=mesh['y'=4,'zl'=2,'x'=4,'zh'=4,'c'=2] {'zh','c'}, dimensions={0}, use_global_device_ids=true | all-gather | bytes 806400 | tf_op jit(solution)/shard_map/all_gather | solution.py:125
  35.0 5.1 %concatenate.41 = bf16[32,70,896]{2,1,0:T(8,128)(2,1)} reshape(bf16[2240,896]{1,0:T(8,128)(2,1)} %convolution_convert_fusion) | data formatting | bytes 8028160 | tf_op jit(solution)/shard_map/concatenate | solution.py:134
  40.8 5.5 %maximum_maximum_fusion = bf16[32,70,1024]{2,1,0:T(8,128)(2,1)} fusion(bf16[32,70,1]{2,1,0:T(8,128)(2,1)S(1)} %concatenate.53, bf16[32,70,896]{2,1,0:T(8,128)(2,1)} %concatenate.41, bf16[1024]{0:T(1024)(128)(2,1)S(1)} %pad.8.clone), kind=kLoop, calls=%fused_computation.14 | loop fusion | flops 13762560 | bytes 8608128 | tf_op jit(solution)/shard_map/concatenate | solution.py:134
  46.3 8.4 %all-to-all-start = ((bf16[32,70,1024]{2,1,0:T(8,128)(2,1)}), bf16[32,70,1024]{2,1,0:T(8,128)(2,1)}, u32[]{:S(2)}, u32[]{:S(2)}) async-start(bf16[32,70,1024]{2,1,0:T(8,128)(2,1)} %maximum_maximum_fusion), calls=%async_computation | async-start | bytes 9437184 | tf_op jit(solution)/shard_map/all_to_all | solution.py:135
  55.2 65.3 %all-to-all-done = bf16[32,70,1024]{2,1,0:T(8,128)(2,1)} async-done(((bf16[32,70,1024]{2,1,0:T(8,128)(2,1)}), bf16[32,70,1024]{2,1,0:T(8,128)(2,1)}, u32[]{:S(2)}, u32[]{:S(2)}) %all-to-all-start) | async-done | bytes 4587552 | tf_op jit(solution)/shard_map/all_to_all | solution.py:135
  125.3 11.9 %all-gather.1 = bf16[4,70,896]{2,1,0:T(8,128)(2,1)S(1)} all-gather(bf16[1,70,896]{2,1,0:T(8,128)(2,1)S(1)} %maximum_bitcast_fusion.1), channel_id=1, replica_groups=mesh['y'=4,'zl'=2,'x'=4,'zh'=4,'c'=2] {'x'}, dimensions={0}, use_global_device_ids=true | all-gather | bytes 627200 | tf_op jit(solution)/shard_map/all_gather | solution.py:76
  137.3 11.4 %all_gather.14 = bf16[560,896]{1,0:T(8,128)(2,1)} all-gather(bf16[280,896]{1,0:T(8,128)(2,1)S(1)} %reshape.480), channel_id=1, replica_groups=mesh['y'=4,'zl'=2,'x'=4,'zh'=4,'c'=2] {'zl'}, dimensions={0}, use_global_device_ids=true | all-gather | bytes 1505280 | tf_op jit(solution)/shard_map/all_gather | solution.py:76
  150.6 46.0 %all-gather.4.cloned.1.call-done = bf16[2240,896]{1,0:T(8,128)(2,1)} async-done(((bf16[560,896]{1,0:T(8,128)(2,1)}), bf16[2240,896]{1,0:T(8,128)(2,1)}) %all-gather.4.cloned.1.call-update) | async-done | bytes 4014096 | tf_op jit(solution)/shard_map/all_gather | solution.py:76
  201.2 4.0 gather_fusion.1
  207.1 5.3 %reshape.455 = bf16[5,448,5,128]{3,2,1,0:T(8,128)(2,1)} reshape(bf16[2240,640]{1,0:T(8,128)(2,1)S(1)} %slice-done) | data formatting | bytes 5734400 | tf_op jit(solution)/shard_map/reshape.13
  214.0 9.7 %fusion = (f32[5,5,448]{2,1,0:T(8,128)S(1)}, f32[5,272,448,5]{2,1,3,0:T(8,128)}) fusion(pred[5,448,272]{1,2,0:T(8,128)(4,1)} %compare_and_fusion, bf16[5,448,5,128]{3,2,1,0:T(8,128)(2,1)} %reshape.455, bf16[5,272,128]{2,1,0:T(8,128)(2,1)S(1)} %get-tuple-element.15), kind=kOutput, calls=%fused_computation.4 | convolution fusion | flops 789006400 | bytes 16055040 | tf_op jit(solution)/shard_map/rikgd,rpkd->rkgip/dot_general | solution.py:156
  223.8 8.5 %fusion.1 = bf16[5,5,448]{2,1,0:T(8,128)(2,1)S(1)} fusion(f32[5,272,448,5]{2,1,3,0:T(8,128)} %get-tuple-element.22, f32[5,5,448]{2,1,0:T(8,128)S(1)} %get-tuple-element.11, pred[5,448,272]{1,2,0:T(8,128)(4,1)S(1)} %copy-done.2), kind=kLoop, calls=%fused_computation.5 | loop fusion | flops 15220800 | bytes 12862080 | tf_op jit(solution)/shard_map/reduce_sum | solution.py:165
  233.8 9.9 %convert_bitcast_fusion = bf16[5,448,1,5,128]{4,1,3,0,2:T(8,128)(2,1)S(1)} fusion(f32[5,272,448,5]{2,1,3,0:T(8,128)} %get-tuple-element.22, f32[5,5,448]{2,1,0:T(8,128)S(1)} %get-tuple-element.11, pred[5,448,272]{1,2,0:T(8,128)(4,1)S(1)} %copy-done.2, bf16[5,272,128]{2,1,0:T(8,128)(2,1)S(1)} %get-tuple-element.14), kind=kOutput, calls=%fused_computation.17 | convolution fusion | flops 796544000 | bytes 16055040 | tf_op jit(solution)/shard_map/rkgip,rpkd->rikgd/dot_general | solution.py:166
  243.7 4.1 copy.92
  247.8 6.2 %concatenate.48 = bf16[32,70,640]{2,1,0:T(8,128)(2,1)S(1)} reshape(bf16[5,448,1,5,128]{4,3,1,0,2:T(8,128)(2,1)} %copy.92) | data formatting | bytes 5734400 | tf_op jit(solution)/shard_map/concatenate | solution.py:189
  257.7 6.9 %concatenate.52 = bf16[32,70,768]{2,1,0:T(8,128)(2,1)} concatenate(bf16[32,70,640]{2,1,0:T(8,128)(2,1)S(1)} %concatenate.48, bf16[32,70,5]{2,1,0:T(8,128)(2,1)} %copy.96, bf16[32,70,5]{2,1,0:T(8,128)(2,1)} %copy.97, bf16[32,70,5]{2,1,0:T(8,128)(2,1)} %copy.98, bf16[32,70,113]{2,1,0:T(8,128)(2,1)} %broadcast_in_dim.118), dimensions={2} | concatenate | bytes 6881280 | tf_op jit(solution)/shard_map/concatenate | solution.py:189
  264.7 7.5 %all-to-all-start.1 = ((bf16[32,70,768]{2,1,0:T(8,128)(2,1)}), bf16[32,70,768]{2,1,0:T(8,128)(2,1)}, u32[]{:S(2)}, u32[]{:S(2)}) async-start(bf16[32,70,768]{2,1,0:T(8,128)(2,1)} %concatenate.52), calls=%async_computation.1 | async-start | bytes 7077888 | tf_op jit(solution)/shard_map/all_to_all | solution.py:190
  272.2 47.2 %all-to-all-done.1 = bf16[32,70,768]{2,1,0:T(8,128)(2,1)} async-done(((bf16[32,70,768]{2,1,0:T(8,128)(2,1)}), bf16[32,70,768]{2,1,0:T(8,128)(2,1)}, u32[]{:S(2)}, u32[]{:S(2)}) %all-to-all-start.1) | async-done | bytes 3440672 | tf_op jit(solution)/shard_map/all_to_all | solution.py:190
  322.3 5.5 %mul.197 = f32[32,70,5,128]{3,2,0,1:T(8,128)} broadcast(f32[32,70,5]{2,0,1:T(8,128)S(1)} %copy.99), dimensions={0,1,2} | broadcast | bytes 5779200 | tf_op jit(solution)/shard_map/mul | solution.py:200
  327.7 9.0 %mul.198 = f32[32,70,640]{2,0,1:T(8,128)} reshape(f32[32,70,5,128]{3,2,0,1:T(8,128)} %mul.197) | data formatting | bytes 11468800 | tf_op jit(solution)/shard_map/mul | solution.py:200
  336.7 6.7 %fusion.7 = bf16[70,640]{1,0:T(8,128)(2,1)S(1)} fusion(f32[32,70,640]{2,0,1:T(8,128)} %mul.198, bf16[32,70,768]{2,1,0:T(8,128)(2,1)} %all-to-all-done.1), kind=kLoop, calls=%fused_computation.12 | loop fusion | flops 4256000 | bytes 8691200 | tf_op jit(solution)/shard_map/reduce_sum | solution.py:200
  343.7 42.9 %all_to_all.28 = bf16[32,70,640]{2,1,0:T(8,128)(2,1)S(1)} all-to-all(bf16[32,70,640]{2,1,0:T(8,128)(2,1)S(1)} %tile.2), channel_id=1, replica_groups=mesh['y'=4,'zl'=2,'x'=4,'zh'=4,'c'=2] {'y','zl','x'}, dimensions={0} | all-to-all | bytes 5734400 | tf_op jit(solution)/shard_map/all_to_all | solution.py:83
  392.3 4.5 %all_to_all.29 = bf16[2,4,280,160]{2,3,1,0:T(8,128)(2,1)S(1)} all-to-all(bf16[2,4,280,160]{2,3,1,0:T(8,128)(2,1)S(1)} %copy.101), channel_id=1, replica_groups=mesh['y'=4,'zl'=2,'x'=4,'zh'=4,'c'=2] {'c'}, dimensions={0} | all-to-all | bytes 1433600 | tf_op jit(solution)/shard_map/all_to_all | solution.py:213
  397.3 21.9 %all_to_all.30 = bf16[4,280,160]{1,2,0:T(8,128)(2,1)S(1)} all-to-all(bf16[4,280,160]{1,2,0:T(8,128)(2,1)S(1)} %reduce_sum.94), channel_id=1, replica_groups=mesh['y'=4,'zl'=2,'x'=4,'zh'=4,'c'=2] {'zh'}, dimensions={0} | all-to-all | bytes 716800 | tf_op jit(solution)/shard_map/all_to_all | solution.py:215
  (94 shorter events, 38.0 us)
Async XLA Ops:
  7.2 24.5 %copy-start = (bf16[160,896]{1,0:T(8,128)(2,1)S(1)}, bf16[160,896]{1,0:T(8,128)(2,1)}, u32[]{:S(2)}) copy-start(bf16[160,896]{1,0:T(8,128)(2,1)} %param.13) | copy-start | bytes 860164
  28.0 3.7 copy-start.7
  46.3 8.5 %copy-start.8 = (bf16[896]{0:T(1024)(128)(2,1)S(1)}, bf16[896]{0:T(1024)(128)(2,1)}, u32[]{:S(2)}) copy-start(bf16[896]{0:T(1024)(128)(2,1)} %param.14) | copy-start | bytes 5380
  46.3 8.6 %copy-start.6 = (s32[5]{0:T(128)S(1)}, s32[5]{0:T(128)}, u32[]{:S(2)}) copy-start(s32[5]{0:T(128)} %param.18) | copy-start | bytes 64
  46.3 8.6 %copy-start.9 = (s32[5]{0:T(128)S(1)}, s32[5]{0:T(128)}, u32[]{:S(2)}) copy-start(s32[5]{0:T(128)} %param.19) | copy-start | bytes 64
  46.3 74.2 %all-to-all-start = ((bf16[32,70,1024]{2,1,0:T(8,128)(2,1)}), bf16[32,70,1024]{2,1,0:T(8,128)(2,1)}, u32[]{:S(2)}, u32[]{:S(2)}) async-start(bf16[32,70,1024]{2,1,0:T(8,128)(2,1)} %maximum_maximum_fusion), calls=%async_computation | async-start | bytes 9437184 | tf_op jit(solution)/shard_map/all_to_all | solution.py:135
  54.7 141.9 %all-gather.4.cloned.1.call-start = ((), (), s32[]{:S(2)}) async-start(), calls=%async_computation.5 | async-start | bytes 5017600 | tf_op jit(solution)/shard_map/all_gather | solution.py:76
  205.3 1.8 slice-start
  214.0 9.8 %copy-start.3 = (bf16[5,272,128]{2,1,0:T(8,128)(2,1)}, bf16[5,272,128]{2,1,0:T(8,128)(2,1)S(1)}, u32[]{:S(2)}) copy-start(bf16[5,272,128]{2,1,0:T(8,128)(2,1)S(1)} %get-tuple-element.15) | copy-start | bytes 1044484
  214.0 19.8 %copy-start.5 = (bf16[5,272,128]{2,1,0:T(8,128)(2,1)}, bf16[5,272,128]{2,1,0:T(8,128)(2,1)S(1)}, u32[]{:S(2)}) copy-start(bf16[5,272,128]{2,1,0:T(8,128)(2,1)S(1)} %get-tuple-element.14) | copy-start | bytes 1044484
  214.0 9.8 %copy-start.2 = (pred[5,448,272]{1,2,0:T(8,128)(4,1)S(1)}, pred[5,448,272]{1,2,0:T(8,128)(4,1)}, u32[]{:S(2)}) copy-start(pred[5,448,272]{1,2,0:T(8,128)(4,1)} %compare_and_fusion) | copy-start | bytes 1827844
  264.7 54.8 %all-to-all-start.1 = ((bf16[32,70,768]{2,1,0:T(8,128)(2,1)}), bf16[32,70,768]{2,1,0:T(8,128)(2,1)}, u32[]{:S(2)}, u32[]{:S(2)}) async-start(bf16[32,70,768]{2,1,0:T(8,128)(2,1)} %concatenate.52), calls=%async_computation.1 | async-start | bytes 7077888 | tf_op jit(solution)/shard_map/all_to_all | solution.py:190
  386.7 2.4 copy-start.10
  389.0 31.0 %copy-start.1 = (bf16[160,896]{1,0:T(8,128)(2,1)S(1)}, bf16[160,896]{1,0:T(8,128)(2,1)}, u32[]{:S(2)}) copy-start(bf16[160,896]{1,0:T(8,128)(2,1)} %param.13) | copy-start | bytes 860164
  392.2 27.1 %copy-start.4 = (bf16[280,160]{0,1:T(8,128)(2,1)S(1)}, bf16[280,160]{0,1:T(8,128)(2,1)}, u32[]{:S(2)}) copy-start(bf16[280,160]{0,1:T(8,128)(2,1)} %param.11) | copy-start | bytes 268804
Sparse Core Ops, SparseCore 0:
  148.9 47.6 all-gather.3
